TPU v7x, 256 devices: a whole 4x4x8 slice. The times are simulated.
256 devices in a mesh: layer: 8 (over y, x_lo), tile: 32 (over z, x_hi, core).
Axes of the slice: x: 4 (x_hi: 2, x_lo: 2; x = x_hi * 2 + x_lo), y: 4, z: 8, core: 2. Of those that a mesh axis runs over, the one named last changes fastest.
Arguments:
- blocks: bfloat16 [8, 32, 320, 128, 128], P('layer', 'tile'), may hold values from 0.00049 to 0.0041
- slot_rows: int32 [8, 32, 320], P('layer', 'tile'), may hold values from 0 to 63, as said below
- slot_cols: int32 [8, 32, 320], P('layer', 'tile'), may hold values from 0 to 127
- rotation: int32 [8, 32, 320], P('layer', 'tile'), may hold values from 0 to 1
- live_block_count: int32 [8, 32], P('layer', 'tile'), may hold values from 64 to 320, as said below
- density: bfloat16 [8, 32, 8192], P('layer', 'tile'), may hold values from 0.29882812 to 3
- start: bfloat16 [8, 32, 64, 8192], P('layer', 'tile'), may hold values from -6 to 6
Outputs:
- vectors: bfloat16 [8, 32, 64, 8192], P('layer', 'tile')
Inputs may be any that keep to these rules, and one draw needn't show every extreme that they name: `slot_rows`: slots 0 to 63 of every device are live and hold the diagonal blocks (row s, source s, no rotation). Only the first live_block_count slots of a device are live; some device has all 320 slots live and some device only 64.
All inputs are finite; a program needn't handle non-finite values.
Results may differ from a plain program's by a relative error of at most 0.005.
Values may be sent and summed in bfloat16 or wider, within the bound.
No kernel may reach another device: no remote copies, remote signals or barrier semaphores. Data moves between devices by JAX's collectives and lax.ppermute only.
A program may use at most 128 MiB of HBM per device.

v0:
```python
import functools

import jax
import jax.numpy as jnp
from jax import lax
from jax.experimental import pallas as pl
from jax.experimental.pallas import tpu as pltpu
from jax.sharding import PartitionSpec as P

UNROLL = 16
TURN = 8
CHUNKS = 8
VM = pltpu.VMEM
VMEM_SPEC = pl.BlockSpec(memory_space=pltpu.VMEM)
SMEM_SPEC = pl.BlockSpec(memory_space=pltpu.SMEM)
HBM_SPEC = pl.BlockSpec(memory_space=pltpu.HBM)
FORWARD_OWN, FORWARD_RIM, ADJOINT_OWN, ADJOINT_RIM = range(4)


def pair_tables(slot_row, slot_col, turned, live_count, num_blocks, places):
    slots = slot_row.shape[0]
    index = jnp.arange(slots, dtype=jnp.int32)
    live = index < live_count
    half = (slot_col >= num_blocks).astype(jnp.int32)
    source = slot_col - half * num_blocks
    keys = jnp.arange(num_blocks, dtype=jnp.int32)
    place = jnp.arange(places, dtype=jnp.int32)
    dest = jnp.stack([slot_row, slot_row, source, source])
    operand = jnp.stack([source, source, slot_row, slot_row])
    side = jnp.arange(4, dtype=jnp.int32)[:, None] & 1
    used = live[None] & (half[None] == side)
    earlier = index[:, None] < index[None, :]
    hit = (dest[:, :, None] == dest[:, None, :]) & used[:, :, None] & earlier[None]
    rank = jnp.sum(hit.astype(jnp.int32), axis=1)
    member = (dest[:, :, None] == keys) & used[:, :, None]
    pairs = (jnp.sum(member.astype(jnp.int32), axis=1) + 1) >> 1
    before = jnp.sum(jnp.where(keys[:, None] < keys[None, :], pairs[:, :, None], 0), axis=1)
    position = 2 * jnp.sum(jnp.where(dest[:, :, None] == keys, before[:, None, :], 0), axis=2) + rank
    position = jnp.where(used, position, -1)
    empty = num_blocks * 512
    packed = index[None] + operand * 512 + dest * 65536 - empty
    tables = jnp.sum(jnp.where(position[:, :, None] == place, packed[:, :, None], 0), axis=1) + empty
    trips = (jnp.sum(pairs, axis=1) + UNROLL - 1) // UNROLL
    flip = live & (turned == 1)
    flip_rank = jnp.sum((flip[:, None] & earlier).astype(jnp.int32), axis=0)
    flip_rank = jnp.where(flip, flip_rank, -1)
    flips = jnp.sum(jnp.where(flip_rank[:, None] == index[None, :], index[:, None] - slots, 0), axis=0) + slots
    flip_trips = (jnp.sum(flip.astype(jnp.int32)) + TURN - 1) // TURN
    meta = jnp.concatenate([trips, jnp.full((4,), flip_trips, jnp.int32)])
    return tables.reshape(-1), flips, meta


def pair_loop(which, meta, tab, source, matrix, acc):
    start = which * (tab.shape[0] // 4)
    transposed = which >= ADJOINT_OWN

    def body(step, carry):
        done = []
        for u in range(UNROLL):
            place = start + (step * UNROLL + u) * 2
            one, two = tab[place], tab[place + 1]
            lhs = jnp.concatenate([source[(one >> 9) & 127], source[(two >> 9) & 127]], axis=1)
            first, second = matrix[one & 511], matrix[two & 511]
            rhs = jnp.concatenate([first, second], axis=0 if transposed else 1)
            dims = (((1,), (0 if transposed else 1,)), ((), ()))
            done.append((one >> 16, lax.dot_general(lhs, rhs, dims, preferred_element_type=jnp.float32)))
        for dest, value in done:
            acc[dest] += value
        return carry

    lax.fori_loop(0, meta[which], body, 0)


def clear(ref):
    def body(b, carry):
        ref[b] = jnp.zeros(ref.shape[1:], ref.dtype)
        return carry

    lax.fori_loop(0, ref.shape[0], body, 0)


def edge_kernel(start, density, head, tail, held, sems):
    size = head.shape[1]
    vectors = start.shape[0]
    edge = head.shape[0] // (vectors + 1)
    width = edge * size
    outs = (head, tail)
    origin = (0, start.shape[1] - width)
    copies = [
        pltpu.make_async_copy(start.at[:, pl.ds(origin[i], width)], held.at[i], sems.at[i]) for i in range(2)
    ]
    for copy in copies:
        copy.start()
    for i in range(2):
        copies[i].wait()
        weights = []
        for b in range(edge):
            cells = pl.ds(origin[i] + b * size, size)
            weight = density[:, cells].astype(jnp.float32)
            weights.append(weight)
            value = held[i, :, b * size : (b + 1) * size].astype(jnp.float32) * weight
            outs[i][b * vectors : (b + 1) * vectors] = value.astype(jnp.bfloat16)
        outs[i][edge * vectors :] = jnp.concatenate(weights, axis=0).astype(jnp.bfloat16)


def first_kernel(meta, tab, flips, blocks, start, density, matrix, rows, source, held, sems):
    slots = blocks.shape[0]
    part = slots // CHUNKS
    copies = [pltpu.make_async_copy(start, held, sems.at[CHUNKS])]
    for c in range(CHUNKS):
        here = pl.ds(c * part, part)
        copies.append(pltpu.make_async_copy(blocks.at[here], matrix.at[here], sems.at[c]))
    for copy in copies:
        copy.start()
    num_blocks, vectors = rows.shape[0], start.shape[0]
    size = blocks.shape[-1]
    clear(rows)
    matrix[slots] = jnp.zeros((size, size), matrix.dtype)
    source[num_blocks] = jnp.zeros(source.shape[1:], source.dtype)
    copies[0].wait()
    top = lax.broadcasted_iota(jnp.int32, (16, size), 0) == 0

    def fill(b, carry):
        cells = pl.ds(pl.multiple_of(b * size, size), size)
        weight = density[:, cells].astype(jnp.float32)
        source[b, :vectors] = (held[:, cells].astype(jnp.float32) * weight).astype(jnp.bfloat16)
        source[b, vectors:] = jnp.where(top, jnp.broadcast_to(weight, (16, size)), 0.0).astype(jnp.bfloat16)
        return carry

    lax.fori_loop(0, num_blocks, fill, 0, unroll=4)
    across = lax.broadcasted_iota(jnp.int32, (size, size), 0)
    along = lax.broadcasted_iota(jnp.int32, (size, size), 1)
    mirror = (across + along == size - 1).astype(jnp.float32).astype(jnp.bfloat16)
    for copy in copies[1:]:
        copy.wait()

    def turn(step, carry):
        done = []
        for u in range(TURN):
            slot = flips[step * TURN + u]
            value = jnp.dot(matrix[slot], mirror, preferred_element_type=jnp.float32)
            done.append((slot, value.astype(jnp.bfloat16)))
        for slot, value in done:
            matrix[slot] = value
        return carry

    lax.fori_loop(0, meta[4], turn, 0)
    pair_loop(FORWARD_OWN, meta, tab, source, matrix, rows)


def own_kernel(meta, tab, matrix, head, middle, tail, rows, source):
    clear(rows)
    num_blocks = rows.shape[0]
    edge = num_blocks // 4
    vectors = rows.shape[1]
    for b in range(edge):
        source[b] = head[b * vectors : (b + 1) * vectors]
        source[num_blocks - edge + b] = tail[b * vectors : (b + 1) * vectors]
    source[edge : num_blocks - edge] = middle[...]
    source[num_blocks] = jnp.zeros(source.shape[1:], source.dtype)
    pair_loop(FORWARD_OWN, meta, tab, source, matrix, rows)


def rim_kernel(first, meta, tab, matrix, rows_in, left, right, upper, lower, *rest):
    del rows_in
    if first:
        rows, image, inverse = rest[:3]
        rest = rest[3:]
    else:
        inverse, rows, image = rest[:3]
        rest = rest[3:]
    backs, (source, total) = rest[:4], rest[4:]
    num_blocks, size = rows.shape[0], rows.shape[2]
    vectors = image.shape[1]
    edge = num_blocks // 4
    for side, rim in enumerate((left, right, upper, lower)):
        for b in range(edge):
            source[side * edge + b, :vectors] = rim[b * vectors : (b + 1) * vectors]
        if first:
            weights = rim[edge * vectors :].astype(jnp.float32)
            top = lax.broadcasted_iota(jnp.int32, (16, size), 0) == 0
            for b in range(edge):
                pad = jnp.where(top, jnp.broadcast_to(weights[b : b + 1], (16, size)), 0.0)
                source[side * edge + b, vectors:] = pad.astype(jnp.bfloat16)
    source[num_blocks] = jnp.zeros(source.shape[1:], source.dtype)
    clear(total)
    pair_loop(FORWARD_RIM, meta, tab, source, matrix, rows)

    def divide(b, carry):
        if first:
            factor = 1.0 / rows[b, vectors : vectors + 8]
            inverse[b] = factor
        else:
            factor = inverse[b]
        image[b] = (rows[b, :vectors] * factor[:1]).astype(jnp.bfloat16)
        return carry

    lax.fori_loop(0, num_blocks, divide, 0, unroll=4)
    image[num_blocks] = jnp.zeros(image.shape[1:], image.dtype)
    pair_loop(ADJOINT_RIM, meta, tab, image, matrix, total)
    for side in range(4):
        for b in range(edge):
            backs[side][b * vectors : (b + 1) * vectors] = total[side * edge + b].astype(jnp.bfloat16)


def adjoint_kernel(meta, tab, matrix, image, total):
    clear(total)
    pair_loop(ADJOINT_OWN, meta, tab, image, matrix, total)


def collect(total, density, lows, highs, store):
    num_blocks, vectors, size = total.shape
    edge = num_blocks // 4

    def add(b, norm, parts):
        value = total[b]
        if parts:
            here = b if parts is lows else b - (num_blocks - edge)
            rows = pl.ds(pl.multiple_of(here * vectors, vectors), vectors)
            value = value + (parts[0][rows].astype(jnp.float32) + parts[1][rows].astype(jnp.float32))
        cells = pl.ds(pl.multiple_of(b * size, size), size)
        weighted = value * density[:, cells].astype(jnp.float32)
        store(b, value, weighted)
        return norm + weighted * value

    norm = jnp.zeros((vectors, size), jnp.float32)
    norm = lax.fori_loop(0, edge, lambda b, n: add(b, n, lows), norm)
    norm = lax.fori_loop(edge, num_blocks - edge, lambda b, n: add(b, n, None), norm)
    norm = lax.fori_loop(num_blocks - edge, num_blocks, lambda b, n: add(b, n, highs), norm)
    ones = jnp.ones((8, size), jnp.float32)
    return lax.dot_general(
        ones, norm, (((1,), (1,)), ((), ())), precision=lax.Precision.HIGHEST, preferred_element_type=jnp.float32
    )


def join_kernel(total, density, low0, low1, high0, high1, head, middle, tail, norm):
    num_blocks, vectors, size = total.shape
    edge = num_blocks // 4
    high_from = num_blocks - edge

    def store(b, value, weighted):
        del value
        scaled = weighted.astype(jnp.bfloat16)

        def rows(first):
            return pl.ds(pl.multiple_of((b - first) * vectors, vectors), vectors)

        @pl.when(b < edge)
        def _():
            head[rows(0)] = scaled

        @pl.when((b >= edge) & (b < high_from))
        def _():
            middle[b - edge] = scaled

        @pl.when(b >= high_from)
        def _():
            tail[rows(high_from)] = scaled

    norm[...] = collect(total, density, (low0, low1), (high0, high1), store)


def sum_kernel(total_in, density, low0, low1, high0, high1, norm, total, message):
    del total_in

    def store(b, value, weighted):
        del weighted
        total[b] = value

    last = collect(total, density, (low0, low1), (high0, high1), store)
    both = jnp.concatenate([norm[...], last], axis=1)[:1]
    message[...] = jnp.broadcast_to(both, message.shape)


def final_kernel(total_cells, sums, total, out):
    num_blocks, vectors, size = total.shape
    both = jnp.sum(sums[...], axis=0, keepdims=True) * (1.0 / total_cells)
    diagonal = lax.broadcasted_iota(jnp.int32, (vectors, size), 0)
    lane = lax.broadcasted_iota(jnp.int32, (vectors, size), 1)
    both = jnp.broadcast_to(both, (vectors, size))
    first = jnp.sum(jnp.where(lane == diagonal, both, 0.0), axis=1, keepdims=True)
    second = jnp.sum(jnp.where(lane == diagonal + vectors, both, 0.0), axis=1, keepdims=True)
    factor = lax.rsqrt(first + 1e-06)
    scale = jnp.broadcast_to(factor * lax.rsqrt(factor * factor * second + 1e-06), (vectors, size))

    def body(b, carry):
        cells = pl.ds(pl.multiple_of(b * size, size), size)
        out[:, cells] = (total[b] * scale).astype(jnp.bfloat16)
        return carry

    lax.fori_loop(0, num_blocks, body, 0, unroll=4)


def shift(x, axis, step, periodic):
    count = lax.axis_size(axis)
    route = [(i, (i + step) % count) for i in range(count) if periodic or 0 <= i + step < count]
    return lax.ppermute(x, axis, route)


def outward(head, tail):
    return (
        shift(tail, "tile", 1, True),
        shift(head, "tile", -1, True),
        shift(tail, "layer", 1, False),
        shift(head, "layer", -1, False),
    )


def call(kernel, name, outs, in_specs, scratch, flops, nbytes, aliases={}):
    return pl.pallas_call(
        kernel,
        name=name,
        out_shape=outs,
        in_specs=in_specs,
        out_specs=[VMEM_SPEC] * len(outs),
        scratch_shapes=scratch,
        input_output_aliases=aliases,
        compiler_params=pltpu.CompilerParams(vmem_limit_bytes=16 * 1024 * 1024),
        cost_estimate=pl.CostEstimate(flops=flops, bytes_accessed=nbytes, transcendentals=0),
    )


def local(blocks, slot_rows, slot_cols, rotation, live_block_count, density, start):
    bf16, f32 = jnp.bfloat16, jnp.float32
    blocks, start = blocks[0, 0], start[0, 0]
    slots, size = blocks.shape[0], blocks.shape[2]
    vectors, cells = start.shape
    num_blocks = cells // size
    edge = num_blocks // 4
    weights = density[0]
    devices = lax.axis_size("layer") * lax.axis_size("tile")
    total_cells = cells * devices
    work = slots * size * size * vectors
    tall = vectors + 16
    rim_type = VM((edge * vectors, size), bf16)
    first_rim_type = VM((edge * (vectors + 1), size), bf16)
    block_f32 = VM((num_blocks, vectors, size), f32)
    tall_f32 = VM((num_blocks, tall, size), f32)
    image_type = VM((num_blocks + 1, vectors, size), bf16)
    middle_type = VM((num_blocks - 2 * edge, vectors, size), bf16)
    norm_type = VM((8, vectors), f32)

    head, tail = call(
        edge_kernel,
        "edges",
        [first_rim_type, first_rim_type],
        [HBM_SPEC, VMEM_SPEC],
        [VM((2, vectors, edge * size), bf16), pltpu.SemaphoreType.DMA((2,))],
        0,
        start.size,
    )(start, weights)
    rims = outward(head, tail)

    places = 2 * ((slots + num_blocks) // 2)
    tab, flips, meta = pair_tables(
        slot_rows[0, 0], slot_cols[0, 0], rotation[0, 0], live_block_count[0, 0], num_blocks, places
    )
    matrix, rows = call(
        first_kernel,
        "own_first",
        [VM((slots + 1, size, size), bf16), tall_f32],
        [SMEM_SPEC] * 3 + [HBM_SPEC, HBM_SPEC, VMEM_SPEC],
        [
            VM((num_blocks + 1, tall, size), bf16),
            VM((vectors, cells), bf16),
            pltpu.SemaphoreType.DMA((CHUNKS + 1,)),
        ],
        2 * work,
        2 * blocks.size * 2,
    )(meta, tab, flips, blocks, start, weights)

    inverse = norm = None
    for turn in range(2):
        first = turn == 0
        if not first:
            (rows,) = call(
                own_kernel,
                "own_next",
                [block_f32],
                [SMEM_SPEC] * 2 + [VMEM_SPEC] * 4,
                [VM((num_blocks + 1, vectors, size), bf16)],
                work,
                blocks.size,
            )(meta, tab, matrix, head, middle, tail)
            rims = outward(head, tail)
        extra = [] if first else [inverse]
        result = call(
            functools.partial(rim_kernel, first),
            "rim_first" if first else "rim_next",
            [tall_f32 if first else block_f32, image_type]
            + ([VM((num_blocks, 8, size), f32)] if first else [])
            + [rim_type] * 4,
            [SMEM_SPEC] * 2 + [VMEM_SPEC] * (6 + len(extra)),
            [VM((num_blocks + 1, tall if first else vectors, size), bf16), block_f32],
            2 * work,
            blocks.size,
            {3: 0},
        )(meta, tab, matrix, rows, *rims, *extra)
        image = result[1]
        if first:
            inverse = result[2]
        left, right, upper, lower = result[-4:]
        lows = (shift(right, "tile", 1, True), shift(lower, "layer", 1, False))
        highs = (shift(left, "tile", -1, True), shift(upper, "layer", -1, False))
        (total,) = call(
            adjoint_kernel,
            "adjoint_first" if first else "adjoint_last",
            [block_f32],
            [SMEM_SPEC] * 2 + [VMEM_SPEC] * 2,
            [],
            work,
            blocks.size,
        )(meta, tab, matrix, image)
        if first:
            head, middle, tail, norm = call(
                join_kernel,
                "join",
                [rim_type, middle_type, rim_type, norm_type],
                [VMEM_SPEC] * 6,
                [],
                0,
                num_blocks * vectors * size * 8,
            )(total, weights, *lows, *highs)
    total, message = call(
        sum_kernel,
        "join_last",
        [block_f32, VM((devices, 2 * vectors), f32)],
        [VMEM_SPEC] * 7,
        [],
        0,
        num_blocks * vectors * size * 8,
        {0: 0},
    )(total, weights, *lows, *highs, norm)
    sums = lax.all_to_all(message, ("layer", "tile"), 0, 0, tiled=True)
    out = call(
        functools.partial(final_kernel, total_cells),
        "write_out",
        [jax.ShapeDtypeStruct((vectors, cells), bf16)],
        [VMEM_SPEC] * 2,
        [],
        0,
        cells * vectors * 6,
    )(sums, total)[0]
    return out[None, None]


def solution(mesh):
    in_specs = (
        P("layer", "tile", None, None, None),
        P("layer", "tile", None),
        P("layer", "tile", None),
        P("layer", "tile", None),
        P("layer", "tile"),
        P("layer", "tile", None),
        P("layer", "tile", None, None),
    )
    out_specs = P("layer", "tile", None, None)
    return jax.shard_map(local, mesh=mesh, in_specs=in_specs, out_specs=out_specs, check_vma=False)
```

profile of v0, /device:TPU:1, one launch (start us, length us, event | category | flops | bytes accessed | tf_op | source)
XLA Modules:
  0.0 136.7 jit_solution(17752936690591332390)
XLA Ops:
  0.0 1.2 copy-done.1
  2.2 4.1 %collective-permute-start.2 = (bf16[1040,128]{1,0:T(8,128)(2,1)S(1)}, bf16[1040,128]{1,0:T(8,128)(2,1)S(1)}, u32[]{:S(2)}, u32[]{:S(2)}) collective-permute-start(bf16[1040,128]{1,0:T(8,128)(2,1)S(1)} %get-tuple-element.28), channel_id=1, source_target_pairs={{0,32},{32,64},{64,96},{96,128},{128,160},{160,192},{192,224},{1,3... | collective-permute-start | bytes 798728 | tf_op jit(solution)/shard_map/ppermute | solution.py:297
  6.3 3.4 %collective-permute-start = (bf16[1040,128]{1,0:T(8,128)(2,1)S(1)}, bf16[1040,128]{1,0:T(8,128)(2,1)S(1)}, u32[]{:S(2)}, u32[]{:S(2)}) collective-permute-start(bf16[1040,128]{1,0:T(8,128)(2,1)S(1)} %get-tuple-element.28), channel_id=1, source_target_pairs={{0,1},{1,2},{2,3},{3,4},{4,5},{5,6},{6,7},{7,8},{8,9},{9,10},{10,1... | collective-permute-start | bytes 798728 | tf_op jit(solution)/shard_map/ppermute | solution.py:297
  9.6 1.3 collective-permute-start.3
  15.4 0.9 fusion.3
  18.3 4.0 %copy-done = bf16[1,1,320,128,128]{4,3,2,1,0:T(8,128)(2,1)S(1)} copy-done((bf16[1,1,320,128,128]{4,3,2,1,0:T(8,128)(2,1)S(1)}, bf16[1,1,320,128,128]{4,3,2,1,0:T(8,128)(2,1)}, u32[]{:S(2)}) %copy-start) | copy-done | bytes 10485784
  23.0 5.4 %own_first.1 = (bf16[321,128,128]{2,1,0:T(8,128)(2,1)S(1)}, f32[64,80,128]{2,1,0:T(8,128)S(1)}) custom-call(s32[8]{0:T(128)S(1)} %concatenate.11.meta, s32[1536]{0:T(1024)S(1)} %add.79.tab, s32[320]{0:T(512)S(1)} %broadcast_add_fusion.1.flips, bf16[320,128,128]{2,1,0:T(8,128)(2,1)S(1)} %bitcast.14, bf16[64,8192]{1,0:T(8,128)(2,1)S(1)} %bitcast.16, ...), custom_call_target="tpu_custom_call" | custom-call | flops 671088640 | bytes 20971520 | tf_op jit(solution)/shard_map/own_first/pallas_call | solution.py:358
  28.5 3.2 %rim_first.1 = (f32[64,80,128]{2,1,0:T(8,128)S(1)}, bf16[65,64,128]{2,1,0:T(8,128)(2,1)S(1)}, f32[64,8,128]{2,1,0:T(8,128)S(1)}, bf16[1024,128]{1,0:T(8,128)(2,1...) custom-call(s32[8]{0:T(128)S(1)} %concatenate.11.meta, ...), custom_call_target="tpu_custom_call", output_to_operand_aliasing={{0}: (3, {})} | custom-call | flops 671088640 | bytes 5242880 | tf_op jit(solution)/shard_map/rim_first/pallas_call | solution.py:387
  31.7 2.2 %collective-permute-start.4 = (bf16[1024,128]{1,0:T(8,128)(2,1)S(1)}, bf16[1024,128]{1,0:T(8,128)(2,1)S(1)}, u32[]{:S(2)}, u32[]{:S(2)}) collective-permute-start(bf16[1024,128]{1,0:T(8,128)(2,1)S(1)} %get-tuple-element.31), channel_id=1, source_target_pairs={{0,1},{1,2},{2,3},{3,4},{4,5},{5,6},{6,7},{7,8},{8,9},{9,10},{10,1... | collective-permute-start | bytes 786440 | tf_op jit(solution)/shard_map/ppermute | solution.py:297
  33.9 3.3 %collective-permute-start.5 = (bf16[1024,128]{1,0:T(8,128)(2,1)S(1)}, bf16[1024,128]{1,0:T(8,128)(2,1)S(1)}, u32[]{:S(2)}, u32[]{:S(2)}) collective-permute-start(bf16[1024,128]{1,0:T(8,128)(2,1)S(1)} %get-tuple-element.32), channel_id=1, source_target_pairs={{0,32},{32,64},{64,96},{96,128},{128,160},{160,192},{192,224},{1,3... | collective-permute-start | bytes 786440 | tf_op jit(solution)/shard_map/ppermute | solution.py:297
  37.2 4.0 %collective-permute-start.6 = (bf16[1024,128]{1,0:T(8,128)(2,1)S(1)}, bf16[1024,128]{1,0:T(8,128)(2,1)S(1)}, u32[]{:S(2)}, u32[]{:S(2)}) collective-permute-start(bf16[1024,128]{1,0:T(8,128)(2,1)S(1)} %get-tuple-element.33), channel_id=1, source_target_pairs={{0,31},{1,0},{2,1},{3,2},{4,3},{5,4},{6,5},{7,6},{8,7},{9,8},{10,9... | collective-permute-start | bytes 786440 | tf_op jit(solution)/shard_map/ppermute | solution.py:297
  41.2 1.3 collective-permute-start.7
  42.5 2.7 %adjoint_first.1.total = f32[64,64,128]{2,1,0:T(8,128)S(1)} custom-call(s32[8]{0:T(128)S(1)} %concatenate.11.meta, s32[1536]{0:T(1024)S(1)} %add.79.tab, bf16[321,128,128]{2,1,0:T(8,128)(2,1)S(1)} %get-tuple-element.26.matrix, bf16[65,64,128]{2,1,0:T(8,128)(2,1)S(1)} %get-tuple-element.30.image), custom_call_target="tpu_custom_call" | custom-call | flops 335544320 | bytes 5242880 | tf_op jit(solution)/shard_map/adjoint_first/pallas_call | solution.py:405
  46.1 13.2 %collective-permute-done.7.high1 = bf16[1024,128]{1,0:T(8,128)(2,1)S(1)} collective-permute-done((bf16[1024,128]{1,0:T(8,128)(2,1)S(1)}, bf16[1024,128]{1,0:T(8,128)(2,1)S(1)}, u32[]{:S(2)}, u32[]{:S(2)}) %collective-permute-start.7) | collective-permute-done | bytes 262176 | tf_op jit(solution)/shard_map/ppermute | solution.py:297
  59.3 1.6 %join.1 = (bf16[1024,128]{1,0:T(8,128)(2,1)S(1)}, bf16[32,64,128]{2,1,0:T(8,128)(2,1)S(1)}, bf16[1024,128]{1,0:T(8,128)(2,1)S(1)}, f32[8,64]{1,0:T(8,128)S(1)}) custom-call(f32[64,64,128]{2,1,0:T(8,128)S(1)} %adjoint_first.1.total, bf16[1,8192]{1,0:T(2,128)(2,1)S(1)} %bitcast.19, bf16[1024,128]{1,0:T(8,128)(2,1)S(1)} %collective-permute-done.4.low0, ...), custom_call_target="tpu_custom_call" | custom-call | bytes 4194304 | tf_op jit(solution)/shard_map/join/pallas_call | solution.py:415
  60.9 1.3 collective-permute-start.11
  62.2 1.4 %collective-permute-start.9 = (bf16[1024,128]{1,0:T(8,128)(2,1)S(1)}, bf16[1024,128]{1,0:T(8,128)(2,1)S(1)}, u32[]{:S(2)}, u32[]{:S(2)}) collective-permute-start(bf16[1024,128]{1,0:T(8,128)(2,1)S(1)} %get-tuple-element.35.head), channel_id=1, source_target_pairs={{0,31},{1,0},{2,1},{3,2},{4,3},{5,4},{6,5},{7,6},{8,7},{9,8},{10,9... | collective-permute-start | bytes 786440 | tf_op jit(solution)/shard_map/ppermute | solution.py:297
  63.6 4.3 %collective-permute-start.10 = (bf16[1024,128]{1,0:T(8,128)(2,1)S(1)}, bf16[1024,128]{1,0:T(8,128)(2,1)S(1)}, u32[]{:S(2)}, u32[]{:S(2)}) collective-permute-start(bf16[1024,128]{1,0:T(8,128)(2,1)S(1)} %get-tuple-element.37.tail), channel_id=1, source_target_pairs={{0,32},{32,64},{64,96},{96,128},{128,160},{160,192},{192,224},{1,3... | collective-permute-start | bytes 786440 | tf_op jit(solution)/shard_map/ppermute | solution.py:297
  67.9 2.6 %collective-permute-start.8 = (bf16[1024,128]{1,0:T(8,128)(2,1)S(1)}, bf16[1024,128]{1,0:T(8,128)(2,1)S(1)}, u32[]{:S(2)}, u32[]{:S(2)}) collective-permute-start(bf16[1024,128]{1,0:T(8,128)(2,1)S(1)} %get-tuple-element.37.tail), channel_id=1, source_target_pairs={{0,1},{1,2},{2,3},{3,4},{4,5},{5,6},{6,7},{7,8},{8,9},{9,10},{10,1... | collective-permute-start | bytes 786440 | tf_op jit(solution)/shard_map/ppermute | solution.py:297
  70.5 3.6 %own_next.1.rows_in = f32[64,64,128]{2,1,0:T(8,128)S(1)} custom-call(s32[8]{0:T(128)S(1)} %concatenate.11.meta, s32[1536]{0:T(1024)S(1)} %add.79.tab, bf16[321,128,128]{2,1,0:T(8,128)(2,1)S(1)} %get-tuple-element.26.matrix, bf16[1024,128]{1,0:T(8,128)(2,1)S(1)} %get-tuple-element.35.head, bf16[32,64,128]{2,1,0:T(8,128)(2,1)S(1)} %get-tuple-element.36.middle, ...), custom_call_target="tpu_custom_call" | custom-call | flops 335544320 | bytes 5242880 | tf_op jit(solution)/shard_map/own_next/pallas_call | solution.py:376
  74.1 1.3 collective-permute-done.8.left
  75.4 3.1 %rim_next.1 = (f32[64,64,128]{2,1,0:T(8,128)S(1)}, bf16[65,64,128]{2,1,0:T(8,128)(2,1)S(1)}, bf16[1024,128]{1,0:T(8,128)(2,1)S(1)}, bf16[1024,128]{1,0:T(8,128)(...) custom-call(s32[8]{0:T(128)S(1)} %concatenate.11.meta, ...), custom_call_target="tpu_custom_call", output_to_operand_aliasing={{0}: (3, {})} | custom-call | flops 671088640 | bytes 5242880 | tf_op jit(solution)/shard_map/rim_next/pallas_call | solution.py:387
  78.5 3.2 %collective-permute-start.12 = (bf16[1024,128]{1,0:T(8,128)(2,1)S(1)}, bf16[1024,128]{1,0:T(8,128)(2,1)S(1)}, u32[]{:S(2)}, u32[]{:S(2)}) collective-permute-start(bf16[1024,128]{1,0:T(8,128)(2,1)S(1)} %get-tuple-element.40), channel_id=1, source_target_pairs={{0,1},{1,2},{2,3},{3,4},{4,5},{5,6},{6,7},{7,8},{8,9},{9,10},{10,1... | collective-permute-start | bytes 786440 | tf_op jit(solution)/shard_map/ppermute | solution.py:297
  81.7 8.2 %collective-permute-start.13 = (bf16[1024,128]{1,0:T(8,128)(2,1)S(1)}, bf16[1024,128]{1,0:T(8,128)(2,1)S(1)}, u32[]{:S(2)}, u32[]{:S(2)}) collective-permute-start(bf16[1024,128]{1,0:T(8,128)(2,1)S(1)} %get-tuple-element.41), channel_id=1, source_target_pairs={{0,32},{32,64},{64,96},{96,128},{128,160},{160,192},{192,224},{1,3... | collective-permute-start | bytes 786440 | tf_op jit(solution)/shard_map/ppermute | solution.py:297
  90.0 1.3 collective-permute-start.15
  91.3 2.7 %adjoint_last.1.total_in = f32[64,64,128]{2,1,0:T(8,128)S(1)} custom-call(s32[8]{0:T(128)S(1)} %concatenate.11.meta, s32[1536]{0:T(1024)S(1)} %add.79.tab, bf16[321,128,128]{2,1,0:T(8,128)(2,1)S(1)} %get-tuple-element.26.matrix, bf16[65,64,128]{2,1,0:T(8,128)(2,1)S(1)} %get-tuple-element.39.image), custom_call_target="tpu_custom_call" | custom-call | flops 335544320 | bytes 5242880 | tf_op jit(solution)/shard_map/adjoint_last/pallas_call | solution.py:405
  94.0 4.0 %collective-permute-done.13.low1 = bf16[1024,128]{1,0:T(8,128)(2,1)S(1)} collective-permute-done((bf16[1024,128]{1,0:T(8,128)(2,1)S(1)}, bf16[1024,128]{1,0:T(8,128)(2,1)S(1)}, u32[]{:S(2)}, u32[]{:S(2)}) %collective-permute-start.13) | collective-permute-done | bytes 262176 | tf_op jit(solution)/shard_map/ppermute | solution.py:297
  98.1 4.8 %collective-permute-done.14.high0 = bf16[1024,128]{1,0:T(8,128)(2,1)S(1)} collective-permute-done((bf16[1024,128]{1,0:T(8,128)(2,1)S(1)}, bf16[1024,128]{1,0:T(8,128)(2,1)S(1)}, u32[]{:S(2)}, u32[]{:S(2)}) %collective-permute-start.14) | collective-permute-done | bytes 262176 | tf_op jit(solution)/shard_map/ppermute | solution.py:297
  102.9 4.3 %collective-permute-done.15.high1 = bf16[1024,128]{1,0:T(8,128)(2,1)S(1)} collective-permute-done((bf16[1024,128]{1,0:T(8,128)(2,1)S(1)}, bf16[1024,128]{1,0:T(8,128)(2,1)S(1)}, u32[]{:S(2)}, u32[]{:S(2)}) %collective-permute-start.15) | collective-permute-done | bytes 262176 | tf_op jit(solution)/shard_map/ppermute | solution.py:297
  107.2 1.0 join_last.1
  108.2 27.2 %all_to_all.11 = f32[256,1,128]{2,1,0:T(1,128)S(1)} all-to-all(f32[256,1,128]{2,1,0:T(1,128)S(1)} %bitcast.22), channel_id=1, replica_groups=mesh['layer'=8,'tile'=32] {'layer','tile'}, dimensions={0} | all-to-all | bytes 262144 | tf_op jit(solution)/shard_map/all_to_all | solution.py:434
  135.4 1.3 write_out.1
  (46 shorter events, 7.6 us)
Async XLA Ops:
  0.0 1.2 copy-start.1
  1.2 0.8 copy-start.3
  2.0 16.3 %copy-start.2 = (bf16[1,1,64,8192]{3,2,1,0:T(8,128)(2,1)S(1)}, bf16[1,1,64,8192]{3,2,1,0:T(8,128)(2,1)}, u32[]{:S(2)}) copy-start(bf16[1,1,64,8192]{3,2,1,0:T(8,128)(2,1)} %param.13) | copy-start | bytes 3145732
  2.2 26.3 %collective-permute-start.2 = (bf16[1040,128]{1,0:T(8,128)(2,1)S(1)}, bf16[1040,128]{1,0:T(8,128)(2,1)S(1)}, u32[]{:S(2)}, u32[]{:S(2)}) collective-permute-start(bf16[1040,128]{1,0:T(8,128)(2,1)S(1)} %get-tuple-element.28), channel_id=1, source_target_pairs={{0,32},{32,64},{64,96},{96,128},{128,160},{160,192},{192,224},{1,3... | collective-permute-start | bytes 798728 | tf_op jit(solution)/shard_map/ppermute | solution.py:297
  6.3 22.2 %collective-permute-start = (bf16[1040,128]{1,0:T(8,128)(2,1)S(1)}, bf16[1040,128]{1,0:T(8,128)(2,1)S(1)}, u32[]{:S(2)}, u32[]{:S(2)}) collective-permute-start(bf16[1040,128]{1,0:T(8,128)(2,1)S(1)} %get-tuple-element.28), channel_id=1, source_target_pairs={{0,1},{1,2},{2,3},{3,4},{4,5},{5,6},{6,7},{7,8},{8,9},{9,10},{10,1... | collective-permute-start | bytes 798728 | tf_op jit(solution)/shard_map/ppermute | solution.py:297
  9.6 18.8 %collective-permute-start.3 = (bf16[1040,128]{1,0:T(8,128)(2,1)S(1)}, bf16[1040,128]{1,0:T(8,128)(2,1)S(1)}, u32[]{:S(2)}, u32[]{:S(2)}) collective-permute-start(bf16[1040,128]{1,0:T(8,128)(2,1)S(1)} %get-tuple-element.29), channel_id=1, source_target_pairs={{32,0},{64,32},{96,64},{128,96},{160,128},{192,160},{224,192},{33,... | collective-permute-start | bytes 798728 | tf_op jit(solution)/shard_map/ppermute | solution.py:297
  10.9 17.5 %collective-permute-start.1 = (bf16[1040,128]{1,0:T(8,128)(2,1)S(1)}, bf16[1040,128]{1,0:T(8,128)(2,1)S(1)}, u32[]{:S(2)}, u32[]{:S(2)}) collective-permute-start(bf16[1040,128]{1,0:T(8,128)(2,1)S(1)} %get-tuple-element.29), channel_id=1, source_target_pairs={{0,31},{1,0},{2,1},{3,2},{4,3},{5,4},{6,5},{7,6},{8,7},{9,8},{10,9... | collective-permute-start | bytes 798728 | tf_op jit(solution)/shard_map/ppermute | solution.py:297
  18.3 4.0 %copy-start = (bf16[1,1,320,128,128]{4,3,2,1,0:T(8,128)(2,1)S(1)}, bf16[1,1,320,128,128]{4,3,2,1,0:T(8,128)(2,1)}, u32[]{:S(2)}) copy-start(bf16[1,1,320,128,128]{4,3,2,1,0:T(8,128)(2,1)} %param.7) | copy-start | bytes 31457284
  22.2 0.8 copy-start.4
  31.7 13.6 %collective-permute-start.4 = (bf16[1024,128]{1,0:T(8,128)(2,1)S(1)}, bf16[1024,128]{1,0:T(8,128)(2,1)S(1)}, u32[]{:S(2)}, u32[]{:S(2)}) collective-permute-start(bf16[1024,128]{1,0:T(8,128)(2,1)S(1)} %get-tuple-element.31), channel_id=1, source_target_pairs={{0,1},{1,2},{2,3},{3,4},{4,5},{5,6},{6,7},{7,8},{8,9},{9,10},{10,1... | collective-permute-start | bytes 786440 | tf_op jit(solution)/shard_map/ppermute | solution.py:297
  33.9 11.3 %collective-permute-start.5 = (bf16[1024,128]{1,0:T(8,128)(2,1)S(1)}, bf16[1024,128]{1,0:T(8,128)(2,1)S(1)}, u32[]{:S(2)}, u32[]{:S(2)}) collective-permute-start(bf16[1024,128]{1,0:T(8,128)(2,1)S(1)} %get-tuple-element.32), channel_id=1, source_target_pairs={{0,32},{32,64},{64,96},{96,128},{128,160},{160,192},{192,224},{1,3... | collective-permute-start | bytes 786440 | tf_op jit(solution)/shard_map/ppermute | solution.py:297
  37.2 8.8 %collective-permute-start.6 = (bf16[1024,128]{1,0:T(8,128)(2,1)S(1)}, bf16[1024,128]{1,0:T(8,128)(2,1)S(1)}, u32[]{:S(2)}, u32[]{:S(2)}) collective-permute-start(bf16[1024,128]{1,0:T(8,128)(2,1)S(1)} %get-tuple-element.33), channel_id=1, source_target_pairs={{0,31},{1,0},{2,1},{3,2},{4,3},{5,4},{6,5},{7,6},{8,7},{9,8},{10,9... | collective-permute-start | bytes 786440 | tf_op jit(solution)/shard_map/ppermute | solution.py:297
  41.2 18.1 %collective-permute-start.7 = (bf16[1024,128]{1,0:T(8,128)(2,1)S(1)}, bf16[1024,128]{1,0:T(8,128)(2,1)S(1)}, u32[]{:S(2)}, u32[]{:S(2)}) collective-permute-start(bf16[1024,128]{1,0:T(8,128)(2,1)S(1)} %get-tuple-element.34), channel_id=1, source_target_pairs={{32,0},{64,32},{96,64},{128,96},{160,128},{192,160},{224,192},{33,... | collective-permute-start | bytes 786440 | tf_op jit(solution)/shard_map/ppermute | solution.py:297
  60.9 13.2 %collective-permute-start.11 = (bf16[1024,128]{1,0:T(8,128)(2,1)S(1)}, bf16[1024,128]{1,0:T(8,128)(2,1)S(1)}, u32[]{:S(2)}, u32[]{:S(2)}) collective-permute-start(bf16[1024,128]{1,0:T(8,128)(2,1)S(1)} %get-tuple-element.35.head), channel_id=1, source_target_pairs={{32,0},{64,32},{96,64},{128,96},{160,128},{192,160},{224,192},{33,... | collective-permute-start | bytes 786440 | tf_op jit(solution)/shard_map/ppermute | solution.py:297
  62.2 11.9 %collective-permute-start.9 = (bf16[1024,128]{1,0:T(8,128)(2,1)S(1)}, bf16[1024,128]{1,0:T(8,128)(2,1)S(1)}, u32[]{:S(2)}, u32[]{:S(2)}) collective-permute-start(bf16[1024,128]{1,0:T(8,128)(2,1)S(1)} %get-tuple-element.35.head), channel_id=1, source_target_pairs={{0,31},{1,0},{2,1},{3,2},{4,3},{5,4},{6,5},{7,6},{8,7},{9,8},{10,9... | collective-permute-start | bytes 786440 | tf_op jit(solution)/shard_map/ppermute | solution.py:297
  63.6 10.5 %collective-permute-start.10 = (bf16[1024,128]{1,0:T(8,128)(2,1)S(1)}, bf16[1024,128]{1,0:T(8,128)(2,1)S(1)}, u32[]{:S(2)}, u32[]{:S(2)}) collective-permute-start(bf16[1024,128]{1,0:T(8,128)(2,1)S(1)} %get-tuple-element.37.tail), channel_id=1, source_target_pairs={{0,32},{32,64},{64,96},{96,128},{128,160},{160,192},{192,224},{1,3... | collective-permute-start | bytes 786440 | tf_op jit(solution)/shard_map/ppermute | solution.py:297
  67.9 7.5 %collective-permute-start.8 = (bf16[1024,128]{1,0:T(8,128)(2,1)S(1)}, bf16[1024,128]{1,0:T(8,128)(2,1)S(1)}, u32[]{:S(2)}, u32[]{:S(2)}) collective-permute-start(bf16[1024,128]{1,0:T(8,128)(2,1)S(1)} %get-tuple-element.37.tail), channel_id=1, source_target_pairs={{0,1},{1,2},{2,3},{3,4},{4,5},{5,6},{6,7},{7,8},{8,9},{9,10},{10,1... | collective-permute-start | bytes 786440 | tf_op jit(solution)/shard_map/ppermute | solution.py:297
  78.5 15.5 %collective-permute-start.12 = (bf16[1024,128]{1,0:T(8,128)(2,1)S(1)}, bf16[1024,128]{1,0:T(8,128)(2,1)S(1)}, u32[]{:S(2)}, u32[]{:S(2)}) collective-permute-start(bf16[1024,128]{1,0:T(8,128)(2,1)S(1)} %get-tuple-element.40), channel_id=1, source_target_pairs={{0,1},{1,2},{2,3},{3,4},{4,5},{5,6},{6,7},{7,8},{8,9},{9,10},{10,1... | collective-permute-start | bytes 786440 | tf_op jit(solution)/shard_map/ppermute | solution.py:297
  81.7 16.3 %collective-permute-start.13 = (bf16[1024,128]{1,0:T(8,128)(2,1)S(1)}, bf16[1024,128]{1,0:T(8,128)(2,1)S(1)}, u32[]{:S(2)}, u32[]{:S(2)}) collective-permute-start(bf16[1024,128]{1,0:T(8,128)(2,1)S(1)} %get-tuple-element.41), channel_id=1, source_target_pairs={{0,32},{32,64},{64,96},{96,128},{128,160},{160,192},{192,224},{1,3... | collective-permute-start | bytes 786440 | tf_op jit(solution)/shard_map/ppermute | solution.py:297
  89.9 13.0 %collective-permute-start.14 = (bf16[1024,128]{1,0:T(8,128)(2,1)S(1)}, bf16[1024,128]{1,0:T(8,128)(2,1)S(1)}, u32[]{:S(2)}, u32[]{:S(2)}) collective-permute-start(bf16[1024,128]{1,0:T(8,128)(2,1)S(1)} %get-tuple-element.42), channel_id=1, source_target_pairs={{0,31},{1,0},{2,1},{3,2},{4,3},{5,4},{6,5},{7,6},{8,7},{9,8},{10,9... | collective-permute-start | bytes 786440 | tf_op jit(solution)/shard_map/ppermute | solution.py:297
  90.0 17.2 %collective-permute-start.15 = (bf16[1024,128]{1,0:T(8,128)(2,1)S(1)}, bf16[1024,128]{1,0:T(8,128)(2,1)S(1)}, u32[]{:S(2)}, u32[]{:S(2)}) collective-permute-start(bf16[1024,128]{1,0:T(8,128)(2,1)S(1)} %get-tuple-element.43), channel_id=1, source_target_pairs={{32,0},{64,32},{96,64},{128,96},{160,128},{192,160},{224,192},{33,... | collective-permute-start | bytes 786440 | tf_op jit(solution)/shard_map/ppermute | solution.py:297
where the time goes:
time: 136 us; the launch traced here: 137 us
  starting transfers between devices  42 us (31%)
  waiting for transfers between devices  28.5 us (21%)
  blocking collectives  27.2 us (20%)
  Pallas kernels  24.7 us (18%)
  local copies, waits for them, and re-layouts  6.73 us (5%)
  other arithmetic  5.77 us (4%)
  between operations  1.7 us (1%)
    ppermute x16, starting transfers between devices, shift(): return lax.ppermute(x, axis, route)  42 us
    ppermute x16, waiting for transfers between devices, shift(): return lax.ppermute(x, axis, route)  28.5 us
    all_to_all x1, blocking collectives, local(): sums = lax.all_to_all(message, ('layer', 'tile'), 0, 0, tiled=True)  27.2 us
    unnamed x10, local copies, waits for them, and re-layouts  6.72 us
    pallas_call x2, Pallas kernels, local(): call(functools.partial(rim_kernel, first), 'rim_first' if first else 'rim...  6.28 us
    pallas_call x2, Pallas kernels, local(): call(adjoint_kernel, 'adjoint_first' if first else 'adjoint_last', [block...  5.43 us
    pallas_call x1, Pallas kernels, local(): call(first_kernel, 'own_first', [VM((slots + 1, size, size), bf16), tall_...  5.41 us
    pallas_call x1, Pallas kernels, local(): call(own_kernel, 'own_next', [block_f32], [SMEM_SPEC] * 2 + [VMEM_SPEC] *...  3.56 us
  transfers between devices with their start and end apart: 16, of which 6 were waited for; matrix products, arithmetic and copies ran while one was open for 4% of the time, Pallas kernels for 11%

commit v1 on v0

--- a/solution.py
+++ b/solution.py
@@ -17,48 +17,69 @@
 FORWARD_OWN, FORWARD_RIM, ADJOINT_OWN, ADJOINT_RIM = range(4)
 
 
-def pair_tables(slot_row, slot_col, turned, live_count, num_blocks, places):
-    slots = slot_row.shape[0]
-    index = jnp.arange(slots, dtype=jnp.int32)
+def fill_tables(live_count, row, col, turned, num_blocks, tab):
+    f32, bf16 = jnp.float32, jnp.bfloat16
+    slots = row.shape[1]
+    places = tab.shape[1]
+    index = lax.broadcasted_iota(jnp.int32, (1, slots), 1)
     live = index < live_count
-    half = (slot_col >= num_blocks).astype(jnp.int32)
-    source = slot_col - half * num_blocks
-    keys = jnp.arange(num_blocks, dtype=jnp.int32)
-    place = jnp.arange(places, dtype=jnp.int32)
-    dest = jnp.stack([slot_row, slot_row, source, source])
-    operand = jnp.stack([source, source, slot_row, slot_row])
-    side = jnp.arange(4, dtype=jnp.int32)[:, None] & 1
-    used = live[None] & (half[None] == side)
-    earlier = index[:, None] < index[None, :]
-    hit = (dest[:, :, None] == dest[:, None, :]) & used[:, :, None] & earlier[None]
-    rank = jnp.sum(hit.astype(jnp.int32), axis=1)
-    member = (dest[:, :, None] == keys) & used[:, :, None]
-    pairs = (jnp.sum(member.astype(jnp.int32), axis=1) + 1) >> 1
-    before = jnp.sum(jnp.where(keys[:, None] < keys[None, :], pairs[:, :, None], 0), axis=1)
-    position = 2 * jnp.sum(jnp.where(dest[:, :, None] == keys, before[:, None, :], 0), axis=2) + rank
-    position = jnp.where(used, position, -1)
-    empty = num_blocks * 512
-    packed = index[None] + operand * 512 + dest * 65536 - empty
-    tables = jnp.sum(jnp.where(position[:, :, None] == place, packed[:, :, None], 0), axis=1) + empty
-    trips = (jnp.sum(pairs, axis=1) + UNROLL - 1) // UNROLL
+    rim = col >= num_blocks
+    source = col - jnp.where(rim, num_blocks, 0)
+    key = lax.broadcasted_iota(jnp.int32, (num_blocks, slots), 0)
+    place = lax.broadcasted_iota(jnp.int32, (places, slots), 0)
+    earlier = (
+        lax.broadcasted_iota(jnp.int32, (slots, slots), 0) < lax.broadcasted_iota(jnp.int32, (slots, slots), 1)
+    ).astype(f32).astype(bf16)
+    below = (
+        lax.broadcasted_iota(jnp.int32, (num_blocks, num_blocks), 1)
+        < lax.broadcasted_iota(jnp.int32, (num_blocks, num_blocks), 0)
+    ).astype(f32).astype(bf16)
+    lane = lax.broadcasted_iota(jnp.int32, (1, places), 1)
+    meta = jnp.zeros((1, places), jnp.int32)
+
+    def invert(position, parts):
+        found = (place == position).astype(f32).astype(bf16)
+        parts = parts + [jnp.zeros((1, slots), jnp.int32)] * (8 - len(parts))
+        values = jnp.concatenate([p.astype(f32) for p in parts], axis=0).astype(bf16)
+        moved = lax.dot_general(values, found, (((1,), (1,)), ((), ())), preferred_element_type=f32)
+        return moved.astype(jnp.int32)
+
+    for which in range(4):
+        dest, operand = (row, source) if which < ADJOINT_OWN else (source, row)
+        used = live & (rim if which % 2 else ~rim)
+        wanted = jnp.where(used, dest, -1)
+        member = (key == wanted).astype(f32)
+        before = jnp.dot(member.astype(bf16), earlier, preferred_element_type=f32)
+        pairs = (jnp.sum(member, axis=1, keepdims=True).astype(jnp.int32) + 1) >> 1
+        wide = jnp.broadcast_to(pairs.astype(f32), (num_blocks, 128)).astype(bf16)
+        offset = jnp.dot(below, wide, preferred_element_type=f32)[:, :1]
+        position = jnp.sum(member * (before + 2.0 * offset), axis=0, keepdims=True).astype(jnp.int32)
+        position = jnp.where(used, position, -1)
+        moved = invert(position, [index & 255, index >> 8, operand - num_blocks, dest])
+        packed = moved[0:1] + (moved[1:2] << 8) + ((moved[2:3] + num_blocks) << 9) + (moved[3:4] << 16)
+        tab[which : which + 1] = packed
+        count = jnp.sum(pairs.astype(f32), axis=0, keepdims=True).astype(jnp.int32)
+        meta = meta + jnp.where(lane == which, (count + (UNROLL - 1)) // UNROLL, 0)
     flip = live & (turned == 1)
-    flip_rank = jnp.sum((flip[:, None] & earlier).astype(jnp.int32), axis=0)
-    flip_rank = jnp.where(flip, flip_rank, -1)
-    flips = jnp.sum(jnp.where(flip_rank[:, None] == index[None, :], index[:, None] - slots, 0), axis=0) + slots
-    flip_trips = (jnp.sum(flip.astype(jnp.int32)) + TURN - 1) // TURN
-    meta = jnp.concatenate([trips, jnp.full((4,), flip_trips, jnp.int32)])
-    return tables.reshape(-1), flips, meta
-
-
-def pair_loop(which, meta, tab, source, matrix, acc):
-    start = which * (tab.shape[0] // 4)
+    ones = jnp.broadcast_to(flip.astype(f32), (8, slots))
+    rank = jnp.dot(ones.astype(bf16), earlier, preferred_element_type=f32)[:1].astype(jnp.int32)
+    rank = jnp.where(flip, rank, -1)
+    moved = invert(rank, [index & 255, index >> 8, flip.astype(jnp.int32)])
+    tab[4:5] = jnp.where(moved[2:3] == 1, moved[0:1] + (moved[1:2] << 8), slots)
+    count = jnp.sum(ones[:1], axis=1, keepdims=True).astype(jnp.int32)
+    meta = meta + jnp.where(lane == 4, (count + (TURN - 1)) // TURN, 0)
+    tab[5:6] = meta
+    tab[6:8] = jnp.zeros((2, places), jnp.int32)
+
+
+def pair_loop(which, tab, source, matrix, acc):
     transposed = which >= ADJOINT_OWN
 
     def body(step, carry):
         done = []
         for u in range(UNROLL):
-            place = start + (step * UNROLL + u) * 2
-            one, two = tab[place], tab[place + 1]
+            place = (step * UNROLL + u) * 2
+            one, two = tab[which, place], tab[which, place + 1]
             lhs = jnp.concatenate([source[(one >> 9) & 127], source[(two >> 9) & 127]], axis=1)
             first, second = matrix[one & 511], matrix[two & 511]
             rhs = jnp.concatenate([first, second], axis=0 if transposed else 1)
@@ -68,7 +89,7 @@
             acc[dest] += value
         return carry
 
-    lax.fori_loop(0, meta[which], body, 0)
+    lax.fori_loop(0, tab[5, which], body, 0)
 
 
 def clear(ref):
@@ -79,7 +100,7 @@
     lax.fori_loop(0, ref.shape[0], body, 0)
 
 
-def edge_kernel(start, density, head, tail, held, sems):
+def edge_kernel(start, density, head, tail, weights, held, raw, sems):
     size = head.shape[1]
     vectors = start.shape[0]
     edge = head.shape[0] // (vectors + 1)
@@ -89,24 +110,26 @@
     copies = [
         pltpu.make_async_copy(start.at[:, pl.ds(origin[i], width)], held.at[i], sems.at[i]) for i in range(2)
     ]
+    copies.append(pltpu.make_async_copy(density, raw, sems.at[2]))
     for copy in copies:
         copy.start()
+    copies[2].wait()
+    for b in range(weights.shape[0]):
+        weights[b : b + 1] = raw[:, b * size : (b + 1) * size].astype(jnp.float32)
     for i in range(2):
         copies[i].wait()
-        weights = []
+        first = origin[i] // size
         for b in range(edge):
-            cells = pl.ds(origin[i] + b * size, size)
-            weight = density[:, cells].astype(jnp.float32)
-            weights.append(weight)
-            value = held[i, :, b * size : (b + 1) * size].astype(jnp.float32) * weight
+            value = held[i, :, b * size : (b + 1) * size].astype(jnp.float32) * weights[first + b : first + b + 1]
             outs[i][b * vectors : (b + 1) * vectors] = value.astype(jnp.bfloat16)
-        outs[i][edge * vectors :] = jnp.concatenate(weights, axis=0).astype(jnp.bfloat16)
-
-
-def first_kernel(meta, tab, flips, blocks, start, density, matrix, rows, source, held, sems):
+        outs[i][edge * vectors :] = weights[first : first + edge].astype(jnp.bfloat16)
+
+
+def first_kernel(count, blocks, start, row, col, turned, weights, matrix, rows, tab, source, held, lists, smem, sems):
     slots = blocks.shape[0]
     part = slots // CHUNKS
-    copies = [pltpu.make_async_copy(start, held, sems.at[CHUNKS])]
+    small = [pltpu.make_async_copy(ref, lists.at[i], sems.at[CHUNKS + 1 + i]) for i, ref in enumerate((row, col, turned))]
+    copies = small + [pltpu.make_async_copy(start, held, sems.at[CHUNKS])]
     for c in range(CHUNKS):
         here = pl.ds(c * part, part)
         copies.append(pltpu.make_async_copy(blocks.at[here], matrix.at[here], sems.at[c]))
@@ -117,12 +140,17 @@
     clear(rows)
     matrix[slots] = jnp.zeros((size, size), matrix.dtype)
     source[num_blocks] = jnp.zeros(source.shape[1:], source.dtype)
-    copies[0].wait()
+    for copy in small:
+        copy.wait()
+    fill_tables(count[0], lists[0], lists[1], lists[2], num_blocks, tab)
+    table_copy = pltpu.make_async_copy(tab, smem, sems.at[CHUNKS + 4])
+    table_copy.start()
+    copies[3].wait()
     top = lax.broadcasted_iota(jnp.int32, (16, size), 0) == 0
 
     def fill(b, carry):
         cells = pl.ds(pl.multiple_of(b * size, size), size)
-        weight = density[:, cells].astype(jnp.float32)
+        weight = weights[pl.ds(b, 1)]
         source[b, :vectors] = (held[:, cells].astype(jnp.float32) * weight).astype(jnp.bfloat16)
         source[b, vectors:] = jnp.where(top, jnp.broadcast_to(weight, (16, size)), 0.0).astype(jnp.bfloat16)
         return carry
@@ -131,24 +159,25 @@
     across = lax.broadcasted_iota(jnp.int32, (size, size), 0)
     along = lax.broadcasted_iota(jnp.int32, (size, size), 1)
     mirror = (across + along == size - 1).astype(jnp.float32).astype(jnp.bfloat16)
-    for copy in copies[1:]:
+    table_copy.wait()
+    for copy in copies[4:]:
         copy.wait()
 
     def turn(step, carry):
         done = []
         for u in range(TURN):
-            slot = flips[step * TURN + u]
+            slot = smem[4, step * TURN + u]
             value = jnp.dot(matrix[slot], mirror, preferred_element_type=jnp.float32)
             done.append((slot, value.astype(jnp.bfloat16)))
         for slot, value in done:
             matrix[slot] = value
         return carry
 
-    lax.fori_loop(0, meta[4], turn, 0)
-    pair_loop(FORWARD_OWN, meta, tab, source, matrix, rows)
-
-
-def own_kernel(meta, tab, matrix, head, middle, tail, rows, source):
+    lax.fori_loop(0, smem[5, 4], turn, 0)
+    pair_loop(FORWARD_OWN, smem, source, matrix, rows)
+
+
+def own_kernel(tab, matrix, head, middle, tail, rows, source):
     clear(rows)
     num_blocks = rows.shape[0]
     edge = num_blocks // 4
@@ -158,10 +187,10 @@
         source[num_blocks - edge + b] = tail[b * vectors : (b + 1) * vectors]
     source[edge : num_blocks - edge] = middle[...]
     source[num_blocks] = jnp.zeros(source.shape[1:], source.dtype)
-    pair_loop(FORWARD_OWN, meta, tab, source, matrix, rows)
-
-
-def rim_kernel(first, meta, tab, matrix, rows_in, left, right, upper, lower, *rest):
+    pair_loop(FORWARD_OWN, tab, source, matrix, rows)
+
+
+def rim_kernel(first, tab, matrix, rows_in, left, right, upper, lower, *rest):
     del rows_in
     if first:
         rows, image, inverse = rest[:3]
@@ -184,7 +213,7 @@
                 source[side * edge + b, vectors:] = pad.astype(jnp.bfloat16)
     source[num_blocks] = jnp.zeros(source.shape[1:], source.dtype)
     clear(total)
-    pair_loop(FORWARD_RIM, meta, tab, source, matrix, rows)
+    pair_loop(FORWARD_RIM, tab, source, matrix, rows)
 
     def divide(b, carry):
         if first:
@@ -197,15 +226,15 @@
 
     lax.fori_loop(0, num_blocks, divide, 0, unroll=4)
     image[num_blocks] = jnp.zeros(image.shape[1:], image.dtype)
-    pair_loop(ADJOINT_RIM, meta, tab, image, matrix, total)
+    pair_loop(ADJOINT_RIM, tab, image, matrix, total)
     for side in range(4):
         for b in range(edge):
             backs[side][b * vectors : (b + 1) * vectors] = total[side * edge + b].astype(jnp.bfloat16)
 
 
-def adjoint_kernel(meta, tab, matrix, image, total):
+def adjoint_kernel(tab, matrix, image, total):
     clear(total)
-    pair_loop(ADJOINT_OWN, meta, tab, image, matrix, total)
+    pair_loop(ADJOINT_OWN, tab, image, matrix, total)
 
 
 def collect(total, density, lows, highs, store):
@@ -218,8 +247,7 @@
             here = b if parts is lows else b - (num_blocks - edge)
             rows = pl.ds(pl.multiple_of(here * vectors, vectors), vectors)
             value = value + (parts[0][rows].astype(jnp.float32) + parts[1][rows].astype(jnp.float32))
-        cells = pl.ds(pl.multiple_of(b * size, size), size)
-        weighted = value * density[:, cells].astype(jnp.float32)
+        weighted = value * density[pl.ds(b, 1)]
         store(b, value, weighted)
         return norm + weighted * value
 
@@ -327,7 +355,6 @@
     vectors, cells = start.shape
     num_blocks = cells // size
     edge = num_blocks // 4
-    weights = density[0]
     devices = lax.axis_size("layer") * lax.axis_size("tile")
     total_cells = cells * devices
     work = slots * size * size * vectors
@@ -340,34 +367,49 @@
     middle_type = VM((num_blocks - 2 * edge, vectors, size), bf16)
     norm_type = VM((8, vectors), f32)
 
-    head, tail = call(
+    def outside(x):
+        return pltpu.with_memory_space_constraint(x, pltpu.HBM)
+
+    start = outside(start)
+    head, tail, weights = call(
         edge_kernel,
         "edges",
-        [first_rim_type, first_rim_type],
-        [HBM_SPEC, VMEM_SPEC],
-        [VM((2, vectors, edge * size), bf16), pltpu.SemaphoreType.DMA((2,))],
+        [first_rim_type, first_rim_type, VM((num_blocks, size), f32)],
+        [HBM_SPEC, HBM_SPEC],
+        [
+            VM((2, vectors, edge * size), bf16),
+            VM((1, cells), bf16),
+            pltpu.SemaphoreType.DMA((3,)),
+        ],
         0,
         start.size,
-    )(start, weights)
+    )(start, outside(density[0]))
     rims = outward(head, tail)
 
     places = 2 * ((slots + num_blocks) // 2)
-    tab, flips, meta = pair_tables(
-        slot_rows[0, 0], slot_cols[0, 0], rotation[0, 0], live_block_count[0, 0], num_blocks, places
-    )
-    matrix, rows = call(
+    matrix, rows, tab = call(
         first_kernel,
         "own_first",
-        [VM((slots + 1, size, size), bf16), tall_f32],
-        [SMEM_SPEC] * 3 + [HBM_SPEC, HBM_SPEC, VMEM_SPEC],
+        [VM((slots + 1, size, size), bf16), tall_f32, VM((8, places), jnp.int32)],
+        [SMEM_SPEC] + [HBM_SPEC] * 5 + [VMEM_SPEC],
         [
             VM((num_blocks + 1, tall, size), bf16),
             VM((vectors, cells), bf16),
-            pltpu.SemaphoreType.DMA((CHUNKS + 1,)),
+            VM((3, 1, slots), jnp.int32),
+            pltpu.SMEM((8, places), jnp.int32),
+            pltpu.SemaphoreType.DMA((CHUNKS + 5,)),
         ],
         2 * work,
         2 * blocks.size * 2,
-    )(meta, tab, flips, blocks, start, weights)
+    )(
+        live_block_count[0],
+        outside(blocks),
+        start,
+        outside(slot_rows[0]),
+        outside(slot_cols[0]),
+        outside(rotation[0]),
+        weights,
+    )
 
     inverse = norm = None
     for turn in range(2):
@@ -377,11 +419,11 @@
                 own_kernel,
                 "own_next",
                 [block_f32],
-                [SMEM_SPEC] * 2 + [VMEM_SPEC] * 4,
+                [SMEM_SPEC] + [VMEM_SPEC] * 4,
                 [VM((num_blocks + 1, vectors, size), bf16)],
                 work,
                 blocks.size,
-            )(meta, tab, matrix, head, middle, tail)
+            )(tab, matrix, head, middle, tail)
             rims = outward(head, tail)
         extra = [] if first else [inverse]
         result = call(
@@ -390,12 +432,12 @@
             [tall_f32 if first else block_f32, image_type]
             + ([VM((num_blocks, 8, size), f32)] if first else [])
             + [rim_type] * 4,
-            [SMEM_SPEC] * 2 + [VMEM_SPEC] * (6 + len(extra)),
+            [SMEM_SPEC] + [VMEM_SPEC] * (6 + len(extra)),
             [VM((num_blocks + 1, tall if first else vectors, size), bf16), block_f32],
             2 * work,
             blocks.size,
-            {3: 0},
-        )(meta, tab, matrix, rows, *rims, *extra)
+            {2: 0},
+        )(tab, matrix, rows, *rims, *extra)
         image = result[1]
         if first:
             inverse = result[2]
@@ -406,11 +448,11 @@
             adjoint_kernel,
             "adjoint_first" if first else "adjoint_last",
             [block_f32],
-            [SMEM_SPEC] * 2 + [VMEM_SPEC] * 2,
+            [SMEM_SPEC] + [VMEM_SPEC] * 2,
             [],
             work,
             blocks.size,
-        )(meta, tab, matrix, image)
+        )(tab, matrix, image)
         if first:
             head, middle, tail, norm = call(
                 join_kernel,

time: 136 us -> 126 us (0.926)
  Pallas kernels: 24.7 us -> 34.6 us
  starting transfers between devices: 42 us -> 34.5 us
  local copies, waits for them, and re-layouts: 6.73 us -> 0 us
  other arithmetic: 5.77 us -> 0 us
    ppermute x16, starting transfers between devices: 42 us -> 34.5 us  [shift(): return lax.ppermute(x, axis, route)]
    unnamed x10 -> x0, local copies, waits for them, and re-layouts: 6.72 us -> none
    pallas_call x1, Pallas kernels: 5.41 us -> 9.89 us  [local(): call(first_kernel, 'own_first', [VM((slots + 1, size, size), bf16), tall_...]
    pallas_call x2, Pallas kernels: 6.28 us -> 9.59 us  [local(): call(functools.partial(rim_kernel, first), 'rim_first' if first else 'rim...]
    reduce_sum x8 -> x0, other arithmetic: 2.48 us -> none  [the longest x1 0.71 us: pair_tables(): flip_trips = (jnp.sum(flip.astype(jnp.int32)) + TURN - 1) // TURN]
    sub x3 -> x0, other arithmetic: 1.54 us -> none  [the longest x1 0.85 us: pair_tables(): packed = index[None] + operand * 512 + dest * 65536 - empty]
    pallas_call x2, Pallas kernels: 3.72 us -> 5.23 us  [the longest x1 4.13 us: local(): call(own_kernel, 'own_next', [block_f32], [SMEM_SPEC] + [VMEM_SPEC] * 4,...]
  transfers between devices with their start and end apart: 16 -> 16, of which waited for: 6 -> 7; matrix products, arithmetic and copies ran while one was open for 4% -> 0% of each run, Pallas kernels for 11% -> 16%
where the time goes in v1:
time: 126 us
  Pallas kernels  34.6 us (27%)
  starting transfers between devices  34.5 us (27%)
  waiting for transfers between devices  28.4 us (23%)
  blocking collectives  27.5 us (22%)
    ppermute x16, starting transfers between devices, shift(): return lax.ppermute(x, axis, route)  34.5 us
    ppermute x16, waiting for transfers between devices, shift(): return lax.ppermute(x, axis, route)  28.4 us
    all_to_all x1, blocking collectives, local(): sums = lax.all_to_all(message, ('layer', 'tile'), 0, 0, tiled=True)  27.5 us
    pallas_call x1, Pallas kernels, local(): call(first_kernel, 'own_first', [VM((slots + 1, size, size), bf16), tall_...  9.89 us
    pallas_call x2, Pallas kernels, local(): call(functools.partial(rim_kernel, first), 'rim_first' if first else 'rim...  9.59 us
    pallas_call x2, Pallas kernels, local(): call(adjoint_kernel, 'adjoint_first' if first else 'adjoint_last', [block...  6.07 us
    pallas_call x1, Pallas kernels, local(): call(own_kernel, 'own_next', [block_f32], [SMEM_SPEC] + [VMEM_SPEC] * 4,...  4.13 us
  transfers between devices with their start and end apart: 16, of which 7 were waited for; matrix products, arithmetic and copies ran while one was open for 0% of the time, Pallas kernels for 16%

profile of v1, /device:TPU:1, one launch (start us, length us, event | category | flops | bytes accessed | tf_op | source)
XLA Modules:
  0.0 125.8 jit_solution(8865090464687840243)
XLA Ops:
  0.0 1.1 edges.1
  1.1 4.0 %collective-permute-start.2 = (bf16[1040,128]{1,0:T(8,128)(2,1)S(1)}, bf16[1040,128]{1,0:T(8,128)(2,1)S(1)}, u32[]{:S(2)}, u32[]{:S(2)}) collective-permute-start(bf16[1040,128]{1,0:T(8,128)(2,1)S(1)} %get-tuple-element.32), channel_id=1, source_target_pairs={{0,32},{32,64},{64,96},{96,128},{128,160},{160,192},{192,224},{1,3... | collective-permute-start | bytes 798728 | tf_op jit(solution)/shard_map/ppermute | solution.py:325
  5.1 3.4 %collective-permute-start = (bf16[1040,128]{1,0:T(8,128)(2,1)S(1)}, bf16[1040,128]{1,0:T(8,128)(2,1)S(1)}, u32[]{:S(2)}, u32[]{:S(2)}) collective-permute-start(bf16[1040,128]{1,0:T(8,128)(2,1)S(1)} %get-tuple-element.32), channel_id=1, source_target_pairs={{0,1},{1,2},{2,3},{3,4},{4,5},{5,6},{6,7},{7,8},{8,9},{9,10},{10,1... | collective-permute-start | bytes 798728 | tf_op jit(solution)/shard_map/ppermute | solution.py:325
  8.4 1.3 %collective-permute-start.3 = (bf16[1040,128]{1,0:T(8,128)(2,1)S(1)}, bf16[1040,128]{1,0:T(8,128)(2,1)S(1)}, u32[]{:S(2)}, u32[]{:S(2)}) collective-permute-start(bf16[1040,128]{1,0:T(8,128)(2,1)S(1)} %get-tuple-element.33), channel_id=1, source_target_pairs={{32,0},{64,32},{96,64},{128,96},{160,128},{192,160},{224,192},{33,... | collective-permute-start | bytes 798728 | tf_op jit(solution)/shard_map/ppermute | solution.py:325
  9.7 0.1 collective-permute-start.1
  10.5 9.9 %own_first.1 = (bf16[321,128,128]{2,1,0:T(8,128)(2,1)S(1)}, f32[64,80,128]{2,1,0:T(8,128)S(1)}, s32[8,384]{1,0:T(8,128)S(1)}) custom-call(s32[1]{0:T(128)} %bitcast.12.count, bf16[320,128,128]{2,1,0:T(8,128)(2,1)} %bitcast.15, bf16[64,8192]{1,0:T(8,128)(2,1)} %bitcast.17, s32[1,320]{1,0:T(1,128)} %bitcast.19, s32[1,320]{1,0:T(1,128)} %bitcast.20, ...), custom_call_target="tpu_custom_call" | custom-call | flops 671088640 | bytes 20971520 | tf_op jit(solution)/shard_map/own_first/pallas_call | solution.py:390
  20.4 4.0 %collective-permute-done.3.lower = bf16[1040,128]{1,0:T(8,128)(2,1)S(1)} collective-permute-done((bf16[1040,128]{1,0:T(8,128)(2,1)S(1)}, bf16[1040,128]{1,0:T(8,128)(2,1)S(1)}, u32[]{:S(2)}, u32[]{:S(2)}) %collective-permute-start.3) | collective-permute-done | bytes 266272 | tf_op jit(solution)/shard_map/ppermute | solution.py:325
  24.4 4.8 %rim_first.1 = (f32[64,80,128]{2,1,0:T(8,128)S(1)}, bf16[65,64,128]{2,1,0:T(8,128)(2,1)S(1)}, f32[64,8,128]{2,1,0:T(8,128)S(1)}, bf16[1024,128]{1,0:T(8,128)(2,1...) custom-call(s32[8,384]{1,0:T(8,128)S(1)} %get-tuple-element.29.tab, ...), custom_call_target="tpu_custom_call", output_to_operand_aliasing={{0}: (2, {})} | custom-call | flops 671088640 | bytes 5242880 | tf_op jit(solution)/shard_map/rim_first/pallas_call | solution.py:429
  29.3 4.0 %collective-permute-start.5 = (bf16[1024,128]{1,0:T(8,128)(2,1)S(1)}, bf16[1024,128]{1,0:T(8,128)(2,1)S(1)}, u32[]{:S(2)}, u32[]{:S(2)}) collective-permute-start(bf16[1024,128]{1,0:T(8,128)(2,1)S(1)} %get-tuple-element.36), channel_id=1, source_target_pairs={{0,32},{32,64},{64,96},{96,128},{128,160},{160,192},{192,224},{1,3... | collective-permute-start | bytes 786440 | tf_op jit(solution)/shard_map/ppermute | solution.py:325
  33.4 0.8 collective-permute-start.6
  34.2 1.3 %collective-permute-start.7 = (bf16[1024,128]{1,0:T(8,128)(2,1)S(1)}, bf16[1024,128]{1,0:T(8,128)(2,1)S(1)}, u32[]{:S(2)}, u32[]{:S(2)}) collective-permute-start(bf16[1024,128]{1,0:T(8,128)(2,1)S(1)} %get-tuple-element.38), channel_id=1, source_target_pairs={{32,0},{64,32},{96,64},{128,96},{160,128},{192,160},{224,192},{33,... | collective-permute-start | bytes 786440 | tf_op jit(solution)/shard_map/ppermute | solution.py:325
  35.5 3.0 %adjoint_first.1.total = f32[64,64,128]{2,1,0:T(8,128)S(1)} custom-call(s32[8,384]{1,0:T(8,128)S(1)} %get-tuple-element.29.tab, bf16[321,128,128]{2,1,0:T(8,128)(2,1)S(1)} %get-tuple-element.30.matrix, bf16[65,64,128]{2,1,0:T(8,128)(2,1)S(1)} %get-tuple-element.34.image), custom_call_target="tpu_custom_call" | custom-call | flops 335544320 | bytes 5242880 | tf_op jit(solution)/shard_map/adjoint_first/pallas_call | solution.py:447
  38.6 5.6 %collective-permute-done.6.high0 = bf16[1024,128]{1,0:T(8,128)(2,1)S(1)} collective-permute-done((bf16[1024,128]{1,0:T(8,128)(2,1)S(1)}, bf16[1024,128]{1,0:T(8,128)(2,1)S(1)}, u32[]{:S(2)}, u32[]{:S(2)}) %collective-permute-start.6) | collective-permute-done | bytes 262176 | tf_op jit(solution)/shard_map/ppermute | solution.py:325
  44.1 5.4 %collective-permute-done.7.high1 = bf16[1024,128]{1,0:T(8,128)(2,1)S(1)} collective-permute-done((bf16[1024,128]{1,0:T(8,128)(2,1)S(1)}, bf16[1024,128]{1,0:T(8,128)(2,1)S(1)}, u32[]{:S(2)}, u32[]{:S(2)}) %collective-permute-start.7) | collective-permute-done | bytes 262176 | tf_op jit(solution)/shard_map/ppermute | solution.py:325
  49.5 1.5 %join.1 = (bf16[1024,128]{1,0:T(8,128)(2,1)S(1)}, bf16[32,64,128]{2,1,0:T(8,128)(2,1)S(1)}, bf16[1024,128]{1,0:T(8,128)(2,1)S(1)}, f32[8,64]{1,0:T(8,128)S(1)}) custom-call(f32[64,64,128]{2,1,0:T(8,128)S(1)} %adjoint_first.1.total, f32[64,128]{1,0:T(8,128)S(1)} %get-tuple-element.28.weights.density, bf16[1024,128]{1,0:T(8,128)(2,1)S(1)} %collective-permute-done.4.low0, ...), custom_call_target="tpu_custom_call" | custom-call | bytes 4194304 | tf_op jit(solution)/shard_map/join/pallas_call | solution.py:457
  51.0 1.3 %collective-permute-start.11 = (bf16[1024,128]{1,0:T(8,128)(2,1)S(1)}, bf16[1024,128]{1,0:T(8,128)(2,1)S(1)}, u32[]{:S(2)}, u32[]{:S(2)}) collective-permute-start(bf16[1024,128]{1,0:T(8,128)(2,1)S(1)} %get-tuple-element.39.head), channel_id=1, source_target_pairs={{32,0},{64,32},{96,64},{128,96},{160,128},{192,160},{224,192},{33,... | collective-permute-start | bytes 786440 | tf_op jit(solution)/shard_map/ppermute | solution.py:325
  52.4 0.5 collective-permute-start.9
  52.9 4.3 %collective-permute-start.10 = (bf16[1024,128]{1,0:T(8,128)(2,1)S(1)}, bf16[1024,128]{1,0:T(8,128)(2,1)S(1)}, u32[]{:S(2)}, u32[]{:S(2)}) collective-permute-start(bf16[1024,128]{1,0:T(8,128)(2,1)S(1)} %get-tuple-element.41.tail), channel_id=1, source_target_pairs={{0,32},{32,64},{64,96},{96,128},{128,160},{160,192},{192,224},{1,3... | collective-permute-start | bytes 786440 | tf_op jit(solution)/shard_map/ppermute | solution.py:325
  57.1 3.5 %collective-permute-start.8 = (bf16[1024,128]{1,0:T(8,128)(2,1)S(1)}, bf16[1024,128]{1,0:T(8,128)(2,1)S(1)}, u32[]{:S(2)}, u32[]{:S(2)}) collective-permute-start(bf16[1024,128]{1,0:T(8,128)(2,1)S(1)} %get-tuple-element.41.tail), channel_id=1, source_target_pairs={{0,1},{1,2},{2,3},{3,4},{4,5},{5,6},{6,7},{7,8},{8,9},{9,10},{10,1... | collective-permute-start | bytes 786440 | tf_op jit(solution)/shard_map/ppermute | solution.py:325
  60.7 4.1 %own_next.1.rows_in = f32[64,64,128]{2,1,0:T(8,128)S(1)} custom-call(s32[8,384]{1,0:T(8,128)S(1)} %get-tuple-element.29.tab, bf16[321,128,128]{2,1,0:T(8,128)(2,1)S(1)} %get-tuple-element.30.matrix, bf16[1024,128]{1,0:T(8,128)(2,1)S(1)} %get-tuple-element.39.head, bf16[32,64,128]{2,1,0:T(8,128)(2,1)S(1)} %get-tuple-element.40.middle, ...), custom_call_target="tpu_custom_call" | custom-call | flops 335544320 | bytes 5242880 | tf_op jit(solution)/shard_map/own_next/pallas_call | solution.py:418
  64.8 2.0 %collective-permute-done.8.left = bf16[1024,128]{1,0:T(8,128)(2,1)S(1)} collective-permute-done((bf16[1024,128]{1,0:T(8,128)(2,1)S(1)}, bf16[1024,128]{1,0:T(8,128)(2,1)S(1)}, u32[]{:S(2)}, u32[]{:S(2)}) %collective-permute-start.8) | collective-permute-done | bytes 262176 | tf_op jit(solution)/shard_map/ppermute | solution.py:325
  66.8 4.7 %rim_next.1 = (f32[64,64,128]{2,1,0:T(8,128)S(1)}, bf16[65,64,128]{2,1,0:T(8,128)(2,1)S(1)}, bf16[1024,128]{1,0:T(8,128)(2,1)S(1)}, bf16[1024,128]{1,0:T(8,128)(...) custom-call(s32[8,384]{1,0:T(8,128)S(1)} %get-tuple-element.29.tab, ...), custom_call_target="tpu_custom_call", output_to_operand_aliasing={{0}: (2, {})} | custom-call | flops 671088640 | bytes 5242880 | tf_op jit(solution)/shard_map/rim_next/pallas_call | solution.py:429
  71.5 3.3 %collective-permute-start.12 = (bf16[1024,128]{1,0:T(8,128)(2,1)S(1)}, bf16[1024,128]{1,0:T(8,128)(2,1)S(1)}, u32[]{:S(2)}, u32[]{:S(2)}) collective-permute-start(bf16[1024,128]{1,0:T(8,128)(2,1)S(1)} %get-tuple-element.44), channel_id=1, source_target_pairs={{0,1},{1,2},{2,3},{3,4},{4,5},{5,6},{6,7},{7,8},{8,9},{9,10},{10,1... | collective-permute-start | bytes 786440 | tf_op jit(solution)/shard_map/ppermute | solution.py:325
  74.8 5.3 %collective-permute-start.13 = (bf16[1024,128]{1,0:T(8,128)(2,1)S(1)}, bf16[1024,128]{1,0:T(8,128)(2,1)S(1)}, u32[]{:S(2)}, u32[]{:S(2)}) collective-permute-start(bf16[1024,128]{1,0:T(8,128)(2,1)S(1)} %get-tuple-element.45), channel_id=1, source_target_pairs={{0,32},{32,64},{64,96},{96,128},{128,160},{160,192},{192,224},{1,3... | collective-permute-start | bytes 786440 | tf_op jit(solution)/shard_map/ppermute | solution.py:325
  80.2 1.3 %collective-permute-start.15 = (bf16[1024,128]{1,0:T(8,128)(2,1)S(1)}, bf16[1024,128]{1,0:T(8,128)(2,1)S(1)}, u32[]{:S(2)}, u32[]{:S(2)}) collective-permute-start(bf16[1024,128]{1,0:T(8,128)(2,1)S(1)} %get-tuple-element.47), channel_id=1, source_target_pairs={{32,0},{64,32},{96,64},{128,96},{160,128},{192,160},{224,192},{33,... | collective-permute-start | bytes 786440 | tf_op jit(solution)/shard_map/ppermute | solution.py:325
  81.5 3.0 %adjoint_last.1.total_in = f32[64,64,128]{2,1,0:T(8,128)S(1)} custom-call(s32[8,384]{1,0:T(8,128)S(1)} %get-tuple-element.29.tab, bf16[321,128,128]{2,1,0:T(8,128)(2,1)S(1)} %get-tuple-element.30.matrix, bf16[65,64,128]{2,1,0:T(8,128)(2,1)S(1)} %get-tuple-element.43.image), custom_call_target="tpu_custom_call" | custom-call | flops 335544320 | bytes 5242880 | tf_op jit(solution)/shard_map/adjoint_last/pallas_call | solution.py:447
  84.5 3.8 %collective-permute-done.13.low1 = bf16[1024,128]{1,0:T(8,128)(2,1)S(1)} collective-permute-done((bf16[1024,128]{1,0:T(8,128)(2,1)S(1)}, bf16[1024,128]{1,0:T(8,128)(2,1)S(1)}, u32[]{:S(2)}, u32[]{:S(2)}) %collective-permute-start.13) | collective-permute-done | bytes 262176 | tf_op jit(solution)/shard_map/ppermute | solution.py:325
  88.4 3.1 %collective-permute-done.14.high0 = bf16[1024,128]{1,0:T(8,128)(2,1)S(1)} collective-permute-done((bf16[1024,128]{1,0:T(8,128)(2,1)S(1)}, bf16[1024,128]{1,0:T(8,128)(2,1)S(1)}, u32[]{:S(2)}, u32[]{:S(2)}) %collective-permute-start.14) | collective-permute-done | bytes 262176 | tf_op jit(solution)/shard_map/ppermute | solution.py:325
  91.5 4.5 %collective-permute-done.15.high1 = bf16[1024,128]{1,0:T(8,128)(2,1)S(1)} collective-permute-done((bf16[1024,128]{1,0:T(8,128)(2,1)S(1)}, bf16[1024,128]{1,0:T(8,128)(2,1)S(1)}, u32[]{:S(2)}, u32[]{:S(2)}) %collective-permute-start.15) | collective-permute-done | bytes 262176 | tf_op jit(solution)/shard_map/ppermute | solution.py:325
  96.0 0.9 join_last.1
  96.9 27.5 %all_to_all.11 = f32[256,1,128]{2,1,0:T(1,128)S(1)} all-to-all(f32[256,1,128]{2,1,0:T(1,128)S(1)} %bitcast.14), channel_id=1, replica_groups=mesh['layer'=8,'tile'=32] {'layer','tile'}, dimensions={0} | all-to-all | bytes 262144 | tf_op jit(solution)/shard_map/all_to_all | solution.py:476
  124.4 1.3 %write_out.1 = bf16[64,8192]{1,0:T(8,128)(2,1)} custom-call(f32[256,128]{1,0:T(8,128)S(1)} %bitcast.13, f32[64,64,128]{2,1,0:T(8,128)S(1)} %get-tuple-element.50.total), custom_call_target="tpu_custom_call" | custom-call | bytes 3145728 | tf_op jit(solution)/shard_map/write_out/pallas_call | solution.py:477
  (11 shorter events, 0.2 us)
Async XLA Ops:
  1.1 19.3 %collective-permute-start.2 = (bf16[1040,128]{1,0:T(8,128)(2,1)S(1)}, bf16[1040,128]{1,0:T(8,128)(2,1)S(1)}, u32[]{:S(2)}, u32[]{:S(2)}) collective-permute-start(bf16[1040,128]{1,0:T(8,128)(2,1)S(1)} %get-tuple-element.32), channel_id=1, source_target_pairs={{0,32},{32,64},{64,96},{96,128},{128,160},{160,192},{192,224},{1,3... | collective-permute-start | bytes 798728 | tf_op jit(solution)/shard_map/ppermute | solution.py:325
  5.1 15.3 %collective-permute-start = (bf16[1040,128]{1,0:T(8,128)(2,1)S(1)}, bf16[1040,128]{1,0:T(8,128)(2,1)S(1)}, u32[]{:S(2)}, u32[]{:S(2)}) collective-permute-start(bf16[1040,128]{1,0:T(8,128)(2,1)S(1)} %get-tuple-element.32), channel_id=1, source_target_pairs={{0,1},{1,2},{2,3},{3,4},{4,5},{5,6},{6,7},{7,8},{8,9},{9,10},{10,1... | collective-permute-start | bytes 798728 | tf_op jit(solution)/shard_map/ppermute | solution.py:325
  8.4 15.9 %collective-permute-start.3 = (bf16[1040,128]{1,0:T(8,128)(2,1)S(1)}, bf16[1040,128]{1,0:T(8,128)(2,1)S(1)}, u32[]{:S(2)}, u32[]{:S(2)}) collective-permute-start(bf16[1040,128]{1,0:T(8,128)(2,1)S(1)} %get-tuple-element.33), channel_id=1, source_target_pairs={{32,0},{64,32},{96,64},{128,96},{160,128},{192,160},{224,192},{33,... | collective-permute-start | bytes 798728 | tf_op jit(solution)/shard_map/ppermute | solution.py:325
  9.7 14.6 %collective-permute-start.1 = (bf16[1040,128]{1,0:T(8,128)(2,1)S(1)}, bf16[1040,128]{1,0:T(8,128)(2,1)S(1)}, u32[]{:S(2)}, u32[]{:S(2)}) collective-permute-start(bf16[1040,128]{1,0:T(8,128)(2,1)S(1)} %get-tuple-element.33), channel_id=1, source_target_pairs={{0,31},{1,0},{2,1},{3,2},{4,3},{5,4},{6,5},{7,6},{8,7},{9,8},{10,9... | collective-permute-start | bytes 798728 | tf_op jit(solution)/shard_map/ppermute | solution.py:325
  29.2 9.3 %collective-permute-start.4 = (bf16[1024,128]{1,0:T(8,128)(2,1)S(1)}, bf16[1024,128]{1,0:T(8,128)(2,1)S(1)}, u32[]{:S(2)}, u32[]{:S(2)}) collective-permute-start(bf16[1024,128]{1,0:T(8,128)(2,1)S(1)} %get-tuple-element.35), channel_id=1, source_target_pairs={{0,1},{1,2},{2,3},{3,4},{4,5},{5,6},{6,7},{7,8},{8,9},{9,10},{10,1... | collective-permute-start | bytes 786440 | tf_op jit(solution)/shard_map/ppermute | solution.py:325
  29.3 9.2 %collective-permute-start.5 = (bf16[1024,128]{1,0:T(8,128)(2,1)S(1)}, bf16[1024,128]{1,0:T(8,128)(2,1)S(1)}, u32[]{:S(2)}, u32[]{:S(2)}) collective-permute-start(bf16[1024,128]{1,0:T(8,128)(2,1)S(1)} %get-tuple-element.36), channel_id=1, source_target_pairs={{0,32},{32,64},{64,96},{96,128},{128,160},{160,192},{192,224},{1,3... | collective-permute-start | bytes 786440 | tf_op jit(solution)/shard_map/ppermute | solution.py:325
  33.4 10.8 %collective-permute-start.6 = (bf16[1024,128]{1,0:T(8,128)(2,1)S(1)}, bf16[1024,128]{1,0:T(8,128)(2,1)S(1)}, u32[]{:S(2)}, u32[]{:S(2)}) collective-permute-start(bf16[1024,128]{1,0:T(8,128)(2,1)S(1)} %get-tuple-element.37), channel_id=1, source_target_pairs={{0,31},{1,0},{2,1},{3,2},{4,3},{5,4},{6,5},{7,6},{8,7},{9,8},{10,9... | collective-permute-start | bytes 786440 | tf_op jit(solution)/shard_map/ppermute | solution.py:325
  34.2 15.3 %collective-permute-start.7 = (bf16[1024,128]{1,0:T(8,128)(2,1)S(1)}, bf16[1024,128]{1,0:T(8,128)(2,1)S(1)}, u32[]{:S(2)}, u32[]{:S(2)}) collective-permute-start(bf16[1024,128]{1,0:T(8,128)(2,1)S(1)} %get-tuple-element.38), channel_id=1, source_target_pairs={{32,0},{64,32},{96,64},{128,96},{160,128},{192,160},{224,192},{33,... | collective-permute-start | bytes 786440 | tf_op jit(solution)/shard_map/ppermute | solution.py:325
  51.0 13.7 %collective-permute-start.11 = (bf16[1024,128]{1,0:T(8,128)(2,1)S(1)}, bf16[1024,128]{1,0:T(8,128)(2,1)S(1)}, u32[]{:S(2)}, u32[]{:S(2)}) collective-permute-start(bf16[1024,128]{1,0:T(8,128)(2,1)S(1)} %get-tuple-element.39.head), channel_id=1, source_target_pairs={{32,0},{64,32},{96,64},{128,96},{160,128},{192,160},{224,192},{33,... | collective-permute-start | bytes 786440 | tf_op jit(solution)/shard_map/ppermute | solution.py:325
  52.4 12.4 %collective-permute-start.9 = (bf16[1024,128]{1,0:T(8,128)(2,1)S(1)}, bf16[1024,128]{1,0:T(8,128)(2,1)S(1)}, u32[]{:S(2)}, u32[]{:S(2)}) collective-permute-start(bf16[1024,128]{1,0:T(8,128)(2,1)S(1)} %get-tuple-element.39.head), channel_id=1, source_target_pairs={{0,31},{1,0},{2,1},{3,2},{4,3},{5,4},{6,5},{7,6},{8,7},{9,8},{10,9... | collective-permute-start | bytes 786440 | tf_op jit(solution)/shard_map/ppermute | solution.py:325
  52.9 11.9 %collective-permute-start.10 = (bf16[1024,128]{1,0:T(8,128)(2,1)S(1)}, bf16[1024,128]{1,0:T(8,128)(2,1)S(1)}, u32[]{:S(2)}, u32[]{:S(2)}) collective-permute-start(bf16[1024,128]{1,0:T(8,128)(2,1)S(1)} %get-tuple-element.41.tail), channel_id=1, source_target_pairs={{0,32},{32,64},{64,96},{96,128},{128,160},{160,192},{192,224},{1,3... | collective-permute-start | bytes 786440 | tf_op jit(solution)/shard_map/ppermute | solution.py:325
  57.1 9.6 %collective-permute-start.8 = (bf16[1024,128]{1,0:T(8,128)(2,1)S(1)}, bf16[1024,128]{1,0:T(8,128)(2,1)S(1)}, u32[]{:S(2)}, u32[]{:S(2)}) collective-permute-start(bf16[1024,128]{1,0:T(8,128)(2,1)S(1)} %get-tuple-element.41.tail), channel_id=1, source_target_pairs={{0,1},{1,2},{2,3},{3,4},{4,5},{5,6},{6,7},{7,8},{8,9},{9,10},{10,1... | collective-permute-start | bytes 786440 | tf_op jit(solution)/shard_map/ppermute | solution.py:325
  71.5 13.0 %collective-permute-start.12 = (bf16[1024,128]{1,0:T(8,128)(2,1)S(1)}, bf16[1024,128]{1,0:T(8,128)(2,1)S(1)}, u32[]{:S(2)}, u32[]{:S(2)}) collective-permute-start(bf16[1024,128]{1,0:T(8,128)(2,1)S(1)} %get-tuple-element.44), channel_id=1, source_target_pairs={{0,1},{1,2},{2,3},{3,4},{4,5},{5,6},{6,7},{7,8},{8,9},{9,10},{10,1... | collective-permute-start | bytes 786440 | tf_op jit(solution)/shard_map/ppermute | solution.py:325
  74.8 13.6 %collective-permute-start.13 = (bf16[1024,128]{1,0:T(8,128)(2,1)S(1)}, bf16[1024,128]{1,0:T(8,128)(2,1)S(1)}, u32[]{:S(2)}, u32[]{:S(2)}) collective-permute-start(bf16[1024,128]{1,0:T(8,128)(2,1)S(1)} %get-tuple-element.45), channel_id=1, source_target_pairs={{0,32},{32,64},{64,96},{96,128},{128,160},{160,192},{192,224},{1,3... | collective-permute-start | bytes 786440 | tf_op jit(solution)/shard_map/ppermute | solution.py:325
  80.1 11.4 %collective-permute-start.14 = (bf16[1024,128]{1,0:T(8,128)(2,1)S(1)}, bf16[1024,128]{1,0:T(8,128)(2,1)S(1)}, u32[]{:S(2)}, u32[]{:S(2)}) collective-permute-start(bf16[1024,128]{1,0:T(8,128)(2,1)S(1)} %get-tuple-element.46), channel_id=1, source_target_pairs={{0,31},{1,0},{2,1},{3,2},{4,3},{5,4},{6,5},{7,6},{8,7},{9,8},{10,9... | collective-permute-start | bytes 786440 | tf_op jit(solution)/shard_map/ppermute | solution.py:325
  80.2 15.8 %collective-permute-start.15 = (bf16[1024,128]{1,0:T(8,128)(2,1)S(1)}, bf16[1024,128]{1,0:T(8,128)(2,1)S(1)}, u32[]{:S(2)}, u32[]{:S(2)}) collective-permute-start(bf16[1024,128]{1,0:T(8,128)(2,1)S(1)} %get-tuple-element.47), channel_id=1, source_target_pairs={{32,0},{64,32},{96,64},{128,96},{160,128},{192,160},{224,192},{33,... | collective-permute-start | bytes 786440 | tf_op jit(solution)/shard_map/ppermute | solution.py:325

commit v2 on v1

--- a/solution.py
+++ b/solution.py
@@ -14,7 +14,7 @@
 VMEM_SPEC = pl.BlockSpec(memory_space=pltpu.VMEM)
 SMEM_SPEC = pl.BlockSpec(memory_space=pltpu.SMEM)
 HBM_SPEC = pl.BlockSpec(memory_space=pltpu.HBM)
-FORWARD_OWN, FORWARD_RIM, ADJOINT_OWN, ADJOINT_RIM = range(4)
+FORWARD_OWN, FORWARD_HEADS, FORWARD_TAILS, ADJOINT_OWN, ADJOINT_HEADS, ADJOINT_TAILS, FLIPS, TRIPS = range(8)
 
 
 def fill_tables(live_count, row, col, turned, num_blocks, tab):
@@ -23,8 +23,13 @@
     places = tab.shape[1]
     index = lax.broadcasted_iota(jnp.int32, (1, slots), 1)
     live = index < live_count
-    rim = col >= num_blocks
-    source = col - jnp.where(rim, num_blocks, 0)
+    edge = num_blocks // 4
+    outer = col - num_blocks
+    side = outer // edge
+    own = outer < 0
+    heads = (outer >= 0) & ((side & 1) == 1)
+    tails = (outer >= 0) & ((side & 1) == 0)
+    source = jnp.where(own, col, (side >> 1) * edge + outer - side * edge)
     key = lax.broadcasted_iota(jnp.int32, (num_blocks, slots), 0)
     place = lax.broadcasted_iota(jnp.int32, (places, slots), 0)
     earlier = (
@@ -44,9 +49,13 @@
         moved = lax.dot_general(values, found, (((1,), (1,)), ((), ())), preferred_element_type=f32)
         return moved.astype(jnp.int32)
 
-    for which in range(4):
-        dest, operand = (row, source) if which < ADJOINT_OWN else (source, row)
-        used = live & (rim if which % 2 else ~rim)
+    parts = ((own, num_blocks), (heads, 2 * edge), (tails, 2 * edge))
+    for which in range(6):
+        chosen, empty = parts[which % 3]
+        dest, operand = row, source
+        if which >= ADJOINT_OWN:
+            dest, operand, empty = source, row, num_blocks
+        used = live & chosen
         wanted = jnp.where(used, dest, -1)
         member = (key == wanted).astype(f32)
         before = jnp.dot(member.astype(bf16), earlier, preferred_element_type=f32)
@@ -55,8 +64,8 @@
         offset = jnp.dot(below, wide, preferred_element_type=f32)[:, :1]
         position = jnp.sum(member * (before + 2.0 * offset), axis=0, keepdims=True).astype(jnp.int32)
         position = jnp.where(used, position, -1)
-        moved = invert(position, [index & 255, index >> 8, operand - num_blocks, dest])
-        packed = moved[0:1] + (moved[1:2] << 8) + ((moved[2:3] + num_blocks) << 9) + (moved[3:4] << 16)
+        moved = invert(position, [index & 255, index >> 8, operand - empty, dest])
+        packed = moved[0:1] + (moved[1:2] << 8) + ((moved[2:3] + empty) << 9) + (moved[3:4] << 16)
         tab[which : which + 1] = packed
         count = jnp.sum(pairs.astype(f32), axis=0, keepdims=True).astype(jnp.int32)
         meta = meta + jnp.where(lane == which, (count + (UNROLL - 1)) // UNROLL, 0)
@@ -65,11 +74,10 @@
     rank = jnp.dot(ones.astype(bf16), earlier, preferred_element_type=f32)[:1].astype(jnp.int32)
     rank = jnp.where(flip, rank, -1)
     moved = invert(rank, [index & 255, index >> 8, flip.astype(jnp.int32)])
-    tab[4:5] = jnp.where(moved[2:3] == 1, moved[0:1] + (moved[1:2] << 8), slots)
+    tab[FLIPS : FLIPS + 1] = jnp.where(moved[2:3] == 1, moved[0:1] + (moved[1:2] << 8), slots)
     count = jnp.sum(ones[:1], axis=1, keepdims=True).astype(jnp.int32)
-    meta = meta + jnp.where(lane == 4, (count + (TURN - 1)) // TURN, 0)
-    tab[5:6] = meta
-    tab[6:8] = jnp.zeros((2, places), jnp.int32)
+    meta = meta + jnp.where(lane == FLIPS, (count + (TURN - 1)) // TURN, 0)
+    tab[TRIPS : TRIPS + 1] = meta
 
 
 def pair_loop(which, tab, source, matrix, acc):
@@ -89,7 +97,7 @@
             acc[dest] += value
         return carry
 
-    lax.fori_loop(0, tab[5, which], body, 0)
+    lax.fori_loop(0, tab[TRIPS, which], body, 0)
 
 
 def clear(ref):
@@ -166,14 +174,14 @@
     def turn(step, carry):
         done = []
         for u in range(TURN):
-            slot = smem[4, step * TURN + u]
+            slot = smem[FLIPS, step * TURN + u]
             value = jnp.dot(matrix[slot], mirror, preferred_element_type=jnp.float32)
             done.append((slot, value.astype(jnp.bfloat16)))
         for slot, value in done:
             matrix[slot] = value
         return carry
 
-    lax.fori_loop(0, smem[5, 4], turn, 0)
+    lax.fori_loop(0, smem[TRIPS, FLIPS], turn, 0)
     pair_loop(FORWARD_OWN, smem, source, matrix, rows)
 
 
@@ -190,19 +198,11 @@
     pair_loop(FORWARD_OWN, tab, source, matrix, rows)
 
 
-def rim_kernel(first, tab, matrix, rows_in, left, right, upper, lower, *rest):
-    del rows_in
-    if first:
-        rows, image, inverse = rest[:3]
-        rest = rest[3:]
-    else:
-        inverse, rows, image = rest[:3]
-        rest = rest[3:]
-    backs, (source, total) = rest[:4], rest[4:]
-    num_blocks, size = rows.shape[0], rows.shape[2]
-    vectors = image.shape[1]
-    edge = num_blocks // 4
-    for side, rim in enumerate((left, right, upper, lower)):
+def load_rims(first, rims, source):
+    edge = source.shape[0] // 2
+    vectors = rims[0].shape[0] // edge - (1 if first else 0)
+    size = source.shape[2]
+    for side, rim in enumerate(rims):
         for b in range(edge):
             source[side * edge + b, :vectors] = rim[b * vectors : (b + 1) * vectors]
         if first:
@@ -211,9 +211,35 @@
             for b in range(edge):
                 pad = jnp.where(top, jnp.broadcast_to(weights[b : b + 1], (16, size)), 0.0)
                 source[side * edge + b, vectors:] = pad.astype(jnp.bfloat16)
-    source[num_blocks] = jnp.zeros(source.shape[1:], source.dtype)
+    source[2 * edge] = jnp.zeros(source.shape[1:], source.dtype)
+
+
+def heads_kernel(first, tab, matrix, rows_in, right, lower, rows, source):
+    del rows_in
+    load_rims(first, (right, lower), source)
+    pair_loop(FORWARD_HEADS, tab, source, matrix, rows)
+
+
+def send_back(total, backs):
+    vectors = total.shape[1]
+    edge = total.shape[0] // 2
+    for side in range(2):
+        for b in range(edge):
+            backs[side][b * vectors : (b + 1) * vectors] = total[side * edge + b].astype(jnp.bfloat16)
+
+
+def middle_kernel(first, tab, matrix, rows_in, left, upper, *rest):
+    del rows_in
+    if first:
+        rows, image, inverse = rest[:3]
+    else:
+        inverse, rows, image = rest[:3]
+    right_back, lower_back, source, total = rest[3:]
+    num_blocks = rows.shape[0]
+    vectors = image.shape[1]
+    load_rims(first, (left, upper), source)
     clear(total)
-    pair_loop(FORWARD_RIM, tab, source, matrix, rows)
+    pair_loop(FORWARD_TAILS, tab, source, matrix, rows)
 
     def divide(b, carry):
         if first:
@@ -226,78 +252,72 @@
 
     lax.fori_loop(0, num_blocks, divide, 0, unroll=4)
     image[num_blocks] = jnp.zeros(image.shape[1:], image.dtype)
-    pair_loop(ADJOINT_RIM, tab, image, matrix, total)
-    for side in range(4):
-        for b in range(edge):
-            backs[side][b * vectors : (b + 1) * vectors] = total[side * edge + b].astype(jnp.bfloat16)
-
-
-def adjoint_kernel(tab, matrix, image, total):
+    pair_loop(ADJOINT_HEADS, tab, image, matrix, total)
+    send_back(total, (right_back, lower_back))
+
+
+def tails_kernel(tab, matrix, image, left_back, upper_back, total):
+    clear(total)
+    pair_loop(ADJOINT_TAILS, tab, image, matrix, total)
+    send_back(total, (left_back, upper_back))
+
+
+def adjoint_kernel(tab, matrix, image, weights, total, norm, *rest):
     clear(total)
     pair_loop(ADJOINT_OWN, tab, image, matrix, total)
-
-
-def collect(total, density, lows, highs, store):
-    num_blocks, vectors, size = total.shape
+    num_blocks = total.shape[0]
     edge = num_blocks // 4
 
-    def add(b, norm, parts):
+    def inside(b, sums):
         value = total[b]
-        if parts:
-            here = b if parts is lows else b - (num_blocks - edge)
-            rows = pl.ds(pl.multiple_of(here * vectors, vectors), vectors)
-            value = value + (parts[0][rows].astype(jnp.float32) + parts[1][rows].astype(jnp.float32))
-        weighted = value * density[pl.ds(b, 1)]
-        store(b, value, weighted)
-        return norm + weighted * value
-
-    norm = jnp.zeros((vectors, size), jnp.float32)
-    norm = lax.fori_loop(0, edge, lambda b, n: add(b, n, lows), norm)
-    norm = lax.fori_loop(edge, num_blocks - edge, lambda b, n: add(b, n, None), norm)
-    norm = lax.fori_loop(num_blocks - edge, num_blocks, lambda b, n: add(b, n, highs), norm)
+        weighted = value * weights[pl.ds(b, 1)]
+        if rest:
+            rest[0][b - edge] = weighted.astype(jnp.bfloat16)
+        return sums + weighted * value
+
+    zero = jnp.zeros(norm.shape, jnp.float32)
+    norm[...] = lax.fori_loop(edge, num_blocks - edge, inside, zero)
+
+
+def add_edge(total, weights, from_block, one, two, sums, store):
+    vectors = total.shape[1]
+
+    def add(b, carry):
+        rows = pl.ds(pl.multiple_of(b * vectors, vectors), vectors)
+        value = total[from_block + b] + (one[rows].astype(jnp.float32) + two[rows].astype(jnp.float32))
+        weighted = value * weights[pl.ds(from_block + b, 1)]
+        store(b, rows, value, weighted)
+        return carry + weighted * value
+
+    return lax.fori_loop(0, total.shape[0] // 4, add, sums, unroll=2)
+
+
+def join_kernel(tail, total, weights, one, two, norm_in, out, norm):
+    def store(b, rows, value, weighted):
+        out[rows] = weighted.astype(jnp.bfloat16)
+
+    from_block = total.shape[0] // 4 * 3 if tail else 0
+    norm[...] = add_edge(total, weights, from_block, one, two, norm_in[...], store)
+
+
+def sum_kernel(total_in, weights, low0, low1, high0, high1, norm_in, norm_first, total, message):
+    del total_in
+    sums = norm_in[...]
+    size = total.shape[2]
+    for from_block, one, two in ((0, low0, low1), (total.shape[0] // 4 * 3, high0, high1)):
+
+        def store(b, rows, value, weighted, from_block=from_block):
+            total[from_block + b] = value
+
+        sums = add_edge(total, weights, from_block, one, two, sums, store)
     ones = jnp.ones((8, size), jnp.float32)
-    return lax.dot_general(
-        ones, norm, (((1,), (1,)), ((), ())), precision=lax.Precision.HIGHEST, preferred_element_type=jnp.float32
-    )
-
-
-def join_kernel(total, density, low0, low1, high0, high1, head, middle, tail, norm):
-    num_blocks, vectors, size = total.shape
-    edge = num_blocks // 4
-    high_from = num_blocks - edge
-
-    def store(b, value, weighted):
-        del value
-        scaled = weighted.astype(jnp.bfloat16)
-
-        def rows(first):
-            return pl.ds(pl.multiple_of((b - first) * vectors, vectors), vectors)
-
-        @pl.when(b < edge)
-        def _():
-            head[rows(0)] = scaled
-
-        @pl.when((b >= edge) & (b < high_from))
-        def _():
-            middle[b - edge] = scaled
-
-        @pl.when(b >= high_from)
-        def _():
-            tail[rows(high_from)] = scaled
-
-    norm[...] = collect(total, density, (low0, low1), (high0, high1), store)
-
-
-def sum_kernel(total_in, density, low0, low1, high0, high1, norm, total, message):
-    del total_in
-
-    def store(b, value, weighted):
-        del weighted
-        total[b] = value
-
-    last = collect(total, density, (low0, low1), (high0, high1), store)
-    both = jnp.concatenate([norm[...], last], axis=1)[:1]
-    message[...] = jnp.broadcast_to(both, message.shape)
+    both = [
+        lax.dot_general(
+            ones, part, (((1,), (1,)), ((), ())), precision=lax.Precision.HIGHEST, preferred_element_type=jnp.float32
+        )
+        for part in (norm_first[...], sums)
+    ]
+    message[...] = jnp.broadcast_to(jnp.concatenate(both, axis=1)[:1], message.shape)
 
 
 def final_kernel(total_cells, sums, total, out):
@@ -325,13 +345,12 @@
     return lax.ppermute(x, axis, route)
 
 
-def outward(head, tail):
-    return (
-        shift(tail, "tile", 1, True),
-        shift(head, "tile", -1, True),
-        shift(tail, "layer", 1, False),
-        shift(head, "layer", -1, False),
-    )
+def heads_out(head):
+    return shift(head, "tile", -1, True), shift(head, "layer", -1, False)
+
+
+def tails_out(tail):
+    return shift(tail, "tile", 1, True), shift(tail, "layer", 1, False)
 
 
 def call(kernel, name, outs, in_specs, scratch, flops, nbytes, aliases={}):
@@ -365,7 +384,7 @@
     tall_f32 = VM((num_blocks, tall, size), f32)
     image_type = VM((num_blocks + 1, vectors, size), bf16)
     middle_type = VM((num_blocks - 2 * edge, vectors, size), bf16)
-    norm_type = VM((8, vectors), f32)
+    norm_type = VM((vectors, size), f32)
 
     def outside(x):
         return pltpu.with_memory_space_constraint(x, pltpu.HBM)
@@ -384,7 +403,7 @@
         0,
         start.size,
     )(start, outside(density[0]))
-    rims = outward(head, tail)
+    heads, tails = heads_out(head), tails_out(tail)
 
     places = 2 * ((slots + num_blocks) // 2)
     matrix, rows, tab = call(
@@ -411,9 +430,13 @@
         weights,
     )
 
-    inverse = norm = None
+    inverse = None
     for turn in range(2):
         first = turn == 0
+        rows_type = tall_f32 if first else block_f32
+        source_type = VM((2 * edge + 1, tall if first else vectors, size), bf16)
+        half_f32 = VM((2 * edge, vectors, size), f32)
+        suffix = "_first" if first else "_next"
         if not first:
             (rows,) = call(
                 own_kernel,
@@ -424,55 +447,84 @@
                 work,
                 blocks.size,
             )(tab, matrix, head, middle, tail)
-            rims = outward(head, tail)
+        (rows,) = call(
+            functools.partial(heads_kernel, first),
+            "heads" + suffix,
+            [rows_type],
+            [SMEM_SPEC] + [VMEM_SPEC] * 4,
+            [source_type],
+            work // 2,
+            blocks.size // 2,
+            {2: 0},
+        )(tab, matrix, rows, *heads)
         extra = [] if first else [inverse]
         result = call(
-            functools.partial(rim_kernel, first),
-            "rim_first" if first else "rim_next",
-            [tall_f32 if first else block_f32, image_type]
-            + ([VM((num_blocks, 8, size), f32)] if first else [])
-            + [rim_type] * 4,
-            [SMEM_SPEC] + [VMEM_SPEC] * (6 + len(extra)),
-            [VM((num_blocks + 1, tall if first else vectors, size), bf16), block_f32],
-            2 * work,
+            functools.partial(middle_kernel, first),
+            "middle" + suffix,
+            [rows_type, image_type] + ([VM((num_blocks, 8, size), f32)] if first else []) + [rim_type] * 2,
+            [SMEM_SPEC] + [VMEM_SPEC] * (4 + len(extra)),
+            [source_type, half_f32],
+            work,
             blocks.size,
             {2: 0},
-        )(tab, matrix, rows, *rims, *extra)
+        )(tab, matrix, rows, *tails, *extra)
         image = result[1]
         if first:
             inverse = result[2]
-        left, right, upper, lower = result[-4:]
+        right, lower = result[-2:]
         lows = (shift(right, "tile", 1, True), shift(lower, "layer", 1, False))
+        left, upper = call(
+            tails_kernel,
+            "tails" + suffix,
+            [rim_type] * 2,
+            [SMEM_SPEC] + [VMEM_SPEC] * 2,
+            [half_f32],
+            work // 2,
+            blocks.size // 2,
+        )(tab, matrix, image)
         highs = (shift(left, "tile", -1, True), shift(upper, "layer", -1, False))
-        (total,) = call(
+        result = call(
             adjoint_kernel,
-            "adjoint_first" if first else "adjoint_last",
-            [block_f32],
-            [SMEM_SPEC] + [VMEM_SPEC] * 2,
+            "adjoint" + suffix,
+            [block_f32, norm_type] + ([middle_type] if first else []),
+            [SMEM_SPEC] + [VMEM_SPEC] * 3,
             [],
             work,
             blocks.size,
-        )(tab, matrix, image)
+        )(tab, matrix, image, weights)
+        total, norm = result[:2]
         if first:
-            head, middle, tail, norm = call(
-                join_kernel,
-                "join",
-                [rim_type, middle_type, rim_type, norm_type],
-                [VMEM_SPEC] * 6,
+            middle = result[2]
+            head, norm = call(
+                functools.partial(join_kernel, False),
+                "join_head",
+                [rim_type, norm_type],
+                [VMEM_SPEC] * 5,
                 [],
                 0,
-                num_blocks * vectors * size * 8,
-            )(total, weights, *lows, *highs)
+                edge * vectors * size * 8,
+            )(total, weights, *lows, norm)
+            heads = heads_out(head)
+            tail, norm_first = call(
+                functools.partial(join_kernel, True),
+                "join_tail",
+                [rim_type, norm_type],
+                [VMEM_SPEC] * 5,
+                [],
+                0,
+                edge * vectors * size * 8,
+            )(total, weights, *highs, norm)
+            tails = tails_out(tail)
     total, message = call(
         sum_kernel,
         "join_last",
         [block_f32, VM((devices, 2 * vectors), f32)],
-        [VMEM_SPEC] * 7,
+        [VMEM_SPEC] * 8,
         [],
         0,
-        num_blocks * vectors * size * 8,
+        2 * edge * vectors * size * 8,
         {0: 0},
-    )(total, weights, *lows, *highs, norm)
+    )(total, weights, *lows, *highs, norm, norm_first)
     sums = lax.all_to_all(message, ("layer", "tile"), 0, 0, tiled=True)
     out = call(
         functools.partial(final_kernel, total_cells),

time: 126 us -> 118 us (0.937)
  waiting for transfers between devices: 28.4 us -> 4.19 us
  starting transfers between devices: 34.5 us -> 52.6 us
  Pallas kernels: 34.6 us -> 30.3 us
  blocking collectives: 27.5 us -> 29.8 us
    ppermute x16, waiting for transfers between devices: 28.4 us -> 4.19 us  [shift(): return lax.ppermute(x, axis, route)]
    ppermute x16, starting transfers between devices: 34.5 us -> 52.6 us  [shift(): return lax.ppermute(x, axis, route)]
    pallas_call x1, Pallas kernels: 9.89 us -> 7.6 us  [local(): call(first_kernel, 'own_first', [VM((slots + 1, size, size), bf16), tall_...]
    all_to_all x1, blocking collectives: 27.5 us -> 29.8 us  [local(): sums = lax.all_to_all(message, ('layer', 'tile'), 0, 0, tiled=True)]
    pallas_call x5 -> x10, Pallas kernels: 17.2 us -> 16 us  [the longest x2 6.1 us: local(): call(adjoint_kernel, 'adjoint' + suffix, [block_f32, norm_type] + ([middl...]
  transfers between devices with their start and end apart: 16 -> 16, of which waited for: 7 -> 2; matrix products, arithmetic and copies ran while one was open for 0% -> 0% of each run, Pallas kernels for 16% -> 20%
where the time goes in v2:
time: 118 us
  starting transfers between devices  52.6 us (45%)
  Pallas kernels  30.3 us (26%)
  blocking collectives  29.8 us (25%)
  waiting for transfers between devices  4.19 us (4%)
    ppermute x16, starting transfers between devices, shift(): return lax.ppermute(x, axis, route)  52.6 us
    all_to_all x1, blocking collectives, local(): sums = lax.all_to_all(message, ('layer', 'tile'), 0, 0, tiled=True)  29.8 us
    pallas_call x1, Pallas kernels, local(): call(first_kernel, 'own_first', [VM((slots + 1, size, size), bf16), tall_...  7.6 us
    pallas_call x2, Pallas kernels, local(): call(adjoint_kernel, 'adjoint' + suffix, [block_f32, norm_type] + ([middl...  6.1 us
    pallas_call x2, Pallas kernels, local(): call(functools.partial(middle_kernel, first), 'middle' + suffix, [rows_ty...  4.22 us
    ppermute x16, waiting for transfers between devices, shift(): return lax.ppermute(x, axis, route)  4.19 us
    pallas_call x1, Pallas kernels, local(): call(own_kernel, 'own_next', [block_f32], [SMEM_SPEC] + [VMEM_SPEC] * 4,...  3.62 us
    pallas_call x2, Pallas kernels, local(): call(tails_kernel, 'tails' + suffix, [rim_type] * 2, [SMEM_SPEC] + [VMEM_...  2.78 us
  transfers between devices with their start and end apart: 16, of which 2 were waited for; matrix products, arithmetic and copies ran while one was open for 0% of the time, Pallas kernels for 20%

profile of v2, /device:TPU:1, one launch (start us, length us, event | category | flops | bytes accessed | tf_op | source)
XLA Modules:
  0.0 117.7 jit_solution(1000744135239286432)
XLA Ops:
  0.0 1.1 edges.1
  1.1 1.3 %collective-permute-start.1 = (bf16[1040,128]{1,0:T(8,128)(2,1)S(1)}, bf16[1040,128]{1,0:T(8,128)(2,1)S(1)}, u32[]{:S(2)}, u32[]{:S(2)}) collective-permute-start(bf16[1040,128]{1,0:T(8,128)(2,1)S(1)} %get-tuple-element.37), channel_id=1, source_target_pairs={{32,0},{64,32},{96,64},{128,96},{160,128},{192,160},{224,192},{33,... | collective-permute-start | bytes 798728 | tf_op jit(solution)/shard_map/ppermute | solution.py:345
  2.4 3.3 %collective-permute-start = (bf16[1040,128]{1,0:T(8,128)(2,1)S(1)}, bf16[1040,128]{1,0:T(8,128)(2,1)S(1)}, u32[]{:S(2)}, u32[]{:S(2)}) collective-permute-start(bf16[1040,128]{1,0:T(8,128)(2,1)S(1)} %get-tuple-element.37), channel_id=1, source_target_pairs={{0,31},{1,0},{2,1},{3,2},{4,3},{5,4},{6,5},{7,6},{8,7},{9,8},{10,9... | collective-permute-start | bytes 798728 | tf_op jit(solution)/shard_map/ppermute | solution.py:345
  5.7 4.3 %collective-permute-start.3 = (bf16[1040,128]{1,0:T(8,128)(2,1)S(1)}, bf16[1040,128]{1,0:T(8,128)(2,1)S(1)}, u32[]{:S(2)}, u32[]{:S(2)}) collective-permute-start(bf16[1040,128]{1,0:T(8,128)(2,1)S(1)} %get-tuple-element.38), channel_id=1, source_target_pairs={{0,32},{32,64},{64,96},{96,128},{128,160},{160,192},{192,224},{1,3... | collective-permute-start | bytes 798728 | tf_op jit(solution)/shard_map/ppermute | solution.py:345
  10.0 1.3 %collective-permute-start.2 = (bf16[1040,128]{1,0:T(8,128)(2,1)S(1)}, bf16[1040,128]{1,0:T(8,128)(2,1)S(1)}, u32[]{:S(2)}, u32[]{:S(2)}) collective-permute-start(bf16[1040,128]{1,0:T(8,128)(2,1)S(1)} %get-tuple-element.38), channel_id=1, source_target_pairs={{0,1},{1,2},{2,3},{3,4},{4,5},{5,6},{6,7},{7,8},{8,9},{9,10},{10,1... | collective-permute-start | bytes 798728 | tf_op jit(solution)/shard_map/ppermute | solution.py:345
  11.9 7.6 %own_first.1 = (bf16[321,128,128]{2,1,0:T(8,128)(2,1)S(1)}, f32[64,80,128]{2,1,0:T(8,128)S(1)}, s32[8,384]{1,0:T(8,128)S(1)}) custom-call(s32[1]{0:T(128)} %bitcast.12.count, bf16[320,128,128]{2,1,0:T(8,128)(2,1)} %bitcast.15, bf16[64,8192]{1,0:T(8,128)(2,1)} %bitcast.17, s32[1,320]{1,0:T(1,128)} %bitcast.19, s32[1,320]{1,0:T(1,128)} %bitcast.20, ...), custom_call_target="tpu_custom_call" | custom-call | flops 671088640 | bytes 20971520 | tf_op jit(solution)/shard_map/own_first/pallas_call | solution.py:409
  19.6 1.3 %heads_first.1.rows_in = f32[64,80,128]{2,1,0:T(8,128)S(1)} custom-call(s32[8,384]{1,0:T(8,128)S(1)} %get-tuple-element.34.tab, bf16[321,128,128]{2,1,0:T(8,128)(2,1)S(1)} %get-tuple-element.35.matrix, f32[64,80,128]{2,1,0:T(8,128)S(1)} %get-tuple-element.36.rows_in, ...), custom_call_target="tpu_custom_call", output_to_operand_aliasing={{}: (2, {})} | custom-call | flops 167772160 | bytes 2621440 | tf_op jit(solution)/shard_map/heads_first/pallas_call | solution.py:450
  20.9 2.2 %middle_first.1 = (f32[64,80,128]{2,1,0:T(8,128)S(1)}, bf16[65,64,128]{2,1,0:T(8,128)(2,1)S(1)}, f32[64,8,128]{2,1,0:T(8,128)S(1)}, bf16[1024,128]{1,0:T(8,128)(2,1)S(1)}, bf16[1024,128]{1,0:T(8,128)(2,1)S(1)}) custom-call(s32[8,384]{1,0:T(8,128)S(1)} %get-tuple-element.34.tab, ...), custom_call_target="tpu_custom_call", output_to_operand_aliasing={{0}: (2, {})} | custom-call | flops 335544320 | bytes 5242880 | tf_op jit(solution)/shard_map/middle_first/pallas_call | solution.py:461
  23.0 0.3 collective-permute-start.4
  23.3 8.2 %collective-permute-start.5 = (bf16[1024,128]{1,0:T(8,128)(2,1)S(1)}, bf16[1024,128]{1,0:T(8,128)(2,1)S(1)}, u32[]{:S(2)}, u32[]{:S(2)}) collective-permute-start(bf16[1024,128]{1,0:T(8,128)(2,1)S(1)} %get-tuple-element.42), channel_id=1, source_target_pairs={{0,32},{32,64},{64,96},{96,128},{128,160},{160,192},{192,224},{1,3... | collective-permute-start | bytes 786440 | tf_op jit(solution)/shard_map/ppermute | solution.py:345
  31.5 1.3 %tails_first.1 = (bf16[1024,128]{1,0:T(8,128)(2,1)S(1)}, bf16[1024,128]{1,0:T(8,128)(2,1)S(1)}) custom-call(s32[8,384]{1,0:T(8,128)S(1)} %get-tuple-element.34.tab, bf16[321,128,128]{2,1,0:T(8,128)(2,1)S(1)} %get-tuple-element.35.matrix, bf16[65,64,128]{2,1,0:T(8,128)(2,1)S(1)} %get-tuple-element.39.image), custom_call_target="tpu_custom_call" | custom-call | flops 167772160 | bytes 2621440 | tf_op jit(solution)/shard_map/tails_first/pallas_call | solution.py:476
  32.8 0.8 collective-permute-start.6
  33.7 1.3 %collective-permute-start.7 = (bf16[1024,128]{1,0:T(8,128)(2,1)S(1)}, bf16[1024,128]{1,0:T(8,128)(2,1)S(1)}, u32[]{:S(2)}, u32[]{:S(2)}) collective-permute-start(bf16[1024,128]{1,0:T(8,128)(2,1)S(1)} %get-tuple-element.47), channel_id=1, source_target_pairs={{32,0},{64,32},{96,64},{128,96},{160,128},{192,160},{224,192},{33,... | collective-permute-start | bytes 786440 | tf_op jit(solution)/shard_map/ppermute | solution.py:345
  35.0 3.1 %adjoint_first.1 = (f32[64,64,128]{2,1,0:T(8,128)S(1)}, f32[64,128]{1,0:T(8,128)S(1)}, bf16[32,64,128]{2,1,0:T(8,128)(2,1)S(1)}) custom-call(s32[8,384]{1,0:T(8,128)S(1)} %get-tuple-element.34.tab, bf16[321,128,128]{2,1,0:T(8,128)(2,1)S(1)} %get-tuple-element.35.matrix, bf16[65,64,128]{2,1,0:T(8,128)(2,1)S(1)} %get-tuple-element.39.image, ...), custom_call_target="tpu_custom_call" | custom-call | flops 335544320 | bytes 5242880 | tf_op jit(solution)/shard_map/adjoint_first/pallas_call | solution.py:486
  38.3 1.3 %collective-permute-start.9 = (bf16[1024,128]{1,0:T(8,128)(2,1)S(1)}, bf16[1024,128]{1,0:T(8,128)(2,1)S(1)}, u32[]{:S(2)}, u32[]{:S(2)}) collective-permute-start(bf16[1024,128]{1,0:T(8,128)(2,1)S(1)} %get-tuple-element.44.head), channel_id=1, source_target_pairs={{32,0},{64,32},{96,64},{128,96},{160,128},{192,160},{224,192},{33,... | collective-permute-start | bytes 786440 | tf_op jit(solution)/shard_map/ppermute | solution.py:345
  39.6 6.5 %collective-permute-start.8 = (bf16[1024,128]{1,0:T(8,128)(2,1)S(1)}, bf16[1024,128]{1,0:T(8,128)(2,1)S(1)}, u32[]{:S(2)}, u32[]{:S(2)}) collective-permute-start(bf16[1024,128]{1,0:T(8,128)(2,1)S(1)} %get-tuple-element.44.head), channel_id=1, source_target_pairs={{0,31},{1,0},{2,1},{3,2},{4,3},{5,4},{6,5},{7,6},{8,7},{9,8},{10,9... | collective-permute-start | bytes 786440 | tf_op jit(solution)/shard_map/ppermute | solution.py:345
  46.3 5.2 %collective-permute-start.11 = (bf16[1024,128]{1,0:T(8,128)(2,1)S(1)}, bf16[1024,128]{1,0:T(8,128)(2,1)S(1)}, u32[]{:S(2)}, u32[]{:S(2)}) collective-permute-start(bf16[1024,128]{1,0:T(8,128)(2,1)S(1)} %get-tuple-element.49.tail), channel_id=1, source_target_pairs={{0,32},{32,64},{64,96},{96,128},{128,160},{160,192},{192,224},{1,3... | collective-permute-start | bytes 786440 | tf_op jit(solution)/shard_map/ppermute | solution.py:345
  51.5 6.7 %collective-permute-start.10 = (bf16[1024,128]{1,0:T(8,128)(2,1)S(1)}, bf16[1024,128]{1,0:T(8,128)(2,1)S(1)}, u32[]{:S(2)}, u32[]{:S(2)}) collective-permute-start(bf16[1024,128]{1,0:T(8,128)(2,1)S(1)} %get-tuple-element.49.tail), channel_id=1, source_target_pairs={{0,1},{1,2},{2,3},{3,4},{4,5},{5,6},{6,7},{7,8},{8,9},{9,10},{10,1... | collective-permute-start | bytes 786440 | tf_op jit(solution)/shard_map/ppermute | solution.py:345
  58.2 3.6 %own_next.1.rows_in = f32[64,64,128]{2,1,0:T(8,128)S(1)} custom-call(s32[8,384]{1,0:T(8,128)S(1)} %get-tuple-element.34.tab, bf16[321,128,128]{2,1,0:T(8,128)(2,1)S(1)} %get-tuple-element.35.matrix, bf16[1024,128]{1,0:T(8,128)(2,1)S(1)} %get-tuple-element.44.head, bf16[32,64,128]{2,1,0:T(8,128)(2,1)S(1)} %get-tuple-element.45.middle, ...), custom_call_target="tpu_custom_call" | custom-call | flops 335544320 | bytes 5242880 | tf_op jit(solution)/shard_map/own_next/pallas_call | solution.py:441
  61.8 1.3 %heads_next.1.rows_in = f32[64,64,128]{2,1,0:T(8,128)S(1)} custom-call(s32[8,384]{1,0:T(8,128)S(1)} %get-tuple-element.34.tab, bf16[321,128,128]{2,1,0:T(8,128)(2,1)S(1)} %get-tuple-element.35.matrix, f32[64,64,128]{2,1,0:T(8,128)S(1)} %own_next.1.rows_in, bf16[1024,128]{1,0:T(8,128)(2,1)S(1)} %collective-permute-done.8.right, ...), custom_call_target="tpu_custom_call", output_to_operand_aliasing={{}: (2, {})} | custom-call | flops 167772160 | bytes 2621440 | tf_op jit(solution)/shard_map/heads_next/pallas_call | solution.py:450
  63.1 2.1 %middle_next.1 = (f32[64,64,128]{2,1,0:T(8,128)S(1)}, bf16[65,64,128]{2,1,0:T(8,128)(2,1)S(1)}, bf16[1024,128]{1,0:T(8,128)(2,1)S(1)}, bf16[1024,128]{1,0:T(8,128)(2,1)S(1)}) custom-call(s32[8,384]{1,0:T(8,128)S(1)} %get-tuple-element.34.tab, bf16[321,128,128]{2,1,0:T(8,128)(2,1)S(1)} %get-tuple-element.35.matrix, ...), custom_call_target="tpu_custom_call", output_to_operand_aliasing={{0}: (2, {})} | custom-call | flops 335544320 | bytes 5242880 | tf_op jit(solution)/shard_map/middle_next/pallas_call | solution.py:461
  65.2 2.8 %collective-permute-start.12 = (bf16[1024,128]{1,0:T(8,128)(2,1)S(1)}, bf16[1024,128]{1,0:T(8,128)(2,1)S(1)}, u32[]{:S(2)}, u32[]{:S(2)}) collective-permute-start(bf16[1024,128]{1,0:T(8,128)(2,1)S(1)} %get-tuple-element.53), channel_id=1, source_target_pairs={{0,1},{1,2},{2,3},{3,4},{4,5},{5,6},{6,7},{7,8},{8,9},{9,10},{10,1... | collective-permute-start | bytes 786440 | tf_op jit(solution)/shard_map/ppermute | solution.py:345
  68.0 3.2 %collective-permute-start.13 = (bf16[1024,128]{1,0:T(8,128)(2,1)S(1)}, bf16[1024,128]{1,0:T(8,128)(2,1)S(1)}, u32[]{:S(2)}, u32[]{:S(2)}) collective-permute-start(bf16[1024,128]{1,0:T(8,128)(2,1)S(1)} %get-tuple-element.54), channel_id=1, source_target_pairs={{0,32},{32,64},{64,96},{96,128},{128,160},{160,192},{192,224},{1,3... | collective-permute-start | bytes 786440 | tf_op jit(solution)/shard_map/ppermute | solution.py:345
  71.3 1.5 %tails_next.1 = (bf16[1024,128]{1,0:T(8,128)(2,1)S(1)}, bf16[1024,128]{1,0:T(8,128)(2,1)S(1)}) custom-call(s32[8,384]{1,0:T(8,128)S(1)} %get-tuple-element.34.tab, bf16[321,128,128]{2,1,0:T(8,128)(2,1)S(1)} %get-tuple-element.35.matrix, bf16[65,64,128]{2,1,0:T(8,128)(2,1)S(1)} %get-tuple-element.51.image), custom_call_target="tpu_custom_call" | custom-call | flops 167772160 | bytes 2621440 | tf_op jit(solution)/shard_map/tails_next/pallas_call | solution.py:476
  72.8 4.7 %collective-permute-start.14 = (bf16[1024,128]{1,0:T(8,128)(2,1)S(1)}, bf16[1024,128]{1,0:T(8,128)(2,1)S(1)}, u32[]{:S(2)}, u32[]{:S(2)}) collective-permute-start(bf16[1024,128]{1,0:T(8,128)(2,1)S(1)} %get-tuple-element.55), channel_id=1, source_target_pairs={{0,31},{1,0},{2,1},{3,2},{4,3},{5,4},{6,5},{7,6},{8,7},{9,8},{10,9... | collective-permute-start | bytes 786440 | tf_op jit(solution)/shard_map/ppermute | solution.py:345
  77.5 1.3 %collective-permute-start.15 = (bf16[1024,128]{1,0:T(8,128)(2,1)S(1)}, bf16[1024,128]{1,0:T(8,128)(2,1)S(1)}, u32[]{:S(2)}, u32[]{:S(2)}) collective-permute-start(bf16[1024,128]{1,0:T(8,128)(2,1)S(1)} %get-tuple-element.56), channel_id=1, source_target_pairs={{32,0},{64,32},{96,64},{128,96},{160,128},{192,160},{224,192},{33,... | collective-permute-start | bytes 786440 | tf_op jit(solution)/shard_map/ppermute | solution.py:345
  78.8 3.0 %adjoint_next.1 = (f32[64,64,128]{2,1,0:T(8,128)S(1)}, f32[64,128]{1,0:T(8,128)S(1)}) custom-call(s32[8,384]{1,0:T(8,128)S(1)} %get-tuple-element.34.tab, bf16[321,128,128]{2,1,0:T(8,128)(2,1)S(1)} %get-tuple-element.35.matrix, bf16[65,64,128]{2,1,0:T(8,128)(2,1)S(1)} %get-tuple-element.51.image, f32[64,128]{1,0:T(8,128)S(1)} %get-tuple-element.33.weights), custom_call_target="tpu_custom_call" | custom-call | flops 335544320 | bytes 5242880 | tf_op jit(solution)/shard_map/adjoint_next/pallas_call | solution.py:486
  81.8 2.4 %collective-permute-done.14.high0 = bf16[1024,128]{1,0:T(8,128)(2,1)S(1)} collective-permute-done((bf16[1024,128]{1,0:T(8,128)(2,1)S(1)}, bf16[1024,128]{1,0:T(8,128)(2,1)S(1)}, u32[]{:S(2)}, u32[]{:S(2)}) %collective-permute-start.14) | collective-permute-done | bytes 262176 | tf_op jit(solution)/shard_map/ppermute | solution.py:345
  84.2 1.8 %collective-permute-done.15.high1 = bf16[1024,128]{1,0:T(8,128)(2,1)S(1)} collective-permute-done((bf16[1024,128]{1,0:T(8,128)(2,1)S(1)}, bf16[1024,128]{1,0:T(8,128)(2,1)S(1)}, u32[]{:S(2)}, u32[]{:S(2)}) %collective-permute-start.15) | collective-permute-done | bytes 262176 | tf_op jit(solution)/shard_map/ppermute | solution.py:345
  86.0 0.6 join_last.1
  86.6 29.8 %all_to_all.11 = f32[256,1,128]{2,1,0:T(1,128)S(1)} all-to-all(f32[256,1,128]{2,1,0:T(1,128)S(1)} %bitcast.14), channel_id=1, replica_groups=mesh['layer'=8,'tile'=32] {'layer','tile'}, dimensions={0} | all-to-all | bytes 262144 | tf_op jit(solution)/shard_map/all_to_all | solution.py:528
  116.4 1.3 %write_out.1 = bf16[64,8192]{1,0:T(8,128)(2,1)} custom-call(f32[256,128]{1,0:T(8,128)S(1)} %bitcast.13, f32[64,64,128]{2,1,0:T(8,128)S(1)} %get-tuple-element.60.total), custom_call_target="tpu_custom_call" | custom-call | bytes 3145728 | tf_op jit(solution)/shard_map/write_out/pallas_call | solution.py:529
  (16 shorter events, 0.4 us)
Async XLA Ops:
  1.1 18.4 %collective-permute-start.1 = (bf16[1040,128]{1,0:T(8,128)(2,1)S(1)}, bf16[1040,128]{1,0:T(8,128)(2,1)S(1)}, u32[]{:S(2)}, u32[]{:S(2)}) collective-permute-start(bf16[1040,128]{1,0:T(8,128)(2,1)S(1)} %get-tuple-element.37), channel_id=1, source_target_pairs={{32,0},{64,32},{96,64},{128,96},{160,128},{192,160},{224,192},{33,... | collective-permute-start | bytes 798728 | tf_op jit(solution)/shard_map/ppermute | solution.py:345
  2.4 17.1 %collective-permute-start = (bf16[1040,128]{1,0:T(8,128)(2,1)S(1)}, bf16[1040,128]{1,0:T(8,128)(2,1)S(1)}, u32[]{:S(2)}, u32[]{:S(2)}) collective-permute-start(bf16[1040,128]{1,0:T(8,128)(2,1)S(1)} %get-tuple-element.37), channel_id=1, source_target_pairs={{0,31},{1,0},{2,1},{3,2},{4,3},{5,4},{6,5},{7,6},{8,7},{9,8},{10,9... | collective-permute-start | bytes 798728 | tf_op jit(solution)/shard_map/ppermute | solution.py:345
  5.7 15.1 %collective-permute-start.3 = (bf16[1040,128]{1,0:T(8,128)(2,1)S(1)}, bf16[1040,128]{1,0:T(8,128)(2,1)S(1)}, u32[]{:S(2)}, u32[]{:S(2)}) collective-permute-start(bf16[1040,128]{1,0:T(8,128)(2,1)S(1)} %get-tuple-element.38), channel_id=1, source_target_pairs={{0,32},{32,64},{64,96},{96,128},{128,160},{160,192},{192,224},{1,3... | collective-permute-start | bytes 798728 | tf_op jit(solution)/shard_map/ppermute | solution.py:345
  10.0 10.9 %collective-permute-start.2 = (bf16[1040,128]{1,0:T(8,128)(2,1)S(1)}, bf16[1040,128]{1,0:T(8,128)(2,1)S(1)}, u32[]{:S(2)}, u32[]{:S(2)}) collective-permute-start(bf16[1040,128]{1,0:T(8,128)(2,1)S(1)} %get-tuple-element.38), channel_id=1, source_target_pairs={{0,1},{1,2},{2,3},{3,4},{4,5},{5,6},{6,7},{7,8},{8,9},{9,10},{10,1... | collective-permute-start | bytes 798728 | tf_op jit(solution)/shard_map/ppermute | solution.py:345
  23.0 15.0 %collective-permute-start.4 = (bf16[1024,128]{1,0:T(8,128)(2,1)S(1)}, bf16[1024,128]{1,0:T(8,128)(2,1)S(1)}, u32[]{:S(2)}, u32[]{:S(2)}) collective-permute-start(bf16[1024,128]{1,0:T(8,128)(2,1)S(1)} %get-tuple-element.41), channel_id=1, source_target_pairs={{0,1},{1,2},{2,3},{3,4},{4,5},{5,6},{6,7},{7,8},{8,9},{9,10},{10,1... | collective-permute-start | bytes 786440 | tf_op jit(solution)/shard_map/ppermute | solution.py:345
  23.3 14.8 %collective-permute-start.5 = (bf16[1024,128]{1,0:T(8,128)(2,1)S(1)}, bf16[1024,128]{1,0:T(8,128)(2,1)S(1)}, u32[]{:S(2)}, u32[]{:S(2)}) collective-permute-start(bf16[1024,128]{1,0:T(8,128)(2,1)S(1)} %get-tuple-element.42), channel_id=1, source_target_pairs={{0,32},{32,64},{64,96},{96,128},{128,160},{160,192},{192,224},{1,3... | collective-permute-start | bytes 786440 | tf_op jit(solution)/shard_map/ppermute | solution.py:345
  32.8 13.2 %collective-permute-start.6 = (bf16[1024,128]{1,0:T(8,128)(2,1)S(1)}, bf16[1024,128]{1,0:T(8,128)(2,1)S(1)}, u32[]{:S(2)}, u32[]{:S(2)}) collective-permute-start(bf16[1024,128]{1,0:T(8,128)(2,1)S(1)} %get-tuple-element.46), channel_id=1, source_target_pairs={{0,31},{1,0},{2,1},{3,2},{4,3},{5,4},{6,5},{7,6},{8,7},{9,8},{10,9... | collective-permute-start | bytes 786440 | tf_op jit(solution)/shard_map/ppermute | solution.py:345
  33.7 12.4 %collective-permute-start.7 = (bf16[1024,128]{1,0:T(8,128)(2,1)S(1)}, bf16[1024,128]{1,0:T(8,128)(2,1)S(1)}, u32[]{:S(2)}, u32[]{:S(2)}) collective-permute-start(bf16[1024,128]{1,0:T(8,128)(2,1)S(1)} %get-tuple-element.47), channel_id=1, source_target_pairs={{32,0},{64,32},{96,64},{128,96},{160,128},{192,160},{224,192},{33,... | collective-permute-start | bytes 786440 | tf_op jit(solution)/shard_map/ppermute | solution.py:345
  38.3 23.6 %collective-permute-start.9 = (bf16[1024,128]{1,0:T(8,128)(2,1)S(1)}, bf16[1024,128]{1,0:T(8,128)(2,1)S(1)}, u32[]{:S(2)}, u32[]{:S(2)}) collective-permute-start(bf16[1024,128]{1,0:T(8,128)(2,1)S(1)} %get-tuple-element.44.head), channel_id=1, source_target_pairs={{32,0},{64,32},{96,64},{128,96},{160,128},{192,160},{224,192},{33,... | collective-permute-start | bytes 786440 | tf_op jit(solution)/shard_map/ppermute | solution.py:345
  39.6 22.3 %collective-permute-start.8 = (bf16[1024,128]{1,0:T(8,128)(2,1)S(1)}, bf16[1024,128]{1,0:T(8,128)(2,1)S(1)}, u32[]{:S(2)}, u32[]{:S(2)}) collective-permute-start(bf16[1024,128]{1,0:T(8,128)(2,1)S(1)} %get-tuple-element.44.head), channel_id=1, source_target_pairs={{0,31},{1,0},{2,1},{3,2},{4,3},{5,4},{6,5},{7,6},{8,7},{9,8},{10,9... | collective-permute-start | bytes 786440 | tf_op jit(solution)/shard_map/ppermute | solution.py:345
  46.3 16.8 %collective-permute-start.11 = (bf16[1024,128]{1,0:T(8,128)(2,1)S(1)}, bf16[1024,128]{1,0:T(8,128)(2,1)S(1)}, u32[]{:S(2)}, u32[]{:S(2)}) collective-permute-start(bf16[1024,128]{1,0:T(8,128)(2,1)S(1)} %get-tuple-element.49.tail), channel_id=1, source_target_pairs={{0,32},{32,64},{64,96},{96,128},{128,160},{160,192},{192,224},{1,3... | collective-permute-start | bytes 786440 | tf_op jit(solution)/shard_map/ppermute | solution.py:345
  51.5 11.6 %collective-permute-start.10 = (bf16[1024,128]{1,0:T(8,128)(2,1)S(1)}, bf16[1024,128]{1,0:T(8,128)(2,1)S(1)}, u32[]{:S(2)}, u32[]{:S(2)}) collective-permute-start(bf16[1024,128]{1,0:T(8,128)(2,1)S(1)} %get-tuple-element.49.tail), channel_id=1, source_target_pairs={{0,1},{1,2},{2,3},{3,4},{4,5},{5,6},{6,7},{7,8},{8,9},{9,10},{10,1... | collective-permute-start | bytes 786440 | tf_op jit(solution)/shard_map/ppermute | solution.py:345
  65.2 16.6 %collective-permute-start.12 = (bf16[1024,128]{1,0:T(8,128)(2,1)S(1)}, bf16[1024,128]{1,0:T(8,128)(2,1)S(1)}, u32[]{:S(2)}, u32[]{:S(2)}) collective-permute-start(bf16[1024,128]{1,0:T(8,128)(2,1)S(1)} %get-tuple-element.53), channel_id=1, source_target_pairs={{0,1},{1,2},{2,3},{3,4},{4,5},{5,6},{6,7},{7,8},{8,9},{9,10},{10,1... | collective-permute-start | bytes 786440 | tf_op jit(solution)/shard_map/ppermute | solution.py:345
  68.0 13.8 %collective-permute-start.13 = (bf16[1024,128]{1,0:T(8,128)(2,1)S(1)}, bf16[1024,128]{1,0:T(8,128)(2,1)S(1)}, u32[]{:S(2)}, u32[]{:S(2)}) collective-permute-start(bf16[1024,128]{1,0:T(8,128)(2,1)S(1)} %get-tuple-element.54), channel_id=1, source_target_pairs={{0,32},{32,64},{64,96},{96,128},{128,160},{160,192},{192,224},{1,3... | collective-permute-start | bytes 786440 | tf_op jit(solution)/shard_map/ppermute | solution.py:345
  72.8 11.5 %collective-permute-start.14 = (bf16[1024,128]{1,0:T(8,128)(2,1)S(1)}, bf16[1024,128]{1,0:T(8,128)(2,1)S(1)}, u32[]{:S(2)}, u32[]{:S(2)}) collective-permute-start(bf16[1024,128]{1,0:T(8,128)(2,1)S(1)} %get-tuple-element.55), channel_id=1, source_target_pairs={{0,31},{1,0},{2,1},{3,2},{4,3},{5,4},{6,5},{7,6},{8,7},{9,8},{10,9... | collective-permute-start | bytes 786440 | tf_op jit(solution)/shard_map/ppermute | solution.py:345
  77.5 8.5 %collective-permute-start.15 = (bf16[1024,128]{1,0:T(8,128)(2,1)S(1)}, bf16[1024,128]{1,0:T(8,128)(2,1)S(1)}, u32[]{:S(2)}, u32[]{:S(2)}) collective-permute-start(bf16[1024,128]{1,0:T(8,128)(2,1)S(1)} %get-tuple-element.56), channel_id=1, source_target_pairs={{32,0},{64,32},{96,64},{128,96},{160,128},{192,160},{224,192},{33,... | collective-permute-start | bytes 786440 | tf_op jit(solution)/shard_map/ppermute | solution.py:345

commit v3 on v2

--- a/solution.py
+++ b/solution.py
@@ -17,7 +17,7 @@
 FORWARD_OWN, FORWARD_HEADS, FORWARD_TAILS, ADJOINT_OWN, ADJOINT_HEADS, ADJOINT_TAILS, FLIPS, TRIPS = range(8)
 
 
-def fill_tables(live_count, row, col, turned, num_blocks, tab):
+def fill_tables(live_count, above, beneath, row, col, turned, num_blocks, tab):
     f32, bf16 = jnp.float32, jnp.bfloat16
     slots = row.shape[1]
     places = tab.shape[1]
@@ -26,6 +26,7 @@
     edge = num_blocks // 4
     outer = col - num_blocks
     side = outer // edge
+    live = live & ((side != 2) | (above == 1)) & ((side != 3) | (beneath == 1))
     own = outer < 0
     heads = (outer >= 0) & ((side & 1) == 1)
     tails = (outer >= 0) & ((side & 1) == 0)
@@ -150,7 +151,7 @@
     source[num_blocks] = jnp.zeros(source.shape[1:], source.dtype)
     for copy in small:
         copy.wait()
-    fill_tables(count[0], lists[0], lists[1], lists[2], num_blocks, tab)
+    fill_tables(count[0], count[1], count[2], lists[0], lists[1], lists[2], num_blocks, tab)
     table_copy = pltpu.make_async_copy(tab, smem, sems.at[CHUNKS + 4])
     table_copy.start()
     copies[3].wait()
@@ -339,18 +340,17 @@
     lax.fori_loop(0, num_blocks, body, 0, unroll=4)
 
 
-def shift(x, axis, step, periodic):
+def shift(x, axis, step):
     count = lax.axis_size(axis)
-    route = [(i, (i + step) % count) for i in range(count) if periodic or 0 <= i + step < count]
-    return lax.ppermute(x, axis, route)
+    return lax.ppermute(x, axis, [(i, (i + step) % count) for i in range(count)])
 
 
 def heads_out(head):
-    return shift(head, "tile", -1, True), shift(head, "layer", -1, False)
+    return shift(head, "tile", -1), shift(head, "layer", -1)
 
 
 def tails_out(tail):
-    return shift(tail, "tile", 1, True), shift(tail, "layer", 1, False)
+    return shift(tail, "tile", 1), shift(tail, "layer", 1)
 
 
 def call(kernel, name, outs, in_specs, scratch, flops, nbytes, aliases={}):
@@ -405,6 +405,9 @@
     )(start, outside(density[0]))
     heads, tails = heads_out(head), tails_out(tail)
 
+    layer = lax.axis_index("layer")
+    above, beneath = layer > 0, layer < lax.axis_size("layer") - 1
+    facts = jnp.stack([live_block_count[0, 0], above.astype(jnp.int32), beneath.astype(jnp.int32)])
     places = 2 * ((slots + num_blocks) // 2)
     matrix, rows, tab = call(
         first_kernel,
@@ -421,7 +424,7 @@
         2 * work,
         2 * blocks.size * 2,
     )(
-        live_block_count[0],
+        facts,
         outside(blocks),
         start,
         outside(slot_rows[0]),
@@ -472,7 +475,7 @@
         if first:
             inverse = result[2]
         right, lower = result[-2:]
-        lows = (shift(right, "tile", 1, True), shift(lower, "layer", 1, False))
+        lows = (shift(right, "tile", 1), shift(lower, "layer", 1))
         left, upper = call(
             tails_kernel,
             "tails" + suffix,
@@ -482,7 +485,7 @@
             work // 2,
             blocks.size // 2,
         )(tab, matrix, image)
-        highs = (shift(left, "tile", -1, True), shift(upper, "layer", -1, False))
+        highs = (shift(left, "tile", -1), shift(upper, "layer", -1))
         result = call(
             adjoint_kernel,
             "adjoint" + suffix,

time: 118 us -> 114 us (0.966)
  starting transfers between devices: 52.6 us -> 24.8 us
  waiting for transfers between devices: 4.19 us -> 26 us
  Pallas kernels: 30.3 us -> 36.8 us
  blocking collectives: 29.8 us -> 24.5 us
    ppermute x16, starting transfers between devices: 52.6 us -> 24.8 us  [shift(): lax.ppermute(x, axis, [(i, (i + step) % count) for i in range(count)])]
    ppermute x16, waiting for transfers between devices: 4.19 us -> 26 us  [shift(): lax.ppermute(x, axis, [(i, (i + step) % count) for i in range(count)])]
    all_to_all x1, blocking collectives: 29.8 us -> 24.5 us  [local(): sums = lax.all_to_all(message, ('layer', 'tile'), 0, 0, tiled=True)]
    pallas_call x1, Pallas kernels: 7.6 us -> 9.97 us  [local(): call(first_kernel, 'own_first', [VM((slots + 1, size, size), bf16), tall_...]
    pallas_call x2, Pallas kernels: 4.22 us -> 5.85 us  [local(): call(functools.partial(middle_kernel, first), 'middle' + suffix, [rows_ty...]
  transfers between devices with their start and end apart: 16 -> 16, of which waited for: 2 -> 7; matrix products, arithmetic and copies ran while one was open for 0% -> 0% of each run, Pallas kernels for 20% -> 25%
where the time goes in v3:
time: 114 us; the launch traced here: 113 us
  Pallas kernels  36.8 us (32%)
  waiting for transfers between devices  26 us (23%)
  starting transfers between devices  24.8 us (22%)
  blocking collectives  24.5 us (21%)
    ppermute x16, waiting for transfers between devices, shift(): lax.ppermute(x, axis, [(i, (i + step) % count) for i in range(count)])  26 us
    ppermute x16, starting transfers between devices, shift(): lax.ppermute(x, axis, [(i, (i + step) % count) for i in range(count)])  24.8 us
    all_to_all x1, blocking collectives, local(): sums = lax.all_to_all(message, ('layer', 'tile'), 0, 0, tiled=True)  24.5 us
    pallas_call x1, Pallas kernels, local(): call(first_kernel, 'own_first', [VM((slots + 1, size, size), bf16), tall_...  9.97 us
    pallas_call x2, Pallas kernels, local(): call(adjoint_kernel, 'adjoint' + suffix, [block_f32, norm_type] + ([middl...  6.71 us
    pallas_call x2, Pallas kernels, local(): call(functools.partial(middle_kernel, first), 'middle' + suffix, [rows_ty...  5.85 us
    pallas_call x1, Pallas kernels, local(): call(own_kernel, 'own_next', [block_f32], [SMEM_SPEC] + [VMEM_SPEC] * 4,...  4.11 us
    pallas_call x2, Pallas kernels, local(): call(functools.partial(heads_kernel, first), 'heads' + suffix, [rows_type...  3.51 us
  transfers between devices with their start and end apart: 16, of which 7 were waited for; matrix products, arithmetic and copies ran while one was open for 0% of the time, Pallas kernels for 25%

profile of v3, /device:TPU:1, one launch (start us, length us, event | category | flops | bytes accessed | tf_op | source)
XLA Modules:
  0.0 113.0 jit_solution(456362306641775617)
XLA Ops:
  0.0 1.1 edges.1
  1.1 4.6 %collective-permute-start.1 = (bf16[1040,128]{1,0:T(8,128)(2,1)S(1)}, bf16[1040,128]{1,0:T(8,128)(2,1)S(1)}, u32[]{:S(2)}, u32[]{:S(2)}) collective-permute-start(bf16[1040,128]{1,0:T(8,128)(2,1)S(1)} %get-tuple-element.37), channel_id=1, source_target_pairs={{0,224},{32,0},{64,32},{96,64},{128,96},{160,128},{192,160},{224,1... | collective-permute-start | bytes 798728 | tf_op jit(solution)/shard_map/ppermute | solution.py:345
  5.7 1.0 collective-permute-start
  6.6 2.3 %collective-permute-start.2 = (bf16[1040,128]{1,0:T(8,128)(2,1)S(1)}, bf16[1040,128]{1,0:T(8,128)(2,1)S(1)}, u32[]{:S(2)}, u32[]{:S(2)}) collective-permute-start(bf16[1040,128]{1,0:T(8,128)(2,1)S(1)} %get-tuple-element.38), channel_id=1, source_target_pairs={{0,1},{1,2},{2,3},{3,4},{4,5},{5,6},{6,7},{7,8},{8,9},{9,10},{10,1... | collective-permute-start | bytes 798728 | tf_op jit(solution)/shard_map/ppermute | solution.py:345
  9.7 10.0 %own_first.1 = (bf16[321,128,128]{2,1,0:T(8,128)(2,1)S(1)}, f32[64,80,128]{2,1,0:T(8,128)S(1)}, s32[8,384]{1,0:T(8,128)S(1)}) custom-call(s32[3]{0:T(128)S(1)} %pad_add_fusion.count, bf16[320,128,128]{2,1,0:T(8,128)(2,1)} %bitcast.17, bf16[64,8192]{1,0:T(8,128)(2,1)} %bitcast.19, s32[1,320]{1,0:T(1,128)} %bitcast.21, s32[1,320]{1,0:T(1,128)} %bitcast.22, ...), custom_call_target="tpu_custom_call" | custom-call | flops 671088640 | bytes 20971520 | tf_op jit(solution)/shard_map/own_first/pallas_call | solution.py:412
  19.7 3.9 %collective-permute-done.right = bf16[1040,128]{1,0:T(8,128)(2,1)S(1)} collective-permute-done((bf16[1040,128]{1,0:T(8,128)(2,1)S(1)}, bf16[1040,128]{1,0:T(8,128)(2,1)S(1)}, u32[]{:S(2)}, u32[]{:S(2)}) %collective-permute-start) | collective-permute-done | bytes 266272 | tf_op jit(solution)/shard_map/ppermute | solution.py:345
  23.6 1.8 %heads_first.1.rows_in = f32[64,80,128]{2,1,0:T(8,128)S(1)} custom-call(s32[8,384]{1,0:T(8,128)S(1)} %get-tuple-element.34.tab, bf16[321,128,128]{2,1,0:T(8,128)(2,1)S(1)} %get-tuple-element.35.matrix, f32[64,80,128]{2,1,0:T(8,128)S(1)} %get-tuple-element.36.rows_in, ...), custom_call_target="tpu_custom_call", output_to_operand_aliasing={{}: (2, {})} | custom-call | flops 167772160 | bytes 2621440 | tf_op jit(solution)/shard_map/heads_first/pallas_call | solution.py:453
  25.4 3.0 %middle_first.1 = (f32[64,80,128]{2,1,0:T(8,128)S(1)}, bf16[65,64,128]{2,1,0:T(8,128)(2,1)S(1)}, f32[64,8,128]{2,1,0:T(8,128)S(1)}, bf16[1024,128]{1,0:T(8,128)(2,1)S(1)}, bf16[1024,128]{1,0:T(8,128)(2,1)S(1)}) custom-call(s32[8,384]{1,0:T(8,128)S(1)} %get-tuple-element.34.tab, ...), custom_call_target="tpu_custom_call", output_to_operand_aliasing={{0}: (2, {})} | custom-call | flops 335544320 | bytes 5242880 | tf_op jit(solution)/shard_map/middle_first/pallas_call | solution.py:464
  28.4 1.4 %collective-permute-start.4 = (bf16[1024,128]{1,0:T(8,128)(2,1)S(1)}, bf16[1024,128]{1,0:T(8,128)(2,1)S(1)}, u32[]{:S(2)}, u32[]{:S(2)}) collective-permute-start(bf16[1024,128]{1,0:T(8,128)(2,1)S(1)} %get-tuple-element.41), channel_id=1, source_target_pairs={{0,1},{1,2},{2,3},{3,4},{4,5},{5,6},{6,7},{7,8},{8,9},{9,10},{10,1... | collective-permute-start | bytes 786440 | tf_op jit(solution)/shard_map/ppermute | solution.py:345
  29.9 1.6 %tails_first.1 = (bf16[1024,128]{1,0:T(8,128)(2,1)S(1)}, bf16[1024,128]{1,0:T(8,128)(2,1)S(1)}) custom-call(s32[8,384]{1,0:T(8,128)S(1)} %get-tuple-element.34.tab, bf16[321,128,128]{2,1,0:T(8,128)(2,1)S(1)} %get-tuple-element.35.matrix, bf16[65,64,128]{2,1,0:T(8,128)(2,1)S(1)} %get-tuple-element.39.image), custom_call_target="tpu_custom_call" | custom-call | flops 167772160 | bytes 2621440 | tf_op jit(solution)/shard_map/tails_first/pallas_call | solution.py:479
  31.6 3.6 %collective-permute-start.7 = (bf16[1024,128]{1,0:T(8,128)(2,1)S(1)}, bf16[1024,128]{1,0:T(8,128)(2,1)S(1)}, u32[]{:S(2)}, u32[]{:S(2)}) collective-permute-start(bf16[1024,128]{1,0:T(8,128)(2,1)S(1)} %get-tuple-element.47), channel_id=1, source_target_pairs={{0,224},{32,0},{64,32},{96,64},{128,96},{160,128},{192,160},{224,1... | collective-permute-start | bytes 786440 | tf_op jit(solution)/shard_map/ppermute | solution.py:345
  35.2 3.4 %adjoint_first.1 = (f32[64,64,128]{2,1,0:T(8,128)S(1)}, f32[64,128]{1,0:T(8,128)S(1)}, bf16[32,64,128]{2,1,0:T(8,128)(2,1)S(1)}) custom-call(s32[8,384]{1,0:T(8,128)S(1)} %get-tuple-element.34.tab, bf16[321,128,128]{2,1,0:T(8,128)(2,1)S(1)} %get-tuple-element.35.matrix, bf16[65,64,128]{2,1,0:T(8,128)(2,1)S(1)} %get-tuple-element.39.image, ...), custom_call_target="tpu_custom_call" | custom-call | flops 335544320 | bytes 5242880 | tf_op jit(solution)/shard_map/adjoint_first/pallas_call | solution.py:489
  38.6 4.2 %collective-permute-done.5.two = bf16[1024,128]{1,0:T(8,128)(2,1)S(1)} collective-permute-done((bf16[1024,128]{1,0:T(8,128)(2,1)S(1)}, bf16[1024,128]{1,0:T(8,128)(2,1)S(1)}, u32[]{:S(2)}, u32[]{:S(2)}) %collective-permute-start.5) | collective-permute-done | bytes 262176 | tf_op jit(solution)/shard_map/ppermute | solution.py:345
  42.8 0.2 join_head.1
  43.0 2.1 %collective-permute-start.9 = (bf16[1024,128]{1,0:T(8,128)(2,1)S(1)}, bf16[1024,128]{1,0:T(8,128)(2,1)S(1)}, u32[]{:S(2)}, u32[]{:S(2)}) collective-permute-start(bf16[1024,128]{1,0:T(8,128)(2,1)S(1)} %get-tuple-element.44.head), channel_id=1, source_target_pairs={{0,224},{32,0},{64,32},{96,64},{128,96},{160,128},{192,160},{224,1... | collective-permute-start | bytes 786440 | tf_op jit(solution)/shard_map/ppermute | solution.py:345
  45.0 1.4 %collective-permute-start.8 = (bf16[1024,128]{1,0:T(8,128)(2,1)S(1)}, bf16[1024,128]{1,0:T(8,128)(2,1)S(1)}, u32[]{:S(2)}, u32[]{:S(2)}) collective-permute-start(bf16[1024,128]{1,0:T(8,128)(2,1)S(1)} %get-tuple-element.44.head), channel_id=1, source_target_pairs={{0,31},{1,0},{2,1},{3,2},{4,3},{5,4},{6,5},{7,6},{8,7},{9,8},{10,9... | collective-permute-start | bytes 786440 | tf_op jit(solution)/shard_map/ppermute | solution.py:345
  46.5 6.1 %collective-permute-done.7.two = bf16[1024,128]{1,0:T(8,128)(2,1)S(1)} collective-permute-done((bf16[1024,128]{1,0:T(8,128)(2,1)S(1)}, bf16[1024,128]{1,0:T(8,128)(2,1)S(1)}, u32[]{:S(2)}, u32[]{:S(2)}) %collective-permute-start.7) | collective-permute-done | bytes 262176 | tf_op jit(solution)/shard_map/ppermute | solution.py:345
  52.8 1.0 collective-permute-start.11
  53.8 4.1 %own_next.1.rows_in = f32[64,64,128]{2,1,0:T(8,128)S(1)} custom-call(s32[8,384]{1,0:T(8,128)S(1)} %get-tuple-element.34.tab, bf16[321,128,128]{2,1,0:T(8,128)(2,1)S(1)} %get-tuple-element.35.matrix, bf16[1024,128]{1,0:T(8,128)(2,1)S(1)} %get-tuple-element.44.head, bf16[32,64,128]{2,1,0:T(8,128)(2,1)S(1)} %get-tuple-element.45.middle, ...), custom_call_target="tpu_custom_call" | custom-call | flops 335544320 | bytes 5242880 | tf_op jit(solution)/shard_map/own_next/pallas_call | solution.py:444
  57.9 0.3 collective-permute-done.9.lower
  58.2 4.8 %collective-permute-done.8.right = bf16[1024,128]{1,0:T(8,128)(2,1)S(1)} collective-permute-done((bf16[1024,128]{1,0:T(8,128)(2,1)S(1)}, bf16[1024,128]{1,0:T(8,128)(2,1)S(1)}, u32[]{:S(2)}, u32[]{:S(2)}) %collective-permute-start.8) | collective-permute-done | bytes 262176 | tf_op jit(solution)/shard_map/ppermute | solution.py:345
  63.0 1.8 %heads_next.1.rows_in = f32[64,64,128]{2,1,0:T(8,128)S(1)} custom-call(s32[8,384]{1,0:T(8,128)S(1)} %get-tuple-element.34.tab, bf16[321,128,128]{2,1,0:T(8,128)(2,1)S(1)} %get-tuple-element.35.matrix, f32[64,64,128]{2,1,0:T(8,128)S(1)} %own_next.1.rows_in, bf16[1024,128]{1,0:T(8,128)(2,1)S(1)} %collective-permute-done.8.right, ...), custom_call_target="tpu_custom_call", output_to_operand_aliasing={{}: (2, {})} | custom-call | flops 167772160 | bytes 2621440 | tf_op jit(solution)/shard_map/heads_next/pallas_call | solution.py:453
  64.8 2.9 %middle_next.1 = (f32[64,64,128]{2,1,0:T(8,128)S(1)}, bf16[65,64,128]{2,1,0:T(8,128)(2,1)S(1)}, bf16[1024,128]{1,0:T(8,128)(2,1)S(1)}, bf16[1024,128]{1,0:T(8,128)(2,1)S(1)}) custom-call(s32[8,384]{1,0:T(8,128)S(1)} %get-tuple-element.34.tab, bf16[321,128,128]{2,1,0:T(8,128)(2,1)S(1)} %get-tuple-element.35.matrix, ...), custom_call_target="tpu_custom_call", output_to_operand_aliasing={{0}: (2, {})} | custom-call | flops 335544320 | bytes 5242880 | tf_op jit(solution)/shard_map/middle_next/pallas_call | solution.py:464
  67.6 3.5 %collective-permute-start.12 = (bf16[1024,128]{1,0:T(8,128)(2,1)S(1)}, bf16[1024,128]{1,0:T(8,128)(2,1)S(1)}, u32[]{:S(2)}, u32[]{:S(2)}) collective-permute-start(bf16[1024,128]{1,0:T(8,128)(2,1)S(1)} %get-tuple-element.53), channel_id=1, source_target_pairs={{0,1},{1,2},{2,3},{3,4},{4,5},{5,6},{6,7},{7,8},{8,9},{9,10},{10,1... | collective-permute-start | bytes 786440 | tf_op jit(solution)/shard_map/ppermute | solution.py:345
  71.2 1.6 %tails_next.1 = (bf16[1024,128]{1,0:T(8,128)(2,1)S(1)}, bf16[1024,128]{1,0:T(8,128)(2,1)S(1)}) custom-call(s32[8,384]{1,0:T(8,128)S(1)} %get-tuple-element.34.tab, bf16[321,128,128]{2,1,0:T(8,128)(2,1)S(1)} %get-tuple-element.35.matrix, bf16[65,64,128]{2,1,0:T(8,128)(2,1)S(1)} %get-tuple-element.51.image), custom_call_target="tpu_custom_call" | custom-call | flops 167772160 | bytes 2621440 | tf_op jit(solution)/shard_map/tails_next/pallas_call | solution.py:479
  72.9 3.6 %collective-permute-start.15 = (bf16[1024,128]{1,0:T(8,128)(2,1)S(1)}, bf16[1024,128]{1,0:T(8,128)(2,1)S(1)}, u32[]{:S(2)}, u32[]{:S(2)}) collective-permute-start(bf16[1024,128]{1,0:T(8,128)(2,1)S(1)} %get-tuple-element.56), channel_id=1, source_target_pairs={{0,224},{32,0},{64,32},{96,64},{128,96},{160,128},{192,160},{224,1... | collective-permute-start | bytes 786440 | tf_op jit(solution)/shard_map/ppermute | solution.py:345
  76.5 3.3 %adjoint_next.1 = (f32[64,64,128]{2,1,0:T(8,128)S(1)}, f32[64,128]{1,0:T(8,128)S(1)}) custom-call(s32[8,384]{1,0:T(8,128)S(1)} %get-tuple-element.34.tab, bf16[321,128,128]{2,1,0:T(8,128)(2,1)S(1)} %get-tuple-element.35.matrix, bf16[65,64,128]{2,1,0:T(8,128)(2,1)S(1)} %get-tuple-element.51.image, f32[64,128]{1,0:T(8,128)S(1)} %get-tuple-element.33.weights), custom_call_target="tpu_custom_call" | custom-call | flops 335544320 | bytes 5242880 | tf_op jit(solution)/shard_map/adjoint_next/pallas_call | solution.py:489
  79.9 4.7 %collective-permute-done.13.low1 = bf16[1024,128]{1,0:T(8,128)(2,1)S(1)} collective-permute-done((bf16[1024,128]{1,0:T(8,128)(2,1)S(1)}, bf16[1024,128]{1,0:T(8,128)(2,1)S(1)}, u32[]{:S(2)}, u32[]{:S(2)}) %collective-permute-start.13) | collective-permute-done | bytes 262176 | tf_op jit(solution)/shard_map/ppermute | solution.py:345
  84.6 1.9 %collective-permute-done.15.high1 = bf16[1024,128]{1,0:T(8,128)(2,1)S(1)} collective-permute-done((bf16[1024,128]{1,0:T(8,128)(2,1)S(1)}, bf16[1024,128]{1,0:T(8,128)(2,1)S(1)}, u32[]{:S(2)}, u32[]{:S(2)}) %collective-permute-start.15) | collective-permute-done | bytes 262176 | tf_op jit(solution)/shard_map/ppermute | solution.py:345
  86.5 0.6 join_last.1
  87.1 24.5 %all_to_all.11 = f32[256,1,128]{2,1,0:T(1,128)S(1)} all-to-all(f32[256,1,128]{2,1,0:T(1,128)S(1)} %bitcast.16), channel_id=1, replica_groups=mesh['layer'=8,'tile'=32] {'layer','tile'}, dimensions={0} | all-to-all | bytes 262144 | tf_op jit(solution)/shard_map/all_to_all | solution.py:531
  111.7 1.3 %write_out.1 = bf16[64,8192]{1,0:T(8,128)(2,1)} custom-call(f32[256,128]{1,0:T(8,128)S(1)} %bitcast.15, f32[64,64,128]{2,1,0:T(8,128)S(1)} %get-tuple-element.60.total), custom_call_target="tpu_custom_call" | custom-call | bytes 3145728 | tf_op jit(solution)/shard_map/write_out/pallas_call | solution.py:532
  (17 shorter events, 0.5 us)
Async XLA Ops:
  1.1 18.6 %collective-permute-start.1 = (bf16[1040,128]{1,0:T(8,128)(2,1)S(1)}, bf16[1040,128]{1,0:T(8,128)(2,1)S(1)}, u32[]{:S(2)}, u32[]{:S(2)}) collective-permute-start(bf16[1040,128]{1,0:T(8,128)(2,1)S(1)} %get-tuple-element.37), channel_id=1, source_target_pairs={{0,224},{32,0},{64,32},{96,64},{128,96},{160,128},{192,160},{224,1... | collective-permute-start | bytes 798728 | tf_op jit(solution)/shard_map/ppermute | solution.py:345
  5.7 18.0 %collective-permute-start = (bf16[1040,128]{1,0:T(8,128)(2,1)S(1)}, bf16[1040,128]{1,0:T(8,128)(2,1)S(1)}, u32[]{:S(2)}, u32[]{:S(2)}) collective-permute-start(bf16[1040,128]{1,0:T(8,128)(2,1)S(1)} %get-tuple-element.37), channel_id=1, source_target_pairs={{0,31},{1,0},{2,1},{3,2},{4,3},{5,4},{6,5},{7,6},{8,7},{9,8},{10,9... | collective-permute-start | bytes 798728 | tf_op jit(solution)/shard_map/ppermute | solution.py:345
  6.6 18.8 %collective-permute-start.3 = (bf16[1040,128]{1,0:T(8,128)(2,1)S(1)}, bf16[1040,128]{1,0:T(8,128)(2,1)S(1)}, u32[]{:S(2)}, u32[]{:S(2)}) collective-permute-start(bf16[1040,128]{1,0:T(8,128)(2,1)S(1)} %get-tuple-element.38), channel_id=1, source_target_pairs={{0,32},{32,64},{64,96},{96,128},{128,160},{160,192},{192,224},{224... | collective-permute-start | bytes 798728 | tf_op jit(solution)/shard_map/ppermute | solution.py:345
  6.6 18.8 %collective-permute-start.2 = (bf16[1040,128]{1,0:T(8,128)(2,1)S(1)}, bf16[1040,128]{1,0:T(8,128)(2,1)S(1)}, u32[]{:S(2)}, u32[]{:S(2)}) collective-permute-start(bf16[1040,128]{1,0:T(8,128)(2,1)S(1)} %get-tuple-element.38), channel_id=1, source_target_pairs={{0,1},{1,2},{2,3},{3,4},{4,5},{5,6},{6,7},{7,8},{8,9},{9,10},{10,1... | collective-permute-start | bytes 798728 | tf_op jit(solution)/shard_map/ppermute | solution.py:345
  28.4 10.2 %collective-permute-start.4 = (bf16[1024,128]{1,0:T(8,128)(2,1)S(1)}, bf16[1024,128]{1,0:T(8,128)(2,1)S(1)}, u32[]{:S(2)}, u32[]{:S(2)}) collective-permute-start(bf16[1024,128]{1,0:T(8,128)(2,1)S(1)} %get-tuple-element.41), channel_id=1, source_target_pairs={{0,1},{1,2},{2,3},{3,4},{4,5},{5,6},{6,7},{7,8},{8,9},{9,10},{10,1... | collective-permute-start | bytes 786440 | tf_op jit(solution)/shard_map/ppermute | solution.py:345
  29.8 13.0 %collective-permute-start.5 = (bf16[1024,128]{1,0:T(8,128)(2,1)S(1)}, bf16[1024,128]{1,0:T(8,128)(2,1)S(1)}, u32[]{:S(2)}, u32[]{:S(2)}) collective-permute-start(bf16[1024,128]{1,0:T(8,128)(2,1)S(1)} %get-tuple-element.42), channel_id=1, source_target_pairs={{0,32},{32,64},{64,96},{96,128},{128,160},{160,192},{192,224},{224... | collective-permute-start | bytes 786440 | tf_op jit(solution)/shard_map/ppermute | solution.py:345
  31.5 15.0 %collective-permute-start.6 = (bf16[1024,128]{1,0:T(8,128)(2,1)S(1)}, bf16[1024,128]{1,0:T(8,128)(2,1)S(1)}, u32[]{:S(2)}, u32[]{:S(2)}) collective-permute-start(bf16[1024,128]{1,0:T(8,128)(2,1)S(1)} %get-tuple-element.46), channel_id=1, source_target_pairs={{0,31},{1,0},{2,1},{3,2},{4,3},{5,4},{6,5},{7,6},{8,7},{9,8},{10,9... | collective-permute-start | bytes 786440 | tf_op jit(solution)/shard_map/ppermute | solution.py:345
  31.6 21.0 %collective-permute-start.7 = (bf16[1024,128]{1,0:T(8,128)(2,1)S(1)}, bf16[1024,128]{1,0:T(8,128)(2,1)S(1)}, u32[]{:S(2)}, u32[]{:S(2)}) collective-permute-start(bf16[1024,128]{1,0:T(8,128)(2,1)S(1)} %get-tuple-element.47), channel_id=1, source_target_pairs={{0,224},{32,0},{64,32},{96,64},{128,96},{160,128},{192,160},{224,1... | collective-permute-start | bytes 786440 | tf_op jit(solution)/shard_map/ppermute | solution.py:345
  43.0 15.2 %collective-permute-start.9 = (bf16[1024,128]{1,0:T(8,128)(2,1)S(1)}, bf16[1024,128]{1,0:T(8,128)(2,1)S(1)}, u32[]{:S(2)}, u32[]{:S(2)}) collective-permute-start(bf16[1024,128]{1,0:T(8,128)(2,1)S(1)} %get-tuple-element.44.head), channel_id=1, source_target_pairs={{0,224},{32,0},{64,32},{96,64},{128,96},{160,128},{192,160},{224,1... | collective-permute-start | bytes 786440 | tf_op jit(solution)/shard_map/ppermute | solution.py:345
  45.0 18.0 %collective-permute-start.8 = (bf16[1024,128]{1,0:T(8,128)(2,1)S(1)}, bf16[1024,128]{1,0:T(8,128)(2,1)S(1)}, u32[]{:S(2)}, u32[]{:S(2)}) collective-permute-start(bf16[1024,128]{1,0:T(8,128)(2,1)S(1)} %get-tuple-element.44.head), channel_id=1, source_target_pairs={{0,31},{1,0},{2,1},{3,2},{4,3},{5,4},{6,5},{7,6},{8,7},{9,8},{10,9... | collective-permute-start | bytes 786440 | tf_op jit(solution)/shard_map/ppermute | solution.py:345
  52.8 12.0 %collective-permute-start.11 = (bf16[1024,128]{1,0:T(8,128)(2,1)S(1)}, bf16[1024,128]{1,0:T(8,128)(2,1)S(1)}, u32[]{:S(2)}, u32[]{:S(2)}) collective-permute-start(bf16[1024,128]{1,0:T(8,128)(2,1)S(1)} %get-tuple-element.49.tail), channel_id=1, source_target_pairs={{0,32},{32,64},{64,96},{96,128},{128,160},{160,192},{192,224},{224... | collective-permute-start | bytes 786440 | tf_op jit(solution)/shard_map/ppermute | solution.py:345
  53.8 11.0 %collective-permute-start.10 = (bf16[1024,128]{1,0:T(8,128)(2,1)S(1)}, bf16[1024,128]{1,0:T(8,128)(2,1)S(1)}, u32[]{:S(2)}, u32[]{:S(2)}) collective-permute-start(bf16[1024,128]{1,0:T(8,128)(2,1)S(1)} %get-tuple-element.49.tail), channel_id=1, source_target_pairs={{0,1},{1,2},{2,3},{3,4},{4,5},{5,6},{6,7},{7,8},{8,9},{9,10},{10,1... | collective-permute-start | bytes 786440 | tf_op jit(solution)/shard_map/ppermute | solution.py:345
  67.6 12.3 %collective-permute-start.12 = (bf16[1024,128]{1,0:T(8,128)(2,1)S(1)}, bf16[1024,128]{1,0:T(8,128)(2,1)S(1)}, u32[]{:S(2)}, u32[]{:S(2)}) collective-permute-start(bf16[1024,128]{1,0:T(8,128)(2,1)S(1)} %get-tuple-element.53), channel_id=1, source_target_pairs={{0,1},{1,2},{2,3},{3,4},{4,5},{5,6},{6,7},{7,8},{8,9},{9,10},{10,1... | collective-permute-start | bytes 786440 | tf_op jit(solution)/shard_map/ppermute | solution.py:345
  71.2 13.4 %collective-permute-start.13 = (bf16[1024,128]{1,0:T(8,128)(2,1)S(1)}, bf16[1024,128]{1,0:T(8,128)(2,1)S(1)}, u32[]{:S(2)}, u32[]{:S(2)}) collective-permute-start(bf16[1024,128]{1,0:T(8,128)(2,1)S(1)} %get-tuple-element.54), channel_id=1, source_target_pairs={{0,32},{32,64},{64,96},{96,128},{128,160},{160,192},{192,224},{224... | collective-permute-start | bytes 786440 | tf_op jit(solution)/shard_map/ppermute | solution.py:345
  72.8 11.8 %collective-permute-start.14 = (bf16[1024,128]{1,0:T(8,128)(2,1)S(1)}, bf16[1024,128]{1,0:T(8,128)(2,1)S(1)}, u32[]{:S(2)}, u32[]{:S(2)}) collective-permute-start(bf16[1024,128]{1,0:T(8,128)(2,1)S(1)} %get-tuple-element.55), channel_id=1, source_target_pairs={{0,31},{1,0},{2,1},{3,2},{4,3},{5,4},{6,5},{7,6},{8,7},{9,8},{10,9... | collective-permute-start | bytes 786440 | tf_op jit(solution)/shard_map/ppermute | solution.py:345
  72.9 13.6 %collective-permute-start.15 = (bf16[1024,128]{1,0:T(8,128)(2,1)S(1)}, bf16[1024,128]{1,0:T(8,128)(2,1)S(1)}, u32[]{:S(2)}, u32[]{:S(2)}) collective-permute-start(bf16[1024,128]{1,0:T(8,128)(2,1)S(1)} %get-tuple-element.56), channel_id=1, source_target_pairs={{0,224},{32,0},{64,32},{96,64},{128,96},{160,128},{192,160},{224,1... | collective-permute-start | bytes 786440 | tf_op jit(solution)/shard_map/ppermute | solution.py:345

commit v4 on v3

--- a/solution.py
+++ b/solution.py
@@ -8,7 +8,8 @@
 from jax.sharding import PartitionSpec as P
 
 UNROLL = 16
-TURN = 8
+HALF = UNROLL // 2
+TURN = 16
 CHUNKS = 8
 VM = pltpu.VMEM
 VMEM_SPEC = pl.BlockSpec(memory_space=pltpu.VMEM)
@@ -32,7 +33,7 @@
     tails = (outer >= 0) & ((side & 1) == 0)
     source = jnp.where(own, col, (side >> 1) * edge + outer - side * edge)
     key = lax.broadcasted_iota(jnp.int32, (num_blocks, slots), 0)
-    place = lax.broadcasted_iota(jnp.int32, (places, slots), 0)
+    spot = lax.broadcasted_iota(jnp.int32, (128, slots), 0)
     earlier = (
         lax.broadcasted_iota(jnp.int32, (slots, slots), 0) < lax.broadcasted_iota(jnp.int32, (slots, slots), 1)
     ).astype(f32).astype(bf16)
@@ -44,38 +45,45 @@
     meta = jnp.zeros((1, places), jnp.int32)
 
     def invert(position, parts):
-        found = (place == position).astype(f32).astype(bf16)
-        parts = parts + [jnp.zeros((1, slots), jnp.int32)] * (8 - len(parts))
-        values = jnp.concatenate([p.astype(f32) for p in parts], axis=0).astype(bf16)
+        found = (spot == (position & 127)).astype(f32).astype(bf16)
+        chunks = places // 128
+        rows = [jnp.where((position >> 7) == c, p, 0) for p in parts for c in range(chunks)]
+        rows = rows + [jnp.zeros((1, slots), jnp.int32)] * (-len(rows) % 16)
+        values = jnp.concatenate([r.astype(f32) for r in rows], axis=0).astype(bf16)
         moved = lax.dot_general(values, found, (((1,), (1,)), ((), ())), preferred_element_type=f32)
-        return moved.astype(jnp.int32)
+        moved = moved.astype(jnp.int32)
+        return [
+            jnp.concatenate([moved[i * chunks + c : i * chunks + c + 1] for c in range(chunks)], axis=1)
+            for i in range(len(parts))
+        ]
 
     parts = ((own, num_blocks), (heads, 2 * edge), (tails, 2 * edge))
+    cases = []
     for which in range(6):
         chosen, empty = parts[which % 3]
         dest, operand = row, source
         if which >= ADJOINT_OWN:
             dest, operand, empty = source, row, num_blocks
         used = live & chosen
-        wanted = jnp.where(used, dest, -1)
-        member = (key == wanted).astype(f32)
-        before = jnp.dot(member.astype(bf16), earlier, preferred_element_type=f32)
+        cases.append((dest, operand, empty, used, (key == jnp.where(used, dest, -1)).astype(f32)))
+    flip = live & (turned == 1)
+    ones = jnp.broadcast_to(flip.astype(f32), (16, slots))
+    members = jnp.concatenate([case[4].astype(bf16) for case in cases] + [ones.astype(bf16)], axis=0)
+    ranks = jnp.dot(members, earlier, preferred_element_type=f32)
+    for which, (dest, operand, empty, used, member) in enumerate(cases):
+        before = ranks[which * num_blocks : (which + 1) * num_blocks]
         pairs = (jnp.sum(member, axis=1, keepdims=True).astype(jnp.int32) + 1) >> 1
         wide = jnp.broadcast_to(pairs.astype(f32), (num_blocks, 128)).astype(bf16)
         offset = jnp.dot(below, wide, preferred_element_type=f32)[:, :1]
         position = jnp.sum(member * (before + 2.0 * offset), axis=0, keepdims=True).astype(jnp.int32)
         position = jnp.where(used, position, -1)
-        moved = invert(position, [index & 255, index >> 8, operand - empty, dest])
-        packed = moved[0:1] + (moved[1:2] << 8) + ((moved[2:3] + empty) << 9) + (moved[3:4] << 16)
-        tab[which : which + 1] = packed
+        low, high, move, to = invert(position, [index & 255, index >> 8, operand - empty, dest])
+        tab[which : which + 1] = low + (high << 8) + ((move + empty) << 9) + (to << 16)
         count = jnp.sum(pairs.astype(f32), axis=0, keepdims=True).astype(jnp.int32)
-        meta = meta + jnp.where(lane == which, (count + (UNROLL - 1)) // UNROLL, 0)
-    flip = live & (turned == 1)
-    ones = jnp.broadcast_to(flip.astype(f32), (8, slots))
-    rank = jnp.dot(ones.astype(bf16), earlier, preferred_element_type=f32)[:1].astype(jnp.int32)
-    rank = jnp.where(flip, rank, -1)
-    moved = invert(rank, [index & 255, index >> 8, flip.astype(jnp.int32)])
-    tab[FLIPS : FLIPS + 1] = jnp.where(moved[2:3] == 1, moved[0:1] + (moved[1:2] << 8), slots)
+        meta = meta + jnp.where(lane == which, (count + (HALF - 1)) // HALF, 0)
+    rank = jnp.where(flip, ranks[6 * num_blocks : 6 * num_blocks + 1].astype(jnp.int32), -1)
+    low, high, hit = invert(rank, [index & 255, index >> 8, flip.astype(jnp.int32)])
+    tab[FLIPS : FLIPS + 1] = jnp.where(hit == 1, low + (high << 8), slots)
     count = jnp.sum(ones[:1], axis=1, keepdims=True).astype(jnp.int32)
     meta = meta + jnp.where(lane == FLIPS, (count + (TURN - 1)) // TURN, 0)
     tab[TRIPS : TRIPS + 1] = meta
@@ -84,10 +92,10 @@
 def pair_loop(which, tab, source, matrix, acc):
     transposed = which >= ADJOINT_OWN
 
-    def body(step, carry):
+    def add(start, count):
         done = []
-        for u in range(UNROLL):
-            place = (step * UNROLL + u) * 2
+        for u in range(count):
+            place = (start + u) * 2
             one, two = tab[which, place], tab[which, place + 1]
             lhs = jnp.concatenate([source[(one >> 9) & 127], source[(two >> 9) & 127]], axis=1)
             first, second = matrix[one & 511], matrix[two & 511]
@@ -96,9 +104,18 @@
             done.append((one >> 16, lax.dot_general(lhs, rhs, dims, preferred_element_type=jnp.float32)))
         for dest, value in done:
             acc[dest] += value
+
+    halves = tab[TRIPS, which]
+
+    def body(step, carry):
+        add(step * UNROLL, UNROLL)
         return carry
 
-    lax.fori_loop(0, tab[TRIPS, which], body, 0)
+    lax.fori_loop(0, halves >> 1, body, 0)
+
+    @pl.when((halves & 1) == 1)
+    def _():
+        add((halves - 1) * HALF, HALF)
 
 
 def clear(ref):

time: 114 us -> 113 us (level)
  Pallas kernels: 36.8 us -> 25.1 us
  waiting for transfers between devices: 26 us -> 32.1 us
  starting transfers between devices: 24.8 us -> 29.9 us
    ppermute x16, waiting for transfers between devices: 26 us -> 32.1 us  [shift(): lax.ppermute(x, axis, [(i, (i + step) % count) for i in range(count)])]
    ppermute x16, starting transfers between devices: 24.8 us -> 29.9 us  [shift(): lax.ppermute(x, axis, [(i, (i + step) % count) for i in range(count)])]
    pallas_call x2, Pallas kernels: 5.85 us -> 2.64 us  [local(): call(functools.partial(middle_kernel, first), 'middle' + suffix, [rows_ty...]
    pallas_call x1, Pallas kernels: 9.97 us -> 6.97 us  [local(): call(first_kernel, 'own_first', [VM((slots + 1, size, size), bf16), tall_...]
    pallas_call x2, Pallas kernels: 3.51 us -> 1.57 us  [local(): call(functools.partial(heads_kernel, first), 'heads' + suffix, [rows_type...]
    pallas_call x2, Pallas kernels: 3.23 us -> 1.97 us  [local(): call(tails_kernel, 'tails' + suffix, [rim_type] * 2, [SMEM_SPEC] + [VMEM_...]
    pallas_call x2, Pallas kernels: 6.71 us -> 5.45 us  [local(): call(adjoint_kernel, 'adjoint' + suffix, [block_f32, norm_type] + ([middl...]
  transfers between devices with their start and end apart: 16 -> 16, of which waited for: 7 -> 9; matrix products, arithmetic and copies ran while one was open for 0% -> 0% of each run, Pallas kernels for 25% -> 17%
where the time goes in v4:
time: 113 us
  waiting for transfers between devices  32.1 us (28%)
  starting transfers between devices  29.9 us (26%)
  Pallas kernels  25.1 us (22%)
  blocking collectives  25 us (22%)
    ppermute x16, waiting for transfers between devices, shift(): lax.ppermute(x, axis, [(i, (i + step) % count) for i in range(count)])  32.1 us
    ppermute x16, starting transfers between devices, shift(): lax.ppermute(x, axis, [(i, (i + step) % count) for i in range(count)])  29.9 us
    all_to_all x1, blocking collectives, local(): sums = lax.all_to_all(message, ('layer', 'tile'), 0, 0, tiled=True)  25 us
    pallas_call x1, Pallas kernels, local(): call(first_kernel, 'own_first', [VM((slots + 1, size, size), bf16), tall_...  6.97 us
    pallas_call x2, Pallas kernels, local(): call(adjoint_kernel, 'adjoint' + suffix, [block_f32, norm_type] + ([middl...  5.45 us
    pallas_call x1, Pallas kernels, local(): call(own_kernel, 'own_next', [block_f32], [SMEM_SPEC] + [VMEM_SPEC] * 4,...  3.13 us
    pallas_call x2, Pallas kernels, local(): call(functools.partial(middle_kernel, first), 'middle' + suffix, [rows_ty...  2.64 us
  transfers between devices with their start and end apart: 16, of which 9 were waited for; matrix products, arithmetic and copies ran while one was open for 0% of the time, Pallas kernels for 17%

profile of v4, /device:TPU:1, one launch (start us, length us, event | category | flops | bytes accessed | tf_op | source)
XLA Modules:
  0.0 113.0 jit_solution(4028259622640161621)
XLA Ops:
  0.0 1.1 edges.1
  1.1 4.6 %collective-permute-start.1 = (bf16[1040,128]{1,0:T(8,128)(2,1)S(1)}, bf16[1040,128]{1,0:T(8,128)(2,1)S(1)}, u32[]{:S(2)}, u32[]{:S(2)}) collective-permute-start(bf16[1040,128]{1,0:T(8,128)(2,1)S(1)} %get-tuple-element.37), channel_id=1, source_target_pairs={{0,224},{32,0},{64,32},{96,64},{128,96},{160,128},{192,160},{224,1... | collective-permute-start | bytes 798728 | tf_op jit(solution)/shard_map/ppermute | solution.py:362
  5.7 1.0 collective-permute-start
  6.6 2.3 %collective-permute-start.2 = (bf16[1040,128]{1,0:T(8,128)(2,1)S(1)}, bf16[1040,128]{1,0:T(8,128)(2,1)S(1)}, u32[]{:S(2)}, u32[]{:S(2)}) collective-permute-start(bf16[1040,128]{1,0:T(8,128)(2,1)S(1)} %get-tuple-element.38), channel_id=1, source_target_pairs={{0,1},{1,2},{2,3},{3,4},{4,5},{5,6},{6,7},{7,8},{8,9},{9,10},{10,1... | collective-permute-start | bytes 798728 | tf_op jit(solution)/shard_map/ppermute | solution.py:362
  9.7 7.0 %own_first.1 = (bf16[321,128,128]{2,1,0:T(8,128)(2,1)S(1)}, f32[64,80,128]{2,1,0:T(8,128)S(1)}, s32[8,384]{1,0:T(8,128)S(1)}) custom-call(s32[3]{0:T(128)S(1)} %pad_add_fusion.count, bf16[320,128,128]{2,1,0:T(8,128)(2,1)} %bitcast.17, bf16[64,8192]{1,0:T(8,128)(2,1)} %bitcast.19, s32[1,320]{1,0:T(1,128)} %bitcast.21, s32[1,320]{1,0:T(1,128)} %bitcast.22, ...), custom_call_target="tpu_custom_call" | custom-call | flops 671088640 | bytes 20971520 | tf_op jit(solution)/shard_map/own_first/pallas_call | solution.py:429
  16.7 6.9 %collective-permute-done.right = bf16[1040,128]{1,0:T(8,128)(2,1)S(1)} collective-permute-done((bf16[1040,128]{1,0:T(8,128)(2,1)S(1)}, bf16[1040,128]{1,0:T(8,128)(2,1)S(1)}, u32[]{:S(2)}, u32[]{:S(2)}) %collective-permute-start) | collective-permute-done | bytes 266272 | tf_op jit(solution)/shard_map/ppermute | solution.py:362
  23.6 0.8 heads_first.1.rows_in
  24.5 1.4 %middle_first.1 = (f32[64,80,128]{2,1,0:T(8,128)S(1)}, bf16[65,64,128]{2,1,0:T(8,128)(2,1)S(1)}, f32[64,8,128]{2,1,0:T(8,128)S(1)}, bf16[1024,128]{1,0:T(8,128)(2,1)S(1)}, bf16[1024,128]{1,0:T(8,128)(2,1)S(1)}) custom-call(s32[8,384]{1,0:T(8,128)S(1)} %get-tuple-element.34.tab, ...), custom_call_target="tpu_custom_call", output_to_operand_aliasing={{0}: (2, {})} | custom-call | flops 335544320 | bytes 5242880 | tf_op jit(solution)/shard_map/middle_first/pallas_call | solution.py:481
  25.8 3.7 %collective-permute-start.4 = (bf16[1024,128]{1,0:T(8,128)(2,1)S(1)}, bf16[1024,128]{1,0:T(8,128)(2,1)S(1)}, u32[]{:S(2)}, u32[]{:S(2)}) collective-permute-start(bf16[1024,128]{1,0:T(8,128)(2,1)S(1)} %get-tuple-element.41), channel_id=1, source_target_pairs={{0,1},{1,2},{2,3},{3,4},{4,5},{5,6},{6,7},{7,8},{8,9},{9,10},{10,1... | collective-permute-start | bytes 786440 | tf_op jit(solution)/shard_map/ppermute | solution.py:362
  29.5 1.2 %collective-permute-start.5 = (bf16[1024,128]{1,0:T(8,128)(2,1)S(1)}, bf16[1024,128]{1,0:T(8,128)(2,1)S(1)}, u32[]{:S(2)}, u32[]{:S(2)}) collective-permute-start(bf16[1024,128]{1,0:T(8,128)(2,1)S(1)} %get-tuple-element.42), channel_id=1, source_target_pairs={{0,32},{32,64},{64,96},{96,128},{128,160},{160,192},{192,224},{224... | collective-permute-start | bytes 786440 | tf_op jit(solution)/shard_map/ppermute | solution.py:362
  30.7 1.0 tails_first.1
  31.8 3.1 %collective-permute-start.7 = (bf16[1024,128]{1,0:T(8,128)(2,1)S(1)}, bf16[1024,128]{1,0:T(8,128)(2,1)S(1)}, u32[]{:S(2)}, u32[]{:S(2)}) collective-permute-start(bf16[1024,128]{1,0:T(8,128)(2,1)S(1)} %get-tuple-element.47), channel_id=1, source_target_pairs={{0,224},{32,0},{64,32},{96,64},{128,96},{160,128},{192,160},{224,1... | collective-permute-start | bytes 786440 | tf_op jit(solution)/shard_map/ppermute | solution.py:362
  34.9 2.7 %adjoint_first.1 = (f32[64,64,128]{2,1,0:T(8,128)S(1)}, f32[64,128]{1,0:T(8,128)S(1)}, bf16[32,64,128]{2,1,0:T(8,128)(2,1)S(1)}) custom-call(s32[8,384]{1,0:T(8,128)S(1)} %get-tuple-element.34.tab, bf16[321,128,128]{2,1,0:T(8,128)(2,1)S(1)} %get-tuple-element.35.matrix, bf16[65,64,128]{2,1,0:T(8,128)(2,1)S(1)} %get-tuple-element.39.image, ...), custom_call_target="tpu_custom_call" | custom-call | flops 335544320 | bytes 5242880 | tf_op jit(solution)/shard_map/adjoint_first/pallas_call | solution.py:506
  37.7 3.8 %collective-permute-done.5.two = bf16[1024,128]{1,0:T(8,128)(2,1)S(1)} collective-permute-done((bf16[1024,128]{1,0:T(8,128)(2,1)S(1)}, bf16[1024,128]{1,0:T(8,128)(2,1)S(1)}, u32[]{:S(2)}, u32[]{:S(2)}) %collective-permute-start.5) | collective-permute-done | bytes 262176 | tf_op jit(solution)/shard_map/ppermute | solution.py:362
  41.6 1.8 %collective-permute-start.9 = (bf16[1024,128]{1,0:T(8,128)(2,1)S(1)}, bf16[1024,128]{1,0:T(8,128)(2,1)S(1)}, u32[]{:S(2)}, u32[]{:S(2)}) collective-permute-start(bf16[1024,128]{1,0:T(8,128)(2,1)S(1)} %get-tuple-element.44.head), channel_id=1, source_target_pairs={{0,224},{32,0},{64,32},{96,64},{128,96},{160,128},{192,160},{224,1... | collective-permute-start | bytes 786440 | tf_op jit(solution)/shard_map/ppermute | solution.py:362
  43.4 3.1 %collective-permute-start.8 = (bf16[1024,128]{1,0:T(8,128)(2,1)S(1)}, bf16[1024,128]{1,0:T(8,128)(2,1)S(1)}, u32[]{:S(2)}, u32[]{:S(2)}) collective-permute-start(bf16[1024,128]{1,0:T(8,128)(2,1)S(1)} %get-tuple-element.44.head), channel_id=1, source_target_pairs={{0,31},{1,0},{2,1},{3,2},{4,3},{5,4},{6,5},{7,6},{8,7},{9,8},{10,9... | collective-permute-start | bytes 786440 | tf_op jit(solution)/shard_map/ppermute | solution.py:362
  46.7 7.2 %collective-permute-done.7.two = bf16[1024,128]{1,0:T(8,128)(2,1)S(1)} collective-permute-done((bf16[1024,128]{1,0:T(8,128)(2,1)S(1)}, bf16[1024,128]{1,0:T(8,128)(2,1)S(1)}, u32[]{:S(2)}, u32[]{:S(2)}) %collective-permute-start.7) | collective-permute-done | bytes 262176 | tf_op jit(solution)/shard_map/ppermute | solution.py:362
  54.2 3.1 %own_next.1.rows_in = f32[64,64,128]{2,1,0:T(8,128)S(1)} custom-call(s32[8,384]{1,0:T(8,128)S(1)} %get-tuple-element.34.tab, bf16[321,128,128]{2,1,0:T(8,128)(2,1)S(1)} %get-tuple-element.35.matrix, bf16[1024,128]{1,0:T(8,128)(2,1)S(1)} %get-tuple-element.44.head, bf16[32,64,128]{2,1,0:T(8,128)(2,1)S(1)} %get-tuple-element.45.middle, ...), custom_call_target="tpu_custom_call" | custom-call | flops 335544320 | bytes 5242880 | tf_op jit(solution)/shard_map/own_next/pallas_call | solution.py:461
  57.3 1.8 %collective-permute-done.9.lower = bf16[1024,128]{1,0:T(8,128)(2,1)S(1)} collective-permute-done((bf16[1024,128]{1,0:T(8,128)(2,1)S(1)}, bf16[1024,128]{1,0:T(8,128)(2,1)S(1)}, u32[]{:S(2)}, u32[]{:S(2)}) %collective-permute-start.9) | collective-permute-done | bytes 262176 | tf_op jit(solution)/shard_map/ppermute | solution.py:362
  59.2 4.4 %collective-permute-done.8.right = bf16[1024,128]{1,0:T(8,128)(2,1)S(1)} collective-permute-done((bf16[1024,128]{1,0:T(8,128)(2,1)S(1)}, bf16[1024,128]{1,0:T(8,128)(2,1)S(1)}, u32[]{:S(2)}, u32[]{:S(2)}) %collective-permute-start.8) | collective-permute-done | bytes 262176 | tf_op jit(solution)/shard_map/ppermute | solution.py:362
  63.5 0.8 heads_next.1.rows_in
  64.3 1.3 %middle_next.1 = (f32[64,64,128]{2,1,0:T(8,128)S(1)}, bf16[65,64,128]{2,1,0:T(8,128)(2,1)S(1)}, bf16[1024,128]{1,0:T(8,128)(2,1)S(1)}, bf16[1024,128]{1,0:T(8,128)(2,1)S(1)}) custom-call(s32[8,384]{1,0:T(8,128)S(1)} %get-tuple-element.34.tab, bf16[321,128,128]{2,1,0:T(8,128)(2,1)S(1)} %get-tuple-element.35.matrix, ...), custom_call_target="tpu_custom_call", output_to_operand_aliasing={{0}: (2, {})} | custom-call | flops 335544320 | bytes 5242880 | tf_op jit(solution)/shard_map/middle_next/pallas_call | solution.py:481
  65.6 4.6 %collective-permute-start.12 = (bf16[1024,128]{1,0:T(8,128)(2,1)S(1)}, bf16[1024,128]{1,0:T(8,128)(2,1)S(1)}, u32[]{:S(2)}, u32[]{:S(2)}) collective-permute-start(bf16[1024,128]{1,0:T(8,128)(2,1)S(1)} %get-tuple-element.53), channel_id=1, source_target_pairs={{0,1},{1,2},{2,3},{3,4},{4,5},{5,6},{6,7},{7,8},{8,9},{9,10},{10,1... | collective-permute-start | bytes 786440 | tf_op jit(solution)/shard_map/ppermute | solution.py:362
  70.1 1.7 %collective-permute-start.13 = (bf16[1024,128]{1,0:T(8,128)(2,1)S(1)}, bf16[1024,128]{1,0:T(8,128)(2,1)S(1)}, u32[]{:S(2)}, u32[]{:S(2)}) collective-permute-start(bf16[1024,128]{1,0:T(8,128)(2,1)S(1)} %get-tuple-element.54), channel_id=1, source_target_pairs={{0,32},{32,64},{64,96},{96,128},{128,160},{160,192},{192,224},{224... | collective-permute-start | bytes 786440 | tf_op jit(solution)/shard_map/ppermute | solution.py:362
  71.8 1.0 tails_next.1
  72.9 2.6 %collective-permute-start.15 = (bf16[1024,128]{1,0:T(8,128)(2,1)S(1)}, bf16[1024,128]{1,0:T(8,128)(2,1)S(1)}, u32[]{:S(2)}, u32[]{:S(2)}) collective-permute-start(bf16[1024,128]{1,0:T(8,128)(2,1)S(1)} %get-tuple-element.56), channel_id=1, source_target_pairs={{0,224},{32,0},{64,32},{96,64},{128,96},{160,128},{192,160},{224,1... | collective-permute-start | bytes 786440 | tf_op jit(solution)/shard_map/ppermute | solution.py:362
  75.5 2.7 %adjoint_next.1 = (f32[64,64,128]{2,1,0:T(8,128)S(1)}, f32[64,128]{1,0:T(8,128)S(1)}) custom-call(s32[8,384]{1,0:T(8,128)S(1)} %get-tuple-element.34.tab, bf16[321,128,128]{2,1,0:T(8,128)(2,1)S(1)} %get-tuple-element.35.matrix, bf16[65,64,128]{2,1,0:T(8,128)(2,1)S(1)} %get-tuple-element.51.image, f32[64,128]{1,0:T(8,128)S(1)} %get-tuple-element.33.weights), custom_call_target="tpu_custom_call" | custom-call | flops 335544320 | bytes 5242880 | tf_op jit(solution)/shard_map/adjoint_next/pallas_call | solution.py:506
  78.2 0.6 collective-permute-done.12.low0
  78.9 4.1 %collective-permute-done.13.low1 = bf16[1024,128]{1,0:T(8,128)(2,1)S(1)} collective-permute-done((bf16[1024,128]{1,0:T(8,128)(2,1)S(1)}, bf16[1024,128]{1,0:T(8,128)(2,1)S(1)}, u32[]{:S(2)}, u32[]{:S(2)}) %collective-permute-start.13) | collective-permute-done | bytes 262176 | tf_op jit(solution)/shard_map/ppermute | solution.py:362
  83.0 3.0 %collective-permute-done.15.high1 = bf16[1024,128]{1,0:T(8,128)(2,1)S(1)} collective-permute-done((bf16[1024,128]{1,0:T(8,128)(2,1)S(1)}, bf16[1024,128]{1,0:T(8,128)(2,1)S(1)}, u32[]{:S(2)}, u32[]{:S(2)}) %collective-permute-start.15) | collective-permute-done | bytes 262176 | tf_op jit(solution)/shard_map/ppermute | solution.py:362
  86.7 25.0 %all_to_all.11 = f32[256,1,128]{2,1,0:T(1,128)S(1)} all-to-all(f32[256,1,128]{2,1,0:T(1,128)S(1)} %bitcast.16), channel_id=1, replica_groups=mesh['layer'=8,'tile'=32] {'layer','tile'}, dimensions={0} | all-to-all | bytes 262144 | tf_op jit(solution)/shard_map/all_to_all | solution.py:548
  111.6 1.3 %write_out.1 = bf16[64,8192]{1,0:T(8,128)(2,1)} custom-call(f32[256,128]{1,0:T(8,128)S(1)} %bitcast.15, f32[64,64,128]{2,1,0:T(8,128)S(1)} %get-tuple-element.60.total), custom_call_target="tpu_custom_call" | custom-call | bytes 3145728 | tf_op jit(solution)/shard_map/write_out/pallas_call | solution.py:549
  (17 shorter events, 1.6 us)
Async XLA Ops:
  1.1 15.6 %collective-permute-start.1 = (bf16[1040,128]{1,0:T(8,128)(2,1)S(1)}, bf16[1040,128]{1,0:T(8,128)(2,1)S(1)}, u32[]{:S(2)}, u32[]{:S(2)}) collective-permute-start(bf16[1040,128]{1,0:T(8,128)(2,1)S(1)} %get-tuple-element.37), channel_id=1, source_target_pairs={{0,224},{32,0},{64,32},{96,64},{128,96},{160,128},{192,160},{224,1... | collective-permute-start | bytes 798728 | tf_op jit(solution)/shard_map/ppermute | solution.py:362
  5.7 18.0 %collective-permute-start = (bf16[1040,128]{1,0:T(8,128)(2,1)S(1)}, bf16[1040,128]{1,0:T(8,128)(2,1)S(1)}, u32[]{:S(2)}, u32[]{:S(2)}) collective-permute-start(bf16[1040,128]{1,0:T(8,128)(2,1)S(1)} %get-tuple-element.37), channel_id=1, source_target_pairs={{0,31},{1,0},{2,1},{3,2},{4,3},{5,4},{6,5},{7,6},{8,7},{9,8},{10,9... | collective-permute-start | bytes 798728 | tf_op jit(solution)/shard_map/ppermute | solution.py:362
  6.6 17.8 %collective-permute-start.3 = (bf16[1040,128]{1,0:T(8,128)(2,1)S(1)}, bf16[1040,128]{1,0:T(8,128)(2,1)S(1)}, u32[]{:S(2)}, u32[]{:S(2)}) collective-permute-start(bf16[1040,128]{1,0:T(8,128)(2,1)S(1)} %get-tuple-element.38), channel_id=1, source_target_pairs={{0,32},{32,64},{64,96},{96,128},{128,160},{160,192},{192,224},{224... | collective-permute-start | bytes 798728 | tf_op jit(solution)/shard_map/ppermute | solution.py:362
  6.6 17.8 %collective-permute-start.2 = (bf16[1040,128]{1,0:T(8,128)(2,1)S(1)}, bf16[1040,128]{1,0:T(8,128)(2,1)S(1)}, u32[]{:S(2)}, u32[]{:S(2)}) collective-permute-start(bf16[1040,128]{1,0:T(8,128)(2,1)S(1)} %get-tuple-element.38), channel_id=1, source_target_pairs={{0,1},{1,2},{2,3},{3,4},{4,5},{5,6},{6,7},{7,8},{8,9},{9,10},{10,1... | collective-permute-start | bytes 798728 | tf_op jit(solution)/shard_map/ppermute | solution.py:362
  25.8 11.8 %collective-permute-start.4 = (bf16[1024,128]{1,0:T(8,128)(2,1)S(1)}, bf16[1024,128]{1,0:T(8,128)(2,1)S(1)}, u32[]{:S(2)}, u32[]{:S(2)}) collective-permute-start(bf16[1024,128]{1,0:T(8,128)(2,1)S(1)} %get-tuple-element.41), channel_id=1, source_target_pairs={{0,1},{1,2},{2,3},{3,4},{4,5},{5,6},{6,7},{7,8},{8,9},{9,10},{10,1... | collective-permute-start | bytes 786440 | tf_op jit(solution)/shard_map/ppermute | solution.py:362
  29.5 11.9 %collective-permute-start.5 = (bf16[1024,128]{1,0:T(8,128)(2,1)S(1)}, bf16[1024,128]{1,0:T(8,128)(2,1)S(1)}, u32[]{:S(2)}, u32[]{:S(2)}) collective-permute-start(bf16[1024,128]{1,0:T(8,128)(2,1)S(1)} %get-tuple-element.42), channel_id=1, source_target_pairs={{0,32},{32,64},{64,96},{96,128},{128,160},{160,192},{192,224},{224... | collective-permute-start | bytes 786440 | tf_op jit(solution)/shard_map/ppermute | solution.py:362
  31.7 15.0 %collective-permute-start.6 = (bf16[1024,128]{1,0:T(8,128)(2,1)S(1)}, bf16[1024,128]{1,0:T(8,128)(2,1)S(1)}, u32[]{:S(2)}, u32[]{:S(2)}) collective-permute-start(bf16[1024,128]{1,0:T(8,128)(2,1)S(1)} %get-tuple-element.46), channel_id=1, source_target_pairs={{0,31},{1,0},{2,1},{3,2},{4,3},{5,4},{6,5},{7,6},{8,7},{9,8},{10,9... | collective-permute-start | bytes 786440 | tf_op jit(solution)/shard_map/ppermute | solution.py:362
  31.8 22.1 %collective-permute-start.7 = (bf16[1024,128]{1,0:T(8,128)(2,1)S(1)}, bf16[1024,128]{1,0:T(8,128)(2,1)S(1)}, u32[]{:S(2)}, u32[]{:S(2)}) collective-permute-start(bf16[1024,128]{1,0:T(8,128)(2,1)S(1)} %get-tuple-element.47), channel_id=1, source_target_pairs={{0,224},{32,0},{64,32},{96,64},{128,96},{160,128},{192,160},{224,1... | collective-permute-start | bytes 786440 | tf_op jit(solution)/shard_map/ppermute | solution.py:362
  41.6 17.5 %collective-permute-start.9 = (bf16[1024,128]{1,0:T(8,128)(2,1)S(1)}, bf16[1024,128]{1,0:T(8,128)(2,1)S(1)}, u32[]{:S(2)}, u32[]{:S(2)}) collective-permute-start(bf16[1024,128]{1,0:T(8,128)(2,1)S(1)} %get-tuple-element.44.head), channel_id=1, source_target_pairs={{0,224},{32,0},{64,32},{96,64},{128,96},{160,128},{192,160},{224,1... | collective-permute-start | bytes 786440 | tf_op jit(solution)/shard_map/ppermute | solution.py:362
  43.4 20.1 %collective-permute-start.8 = (bf16[1024,128]{1,0:T(8,128)(2,1)S(1)}, bf16[1024,128]{1,0:T(8,128)(2,1)S(1)}, u32[]{:S(2)}, u32[]{:S(2)}) collective-permute-start(bf16[1024,128]{1,0:T(8,128)(2,1)S(1)} %get-tuple-element.44.head), channel_id=1, source_target_pairs={{0,31},{1,0},{2,1},{3,2},{4,3},{5,4},{6,5},{7,6},{8,7},{9,8},{10,9... | collective-permute-start | bytes 786440 | tf_op jit(solution)/shard_map/ppermute | solution.py:362
  54.0 10.3 %collective-permute-start.11 = (bf16[1024,128]{1,0:T(8,128)(2,1)S(1)}, bf16[1024,128]{1,0:T(8,128)(2,1)S(1)}, u32[]{:S(2)}, u32[]{:S(2)}) collective-permute-start(bf16[1024,128]{1,0:T(8,128)(2,1)S(1)} %get-tuple-element.49.tail), channel_id=1, source_target_pairs={{0,32},{32,64},{64,96},{96,128},{128,160},{160,192},{192,224},{224... | collective-permute-start | bytes 786440 | tf_op jit(solution)/shard_map/ppermute | solution.py:362
  54.1 10.2 %collective-permute-start.10 = (bf16[1024,128]{1,0:T(8,128)(2,1)S(1)}, bf16[1024,128]{1,0:T(8,128)(2,1)S(1)}, u32[]{:S(2)}, u32[]{:S(2)}) collective-permute-start(bf16[1024,128]{1,0:T(8,128)(2,1)S(1)} %get-tuple-element.49.tail), channel_id=1, source_target_pairs={{0,1},{1,2},{2,3},{3,4},{4,5},{5,6},{6,7},{7,8},{8,9},{9,10},{10,1... | collective-permute-start | bytes 786440 | tf_op jit(solution)/shard_map/ppermute | solution.py:362
  65.6 13.3 %collective-permute-start.12 = (bf16[1024,128]{1,0:T(8,128)(2,1)S(1)}, bf16[1024,128]{1,0:T(8,128)(2,1)S(1)}, u32[]{:S(2)}, u32[]{:S(2)}) collective-permute-start(bf16[1024,128]{1,0:T(8,128)(2,1)S(1)} %get-tuple-element.53), channel_id=1, source_target_pairs={{0,1},{1,2},{2,3},{3,4},{4,5},{5,6},{6,7},{7,8},{8,9},{9,10},{10,1... | collective-permute-start | bytes 786440 | tf_op jit(solution)/shard_map/ppermute | solution.py:362
  70.1 12.9 %collective-permute-start.13 = (bf16[1024,128]{1,0:T(8,128)(2,1)S(1)}, bf16[1024,128]{1,0:T(8,128)(2,1)S(1)}, u32[]{:S(2)}, u32[]{:S(2)}) collective-permute-start(bf16[1024,128]{1,0:T(8,128)(2,1)S(1)} %get-tuple-element.54), channel_id=1, source_target_pairs={{0,32},{32,64},{64,96},{96,128},{128,160},{160,192},{192,224},{224... | collective-permute-start | bytes 786440 | tf_op jit(solution)/shard_map/ppermute | solution.py:362
  72.8 10.2 %collective-permute-start.14 = (bf16[1024,128]{1,0:T(8,128)(2,1)S(1)}, bf16[1024,128]{1,0:T(8,128)(2,1)S(1)}, u32[]{:S(2)}, u32[]{:S(2)}) collective-permute-start(bf16[1024,128]{1,0:T(8,128)(2,1)S(1)} %get-tuple-element.55), channel_id=1, source_target_pairs={{0,31},{1,0},{2,1},{3,2},{4,3},{5,4},{6,5},{7,6},{8,7},{9,8},{10,9... | collective-permute-start | bytes 786440 | tf_op jit(solution)/shard_map/ppermute | solution.py:362
  72.9 13.1 %collective-permute-start.15 = (bf16[1024,128]{1,0:T(8,128)(2,1)S(1)}, bf16[1024,128]{1,0:T(8,128)(2,1)S(1)}, u32[]{:S(2)}, u32[]{:S(2)}) collective-permute-start(bf16[1024,128]{1,0:T(8,128)(2,1)S(1)} %get-tuple-element.56), channel_id=1, source_target_pairs={{0,224},{32,0},{64,32},{96,64},{128,96},{160,128},{192,160},{224,1... | collective-permute-start | bytes 786440 | tf_op jit(solution)/shard_map/ppermute | solution.py:362

commit v5 on v4

--- a/solution.py
+++ b/solution.py
@@ -15,7 +15,7 @@
 VMEM_SPEC = pl.BlockSpec(memory_space=pltpu.VMEM)
 SMEM_SPEC = pl.BlockSpec(memory_space=pltpu.SMEM)
 HBM_SPEC = pl.BlockSpec(memory_space=pltpu.HBM)
-FORWARD_OWN, FORWARD_HEADS, FORWARD_TAILS, ADJOINT_OWN, ADJOINT_HEADS, ADJOINT_TAILS, FLIPS, TRIPS = range(8)
+INNER, OUTER, FORWARD_HEADS, FORWARD_TAILS, ADJOINT_OWN, ADJOINT_HEADS, ADJOINT_TAILS, FLIPS = range(8)
 
 
 def fill_tables(live_count, above, beneath, row, col, turned, num_blocks, tab):
@@ -57,11 +57,12 @@
             for i in range(len(parts))
         ]
 
-    parts = ((own, num_blocks), (heads, 2 * edge), (tails, 2 * edge))
+    inner = own & (col >= edge) & (col < num_blocks - edge)
+    parts = (inner, own & ~inner, heads, tails, own, heads, tails)
     cases = []
-    for which in range(6):
-        chosen, empty = parts[which % 3]
-        dest, operand = row, source
+    for which in range(FLIPS):
+        chosen = parts[which]
+        dest, operand, empty = row, source, num_blocks if which < FORWARD_HEADS else 2 * edge
         if which >= ADJOINT_OWN:
             dest, operand, empty = source, row, num_blocks
         used = live & chosen
@@ -80,13 +81,13 @@
         low, high, move, to = invert(position, [index & 255, index >> 8, operand - empty, dest])
         tab[which : which + 1] = low + (high << 8) + ((move + empty) << 9) + (to << 16)
         count = jnp.sum(pairs.astype(f32), axis=0, keepdims=True).astype(jnp.int32)
-        meta = meta + jnp.where(lane == which, (count + (HALF - 1)) // HALF, 0)
-    rank = jnp.where(flip, ranks[6 * num_blocks : 6 * num_blocks + 1].astype(jnp.int32), -1)
+        meta = meta + jnp.where(lane == slots + which, (count + (HALF - 1)) // HALF, 0)
+    rank = jnp.where(flip, ranks[FLIPS * num_blocks : FLIPS * num_blocks + 1].astype(jnp.int32), -1)
     low, high, hit = invert(rank, [index & 255, index >> 8, flip.astype(jnp.int32)])
-    tab[FLIPS : FLIPS + 1] = jnp.where(hit == 1, low + (high << 8), slots)
     count = jnp.sum(ones[:1], axis=1, keepdims=True).astype(jnp.int32)
-    meta = meta + jnp.where(lane == FLIPS, (count + (TURN - 1)) // TURN, 0)
-    tab[TRIPS : TRIPS + 1] = meta
+    meta = meta + jnp.where(lane == slots + FLIPS, (count + (TURN - 1)) // TURN, 0)
+    flips = jnp.where(hit == 1, low + (high << 8), slots)
+    tab[FLIPS : FLIPS + 1] = jnp.where(lane < slots, flips, meta)
 
 
 def pair_loop(which, tab, source, matrix, acc):
@@ -105,7 +106,7 @@
         for dest, value in done:
             acc[dest] += value
 
-    halves = tab[TRIPS, which]
+    halves = tab[FLIPS, matrix.shape[0] - 1 + which]
 
     def body(step, carry):
         add(step * UNROLL, UNROLL)
@@ -199,21 +200,29 @@
             matrix[slot] = value
         return carry
 
-    lax.fori_loop(0, smem[TRIPS, FLIPS], turn, 0)
-    pair_loop(FORWARD_OWN, smem, source, matrix, rows)
-
-
-def own_kernel(tab, matrix, head, middle, tail, rows, source):
+    lax.fori_loop(0, smem[FLIPS, slots + FLIPS], turn, 0)
+    pair_loop(INNER, smem, source, matrix, rows)
+    pair_loop(OUTER, smem, source, matrix, rows)
+
+
+def inner_kernel(tab, matrix, middle, rows, source):
     clear(rows)
     num_blocks = rows.shape[0]
     edge = num_blocks // 4
-    vectors = rows.shape[1]
+    source[edge : num_blocks - edge] = middle[...]
+    source[num_blocks] = jnp.zeros(source.shape[1:], source.dtype)
+    pair_loop(INNER, tab, source, matrix, rows)
+
+
+def outer_kernel(tab, matrix, head, tail, rows_in, rows, source):
+    del rows_in
+    num_blocks, vectors = rows.shape[:2]
+    edge = num_blocks // 4
     for b in range(edge):
         source[b] = head[b * vectors : (b + 1) * vectors]
         source[num_blocks - edge + b] = tail[b * vectors : (b + 1) * vectors]
-    source[edge : num_blocks - edge] = middle[...]
     source[num_blocks] = jnp.zeros(source.shape[1:], source.dtype)
-    pair_loop(FORWARD_OWN, tab, source, matrix, rows)
+    pair_loop(OUTER, tab, source, matrix, rows)
 
 
 def load_rims(first, rims, source):
@@ -459,14 +468,15 @@
         suffix = "_first" if first else "_next"
         if not first:
             (rows,) = call(
-                own_kernel,
-                "own_next",
+                outer_kernel,
+                "outer",
                 [block_f32],
                 [SMEM_SPEC] + [VMEM_SPEC] * 4,
                 [VM((num_blocks + 1, vectors, size), bf16)],
-                work,
-                blocks.size,
-            )(tab, matrix, head, middle, tail)
+                work // 2,
+                blocks.size // 2,
+                {4: 0},
+            )(tab, matrix, head, tail, rows)
         (rows,) = call(
             functools.partial(heads_kernel, first),
             "heads" + suffix,
@@ -514,7 +524,15 @@
         )(tab, matrix, image, weights)
         total, norm = result[:2]
         if first:
-            middle = result[2]
+            (rows,) = call(
+                inner_kernel,
+                "inner",
+                [block_f32],
+                [SMEM_SPEC] + [VMEM_SPEC] * 2,
+                [VM((num_blocks + 1, vectors, size), bf16)],
+                work // 2,
+                blocks.size // 2,
+            )(tab, matrix, result[2])
             head, norm = call(
                 functools.partial(join_kernel, False),
                 "join_head",
@@ -525,6 +543,7 @@
                 edge * vectors * size * 8,
             )(total, weights, *lows, norm)
             heads = heads_out(head)
+            norm, rows = lax.optimization_barrier((norm, rows))
             tail, norm_first = call(
                 functools.partial(join_kernel, True),
                 "join_tail",

time: 113 us -> 112 us (level)
  starting transfers between devices: 29.9 us -> 23.8 us
  Pallas kernels: 25.1 us -> 29.8 us
  waiting for transfers between devices: 32.1 us -> 34.5 us
  blocking collectives: 25 us -> 23.1 us
    ppermute x16, starting transfers between devices: 29.9 us -> 23.8 us  [shift(): lax.ppermute(x, axis, [(i, (i + step) % count) for i in range(count)])]
    ppermute x16, waiting for transfers between devices: 32.1 us -> 34.5 us  [shift(): lax.ppermute(x, axis, [(i, (i + step) % count) for i in range(count)])]
    all_to_all x1, blocking collectives: 25 us -> 23.1 us  [local(): sums = lax.all_to_all(message, ('layer', 'tile'), 0, 0, tiled=True)]
    pallas_call x1 -> x2, Pallas kernels: 3.13 us -> 4.47 us  [the longest x1 2.41 us: local(): call(inner_kernel, 'inner', [block_f32], [SMEM_SPEC] + [VMEM_SPEC] * 2, [...]
  transfers between devices with their start and end apart: 16 -> 16, of which waited for: 9 -> 8; matrix products, arithmetic and copies ran while one was open for 0% -> 0% of each run, Pallas kernels for 17% -> 20%
where the time goes in v5:
time: 112 us
  waiting for transfers between devices  34.5 us (31%)
  Pallas kernels  29.8 us (27%)
  starting transfers between devices  23.8 us (21%)
  blocking collectives  23.1 us (21%)
    ppermute x16, waiting for transfers between devices, shift(): lax.ppermute(x, axis, [(i, (i + step) % count) for i in range(count)])  34.5 us
    ppermute x16, starting transfers between devices, shift(): lax.ppermute(x, axis, [(i, (i + step) % count) for i in range(count)])  23.8 us
    all_to_all x1, blocking collectives, local(): sums = lax.all_to_all(message, ('layer', 'tile'), 0, 0, tiled=True)  23.1 us
    pallas_call x1, Pallas kernels, local(): call(first_kernel, 'own_first', [VM((slots + 1, size, size), bf16), tall_...  7.89 us
    pallas_call x2, Pallas kernels, local(): call(adjoint_kernel, 'adjoint' + suffix, [block_f32, norm_type] + ([middl...  5.63 us
    pallas_call x2, Pallas kernels, local(): call(functools.partial(middle_kernel, first), 'middle' + suffix, [rows_ty...  3.76 us
    pallas_call x2, Pallas kernels, local(): call(tails_kernel, 'tails' + suffix, [rim_type] * 2, [SMEM_SPEC] + [VMEM_...  2.45 us
    pallas_call x1, Pallas kernels, local(): call(inner_kernel, 'inner', [block_f32], [SMEM_SPEC] + [VMEM_SPEC] * 2, [...  2.41 us
  transfers between devices with their start and end apart: 16, of which 8 were waited for; matrix products, arithmetic and copies ran while one was open for 0% of the time, Pallas kernels for 20%

profile of v5, /device:TPU:1, one launch (start us, length us, event | category | flops | bytes accessed | tf_op | source)
XLA Modules:
  0.0 112.1 jit_solution(2744913062362355770)
XLA Ops:
  0.0 1.1 edges.1
  1.1 4.6 %collective-permute-start.1 = (bf16[1040,128]{1,0:T(8,128)(2,1)S(1)}, bf16[1040,128]{1,0:T(8,128)(2,1)S(1)}, u32[]{:S(2)}, u32[]{:S(2)}) collective-permute-start(bf16[1040,128]{1,0:T(8,128)(2,1)S(1)} %get-tuple-element.39), channel_id=1, source_target_pairs={{0,224},{32,0},{64,32},{96,64},{128,96},{160,128},{192,160},{224,1... | collective-permute-start | bytes 798728 | tf_op jit(solution)/shard_map/ppermute | solution.py:371
  5.7 1.0 collective-permute-start
  6.6 2.3 %collective-permute-start.2 = (bf16[1040,128]{1,0:T(8,128)(2,1)S(1)}, bf16[1040,128]{1,0:T(8,128)(2,1)S(1)}, u32[]{:S(2)}, u32[]{:S(2)}) collective-permute-start(bf16[1040,128]{1,0:T(8,128)(2,1)S(1)} %get-tuple-element.40), channel_id=1, source_target_pairs={{0,1},{1,2},{2,3},{3,4},{4,5},{5,6},{6,7},{7,8},{8,9},{9,10},{10,1... | collective-permute-start | bytes 798728 | tf_op jit(solution)/shard_map/ppermute | solution.py:371
  9.7 7.9 %own_first.1 = (bf16[321,128,128]{2,1,0:T(8,128)(2,1)S(1)}, f32[64,80,128]{2,1,0:T(8,128)S(1)}, s32[8,384]{1,0:T(8,128)S(1)}) custom-call(s32[3]{0:T(128)S(1)} %pad_add_fusion.count, bf16[320,128,128]{2,1,0:T(8,128)(2,1)} %bitcast.17, bf16[64,8192]{1,0:T(8,128)(2,1)} %bitcast.19, s32[1,320]{1,0:T(1,128)} %bitcast.21, s32[1,320]{1,0:T(1,128)} %bitcast.22, ...), custom_call_target="tpu_custom_call" | custom-call | flops 671088640 | bytes 20971520 | tf_op jit(solution)/shard_map/own_first/pallas_call | solution.py:438
  17.6 6.0 %collective-permute-done.right = bf16[1040,128]{1,0:T(8,128)(2,1)S(1)} collective-permute-done((bf16[1040,128]{1,0:T(8,128)(2,1)S(1)}, bf16[1040,128]{1,0:T(8,128)(2,1)S(1)}, u32[]{:S(2)}, u32[]{:S(2)}) %collective-permute-start) | collective-permute-done | bytes 266272 | tf_op jit(solution)/shard_map/ppermute | solution.py:371
  23.6 1.1 heads_first.1.rows_in
  24.8 1.9 %middle_first.1 = (f32[64,80,128]{2,1,0:T(8,128)S(1)}, bf16[65,64,128]{2,1,0:T(8,128)(2,1)S(1)}, f32[64,8,128]{2,1,0:T(8,128)S(1)}, bf16[1024,128]{1,0:T(8,128)(2,1)S(1)}, bf16[1024,128]{1,0:T(8,128)(2,1)S(1)}) custom-call(s32[8,384]{1,0:T(8,128)S(1)} %get-tuple-element.36.tab, ...), custom_call_target="tpu_custom_call", output_to_operand_aliasing={{0}: (2, {})} | custom-call | flops 335544320 | bytes 5242880 | tf_op jit(solution)/shard_map/middle_first/pallas_call | solution.py:491
  26.7 2.7 %collective-permute-start.4 = (bf16[1024,128]{1,0:T(8,128)(2,1)S(1)}, bf16[1024,128]{1,0:T(8,128)(2,1)S(1)}, u32[]{:S(2)}, u32[]{:S(2)}) collective-permute-start(bf16[1024,128]{1,0:T(8,128)(2,1)S(1)} %get-tuple-element.43), channel_id=1, source_target_pairs={{0,1},{1,2},{2,3},{3,4},{4,5},{5,6},{6,7},{7,8},{8,9},{9,10},{10,1... | collective-permute-start | bytes 786440 | tf_op jit(solution)/shard_map/ppermute | solution.py:371
  29.4 1.1 collective-permute-start.5
  30.4 1.2 %tails_first.1 = (bf16[1024,128]{1,0:T(8,128)(2,1)S(1)}, bf16[1024,128]{1,0:T(8,128)(2,1)S(1)}) custom-call(s32[8,384]{1,0:T(8,128)S(1)} %get-tuple-element.36.tab, bf16[321,128,128]{2,1,0:T(8,128)(2,1)S(1)} %get-tuple-element.37.matrix, bf16[65,64,128]{2,1,0:T(8,128)(2,1)S(1)} %get-tuple-element.41.image), custom_call_target="tpu_custom_call" | custom-call | flops 167772160 | bytes 2621440 | tf_op jit(solution)/shard_map/tails_first/pallas_call | solution.py:506
  31.9 2.5 %collective-permute-start.7 = (bf16[1024,128]{1,0:T(8,128)(2,1)S(1)}, bf16[1024,128]{1,0:T(8,128)(2,1)S(1)}, u32[]{:S(2)}, u32[]{:S(2)}) collective-permute-start(bf16[1024,128]{1,0:T(8,128)(2,1)S(1)} %get-tuple-element.48), channel_id=1, source_target_pairs={{0,224},{32,0},{64,32},{96,64},{128,96},{160,128},{192,160},{224,1... | collective-permute-start | bytes 786440 | tf_op jit(solution)/shard_map/ppermute | solution.py:371
  34.4 2.9 %adjoint_first.1 = (f32[64,64,128]{2,1,0:T(8,128)S(1)}, f32[64,128]{1,0:T(8,128)S(1)}, bf16[32,64,128]{2,1,0:T(8,128)(2,1)S(1)}) custom-call(s32[8,384]{1,0:T(8,128)S(1)} %get-tuple-element.36.tab, bf16[321,128,128]{2,1,0:T(8,128)(2,1)S(1)} %get-tuple-element.37.matrix, bf16[65,64,128]{2,1,0:T(8,128)(2,1)S(1)} %get-tuple-element.41.image, ...), custom_call_target="tpu_custom_call" | custom-call | flops 335544320 | bytes 5242880 | tf_op jit(solution)/shard_map/adjoint_first/pallas_call | solution.py:516
  37.4 5.9 %collective-permute-done.5.two = bf16[1024,128]{1,0:T(8,128)(2,1)S(1)} collective-permute-done((bf16[1024,128]{1,0:T(8,128)(2,1)S(1)}, bf16[1024,128]{1,0:T(8,128)(2,1)S(1)}, u32[]{:S(2)}, u32[]{:S(2)}) %collective-permute-start.5) | collective-permute-done | bytes 262176 | tf_op jit(solution)/shard_map/ppermute | solution.py:371
  43.7 0.8 collective-permute-start.8
  44.5 2.4 %inner.1.rows_in = f32[64,64,128]{2,1,0:T(8,128)S(1)} custom-call(s32[8,384]{1,0:T(8,128)S(1)} %get-tuple-element.36.tab, bf16[321,128,128]{2,1,0:T(8,128)(2,1)S(1)} %get-tuple-element.37.matrix, bf16[32,64,128]{2,1,0:T(8,128)(2,1)S(1)} %get-tuple-element.50.middle), custom_call_target="tpu_custom_call" | custom-call | flops 167772160 | bytes 2621440 | tf_op jit(solution)/shard_map/inner/pallas_call | solution.py:527
  46.9 6.6 %collective-permute-done.7.two = bf16[1024,128]{1,0:T(8,128)(2,1)S(1)} collective-permute-done((bf16[1024,128]{1,0:T(8,128)(2,1)S(1)}, bf16[1024,128]{1,0:T(8,128)(2,1)S(1)}, u32[]{:S(2)}, u32[]{:S(2)}) %collective-permute-start.7) | collective-permute-done | bytes 262176 | tf_op jit(solution)/shard_map/ppermute | solution.py:371
  54.1 2.1 %outer.1.rows_in = f32[64,64,128]{2,1,0:T(8,128)S(1)} custom-call(s32[8,384]{1,0:T(8,128)S(1)} %get-tuple-element.36.tab, bf16[321,128,128]{2,1,0:T(8,128)(2,1)S(1)} %get-tuple-element.37.matrix, bf16[1024,128]{1,0:T(8,128)(2,1)S(1)} %get-tuple-element.46.head, bf16[1024,128]{1,0:T(8,128)(2,1)S(1)} %get-tuple-element.52.tail, ...), custom_call_target="tpu_custom_call", output_to_operand_aliasing={{}: (4, {})} | custom-call | flops 167772160 | bytes 2621440 | tf_op jit(solution)/shard_map/outer/pallas_call | solution.py:470
  56.2 3.0 %collective-permute-done.9.lower = bf16[1024,128]{1,0:T(8,128)(2,1)S(1)} collective-permute-done((bf16[1024,128]{1,0:T(8,128)(2,1)S(1)}, bf16[1024,128]{1,0:T(8,128)(2,1)S(1)}, u32[]{:S(2)}, u32[]{:S(2)}) %collective-permute-start.9) | collective-permute-done | bytes 262176 | tf_op jit(solution)/shard_map/ppermute | solution.py:371
  59.1 4.3 %collective-permute-done.8.right = bf16[1024,128]{1,0:T(8,128)(2,1)S(1)} collective-permute-done((bf16[1024,128]{1,0:T(8,128)(2,1)S(1)}, bf16[1024,128]{1,0:T(8,128)(2,1)S(1)}, u32[]{:S(2)}, u32[]{:S(2)}) %collective-permute-start.8) | collective-permute-done | bytes 262176 | tf_op jit(solution)/shard_map/ppermute | solution.py:371
  63.4 1.1 heads_next.1.rows_in
  64.5 1.8 %middle_next.1 = (f32[64,64,128]{2,1,0:T(8,128)S(1)}, bf16[65,64,128]{2,1,0:T(8,128)(2,1)S(1)}, bf16[1024,128]{1,0:T(8,128)(2,1)S(1)}, bf16[1024,128]{1,0:T(8,128)(2,1)S(1)}) custom-call(s32[8,384]{1,0:T(8,128)S(1)} %get-tuple-element.36.tab, bf16[321,128,128]{2,1,0:T(8,128)(2,1)S(1)} %get-tuple-element.37.matrix, ...), custom_call_target="tpu_custom_call", output_to_operand_aliasing={{0}: (2, {})} | custom-call | flops 335544320 | bytes 5242880 | tf_op jit(solution)/shard_map/middle_next/pallas_call | solution.py:491
  66.4 4.2 %collective-permute-start.12 = (bf16[1024,128]{1,0:T(8,128)(2,1)S(1)}, bf16[1024,128]{1,0:T(8,128)(2,1)S(1)}, u32[]{:S(2)}, u32[]{:S(2)}) collective-permute-start(bf16[1024,128]{1,0:T(8,128)(2,1)S(1)} %get-tuple-element.57), channel_id=1, source_target_pairs={{0,1},{1,2},{2,3},{3,4},{4,5},{5,6},{6,7},{7,8},{8,9},{9,10},{10,1... | collective-permute-start | bytes 786440 | tf_op jit(solution)/shard_map/ppermute | solution.py:371
  70.5 0.8 collective-permute-start.13
  71.3 1.2 %tails_next.1 = (bf16[1024,128]{1,0:T(8,128)(2,1)S(1)}, bf16[1024,128]{1,0:T(8,128)(2,1)S(1)}) custom-call(s32[8,384]{1,0:T(8,128)S(1)} %get-tuple-element.36.tab, bf16[321,128,128]{2,1,0:T(8,128)(2,1)S(1)} %get-tuple-element.37.matrix, bf16[65,64,128]{2,1,0:T(8,128)(2,1)S(1)} %get-tuple-element.55.image), custom_call_target="tpu_custom_call" | custom-call | flops 167772160 | bytes 2621440 | tf_op jit(solution)/shard_map/tails_next/pallas_call | solution.py:506
  72.6 3.0 %collective-permute-start.15 = (bf16[1024,128]{1,0:T(8,128)(2,1)S(1)}, bf16[1024,128]{1,0:T(8,128)(2,1)S(1)}, u32[]{:S(2)}, u32[]{:S(2)}) collective-permute-start(bf16[1024,128]{1,0:T(8,128)(2,1)S(1)} %get-tuple-element.60), channel_id=1, source_target_pairs={{0,224},{32,0},{64,32},{96,64},{128,96},{160,128},{192,160},{224,1... | collective-permute-start | bytes 786440 | tf_op jit(solution)/shard_map/ppermute | solution.py:371
  75.6 2.7 %adjoint_next.1 = (f32[64,64,128]{2,1,0:T(8,128)S(1)}, f32[64,128]{1,0:T(8,128)S(1)}) custom-call(s32[8,384]{1,0:T(8,128)S(1)} %get-tuple-element.36.tab, bf16[321,128,128]{2,1,0:T(8,128)(2,1)S(1)} %get-tuple-element.37.matrix, bf16[65,64,128]{2,1,0:T(8,128)(2,1)S(1)} %get-tuple-element.55.image, f32[64,128]{1,0:T(8,128)S(1)} %get-tuple-element.35.weights), custom_call_target="tpu_custom_call" | custom-call | flops 335544320 | bytes 5242880 | tf_op jit(solution)/shard_map/adjoint_next/pallas_call | solution.py:516
  78.8 7.2 %collective-permute-done.13.low1 = bf16[1024,128]{1,0:T(8,128)(2,1)S(1)} collective-permute-done((bf16[1024,128]{1,0:T(8,128)(2,1)S(1)}, bf16[1024,128]{1,0:T(8,128)(2,1)S(1)}, u32[]{:S(2)}, u32[]{:S(2)}) %collective-permute-start.13) | collective-permute-done | bytes 262176 | tf_op jit(solution)/shard_map/ppermute | solution.py:371
  86.0 1.1 collective-permute-done.15.high1
  87.1 0.6 join_last.1
  87.7 23.1 %all_to_all.11 = f32[256,1,128]{2,1,0:T(1,128)S(1)} all-to-all(f32[256,1,128]{2,1,0:T(1,128)S(1)} %bitcast.16), channel_id=1, replica_groups=mesh['layer'=8,'tile'=32] {'layer','tile'}, dimensions={0} | all-to-all | bytes 262144 | tf_op jit(solution)/shard_map/all_to_all | solution.py:567
  110.8 1.3 %write_out.1 = bf16[64,8192]{1,0:T(8,128)(2,1)} custom-call(f32[256,128]{1,0:T(8,128)S(1)} %bitcast.15, f32[64,64,128]{2,1,0:T(8,128)S(1)} %get-tuple-element.64.total), custom_call_target="tpu_custom_call" | custom-call | bytes 3145728 | tf_op jit(solution)/shard_map/write_out/pallas_call | solution.py:568
  (18 shorter events, 1.9 us)
Async XLA Ops:
  1.1 16.5 %collective-permute-start.1 = (bf16[1040,128]{1,0:T(8,128)(2,1)S(1)}, bf16[1040,128]{1,0:T(8,128)(2,1)S(1)}, u32[]{:S(2)}, u32[]{:S(2)}) collective-permute-start(bf16[1040,128]{1,0:T(8,128)(2,1)S(1)} %get-tuple-element.39), channel_id=1, source_target_pairs={{0,224},{32,0},{64,32},{96,64},{128,96},{160,128},{192,160},{224,1... | collective-permute-start | bytes 798728 | tf_op jit(solution)/shard_map/ppermute | solution.py:371
  5.7 18.0 %collective-permute-start = (bf16[1040,128]{1,0:T(8,128)(2,1)S(1)}, bf16[1040,128]{1,0:T(8,128)(2,1)S(1)}, u32[]{:S(2)}, u32[]{:S(2)}) collective-permute-start(bf16[1040,128]{1,0:T(8,128)(2,1)S(1)} %get-tuple-element.39), channel_id=1, source_target_pairs={{0,31},{1,0},{2,1},{3,2},{4,3},{5,4},{6,5},{7,6},{8,7},{9,8},{10,9... | collective-permute-start | bytes 798728 | tf_op jit(solution)/shard_map/ppermute | solution.py:371
  6.6 18.1 %collective-permute-start.3 = (bf16[1040,128]{1,0:T(8,128)(2,1)S(1)}, bf16[1040,128]{1,0:T(8,128)(2,1)S(1)}, u32[]{:S(2)}, u32[]{:S(2)}) collective-permute-start(bf16[1040,128]{1,0:T(8,128)(2,1)S(1)} %get-tuple-element.40), channel_id=1, source_target_pairs={{0,32},{32,64},{64,96},{96,128},{128,160},{160,192},{192,224},{224... | collective-permute-start | bytes 798728 | tf_op jit(solution)/shard_map/ppermute | solution.py:371
  6.6 18.1 %collective-permute-start.2 = (bf16[1040,128]{1,0:T(8,128)(2,1)S(1)}, bf16[1040,128]{1,0:T(8,128)(2,1)S(1)}, u32[]{:S(2)}, u32[]{:S(2)}) collective-permute-start(bf16[1040,128]{1,0:T(8,128)(2,1)S(1)} %get-tuple-element.40), channel_id=1, source_target_pairs={{0,1},{1,2},{2,3},{3,4},{4,5},{5,6},{6,7},{7,8},{8,9},{9,10},{10,1... | collective-permute-start | bytes 798728 | tf_op jit(solution)/shard_map/ppermute | solution.py:371
  26.7 10.7 %collective-permute-start.4 = (bf16[1024,128]{1,0:T(8,128)(2,1)S(1)}, bf16[1024,128]{1,0:T(8,128)(2,1)S(1)}, u32[]{:S(2)}, u32[]{:S(2)}) collective-permute-start(bf16[1024,128]{1,0:T(8,128)(2,1)S(1)} %get-tuple-element.43), channel_id=1, source_target_pairs={{0,1},{1,2},{2,3},{3,4},{4,5},{5,6},{6,7},{7,8},{8,9},{9,10},{10,1... | collective-permute-start | bytes 786440 | tf_op jit(solution)/shard_map/ppermute | solution.py:371
  29.4 13.9 %collective-permute-start.5 = (bf16[1024,128]{1,0:T(8,128)(2,1)S(1)}, bf16[1024,128]{1,0:T(8,128)(2,1)S(1)}, u32[]{:S(2)}, u32[]{:S(2)}) collective-permute-start(bf16[1024,128]{1,0:T(8,128)(2,1)S(1)} %get-tuple-element.44), channel_id=1, source_target_pairs={{0,32},{32,64},{64,96},{96,128},{128,160},{160,192},{192,224},{224... | collective-permute-start | bytes 786440 | tf_op jit(solution)/shard_map/ppermute | solution.py:371
  31.7 15.2 %collective-permute-start.6 = (bf16[1024,128]{1,0:T(8,128)(2,1)S(1)}, bf16[1024,128]{1,0:T(8,128)(2,1)S(1)}, u32[]{:S(2)}, u32[]{:S(2)}) collective-permute-start(bf16[1024,128]{1,0:T(8,128)(2,1)S(1)} %get-tuple-element.47), channel_id=1, source_target_pairs={{0,31},{1,0},{2,1},{3,2},{4,3},{5,4},{6,5},{7,6},{8,7},{9,8},{10,9... | collective-permute-start | bytes 786440 | tf_op jit(solution)/shard_map/ppermute | solution.py:371
  31.9 21.6 %collective-permute-start.7 = (bf16[1024,128]{1,0:T(8,128)(2,1)S(1)}, bf16[1024,128]{1,0:T(8,128)(2,1)S(1)}, u32[]{:S(2)}, u32[]{:S(2)}) collective-permute-start(bf16[1024,128]{1,0:T(8,128)(2,1)S(1)} %get-tuple-element.48), channel_id=1, source_target_pairs={{0,224},{32,0},{64,32},{96,64},{128,96},{160,128},{192,160},{224,1... | collective-permute-start | bytes 786440 | tf_op jit(solution)/shard_map/ppermute | solution.py:371
  43.4 15.7 %collective-permute-start.9 = (bf16[1024,128]{1,0:T(8,128)(2,1)S(1)}, bf16[1024,128]{1,0:T(8,128)(2,1)S(1)}, u32[]{:S(2)}, u32[]{:S(2)}) collective-permute-start(bf16[1024,128]{1,0:T(8,128)(2,1)S(1)} %get-tuple-element.46.head), channel_id=1, source_target_pairs={{0,224},{32,0},{64,32},{96,64},{128,96},{160,128},{192,160},{224,1... | collective-permute-start | bytes 786440 | tf_op jit(solution)/shard_map/ppermute | solution.py:371
  43.7 19.7 %collective-permute-start.8 = (bf16[1024,128]{1,0:T(8,128)(2,1)S(1)}, bf16[1024,128]{1,0:T(8,128)(2,1)S(1)}, u32[]{:S(2)}, u32[]{:S(2)}) collective-permute-start(bf16[1024,128]{1,0:T(8,128)(2,1)S(1)} %get-tuple-element.46.head), channel_id=1, source_target_pairs={{0,31},{1,0},{2,1},{3,2},{4,3},{5,4},{6,5},{7,6},{8,7},{9,8},{10,9... | collective-permute-start | bytes 786440 | tf_op jit(solution)/shard_map/ppermute | solution.py:371
  53.7 10.8 %collective-permute-start.11 = (bf16[1024,128]{1,0:T(8,128)(2,1)S(1)}, bf16[1024,128]{1,0:T(8,128)(2,1)S(1)}, u32[]{:S(2)}, u32[]{:S(2)}) collective-permute-start(bf16[1024,128]{1,0:T(8,128)(2,1)S(1)} %get-tuple-element.52.tail), channel_id=1, source_target_pairs={{0,32},{32,64},{64,96},{96,128},{128,160},{160,192},{192,224},{224... | collective-permute-start | bytes 786440 | tf_op jit(solution)/shard_map/ppermute | solution.py:371
  53.8 10.7 %collective-permute-start.10 = (bf16[1024,128]{1,0:T(8,128)(2,1)S(1)}, bf16[1024,128]{1,0:T(8,128)(2,1)S(1)}, u32[]{:S(2)}, u32[]{:S(2)}) collective-permute-start(bf16[1024,128]{1,0:T(8,128)(2,1)S(1)} %get-tuple-element.52.tail), channel_id=1, source_target_pairs={{0,1},{1,2},{2,3},{3,4},{4,5},{5,6},{6,7},{7,8},{8,9},{9,10},{10,1... | collective-permute-start | bytes 786440 | tf_op jit(solution)/shard_map/ppermute | solution.py:371
  66.4 12.4 %collective-permute-start.12 = (bf16[1024,128]{1,0:T(8,128)(2,1)S(1)}, bf16[1024,128]{1,0:T(8,128)(2,1)S(1)}, u32[]{:S(2)}, u32[]{:S(2)}) collective-permute-start(bf16[1024,128]{1,0:T(8,128)(2,1)S(1)} %get-tuple-element.57), channel_id=1, source_target_pairs={{0,1},{1,2},{2,3},{3,4},{4,5},{5,6},{6,7},{7,8},{8,9},{9,10},{10,1... | collective-permute-start | bytes 786440 | tf_op jit(solution)/shard_map/ppermute | solution.py:371
  70.5 15.4 %collective-permute-start.13 = (bf16[1024,128]{1,0:T(8,128)(2,1)S(1)}, bf16[1024,128]{1,0:T(8,128)(2,1)S(1)}, u32[]{:S(2)}, u32[]{:S(2)}) collective-permute-start(bf16[1024,128]{1,0:T(8,128)(2,1)S(1)} %get-tuple-element.58), channel_id=1, source_target_pairs={{0,32},{32,64},{64,96},{96,128},{128,160},{160,192},{192,224},{224... | collective-permute-start | bytes 786440 | tf_op jit(solution)/shard_map/ppermute | solution.py:371
  72.5 13.4 %collective-permute-start.14 = (bf16[1024,128]{1,0:T(8,128)(2,1)S(1)}, bf16[1024,128]{1,0:T(8,128)(2,1)S(1)}, u32[]{:S(2)}, u32[]{:S(2)}) collective-permute-start(bf16[1024,128]{1,0:T(8,128)(2,1)S(1)} %get-tuple-element.59), channel_id=1, source_target_pairs={{0,31},{1,0},{2,1},{3,2},{4,3},{5,4},{6,5},{7,6},{8,7},{9,8},{10,9... | collective-permute-start | bytes 786440 | tf_op jit(solution)/shard_map/ppermute | solution.py:371
  72.6 14.4 %collective-permute-start.15 = (bf16[1024,128]{1,0:T(8,128)(2,1)S(1)}, bf16[1024,128]{1,0:T(8,128)(2,1)S(1)}, u32[]{:S(2)}, u32[]{:S(2)}) collective-permute-start(bf16[1024,128]{1,0:T(8,128)(2,1)S(1)} %get-tuple-element.60), channel_id=1, source_target_pairs={{0,224},{32,0},{64,32},{96,64},{128,96},{160,128},{192,160},{224,1... | collective-permute-start | bytes 786440 | tf_op jit(solution)/shard_map/ppermute | solution.py:371

commit v6 on v4

--- a/solution.py
+++ b/solution.py
@@ -252,7 +252,7 @@
         rows, image, inverse = rest[:3]
     else:
         inverse, rows, image = rest[:3]
-    right_back, lower_back, source, total = rest[3:]
+    lower_back, right_back, source, total = rest[3:]
     num_blocks = rows.shape[0]
     vectors = image.shape[1]
     load_rims(first, (left, upper), source)
@@ -274,7 +274,7 @@
     send_back(total, (right_back, lower_back))
 
 
-def tails_kernel(tab, matrix, image, left_back, upper_back, total):
+def tails_kernel(tab, matrix, image, upper_back, left_back, total):
     clear(total)
     pair_loop(ADJOINT_TAILS, tab, image, matrix, total)
     send_back(total, (left_back, upper_back))
@@ -491,9 +491,9 @@
         image = result[1]
         if first:
             inverse = result[2]
-        right, lower = result[-2:]
-        lows = (shift(right, "tile", 1), shift(lower, "layer", 1))
-        left, upper = call(
+        lower, right = result[-2:]
+        lows = (shift(lower, "layer", 1), shift(right, "tile", 1))
+        upper, left = call(
             tails_kernel,
             "tails" + suffix,
             [rim_type] * 2,
@@ -502,7 +502,7 @@
             work // 2,
             blocks.size // 2,
         )(tab, matrix, image)
-        highs = (shift(left, "tile", -1), shift(upper, "layer", -1))
+        highs = (shift(upper, "layer", -1), shift(left, "tile", -1))
         result = call(
             adjoint_kernel,
             "adjoint" + suffix,

time: 113 us -> 113 us (level)
  waiting for transfers between devices: 32.1 us -> 23.6 us
  Pallas kernels: 25.1 us -> 32.6 us
  starting transfers between devices: 29.9 us -> 32.2 us
    ppermute x16, waiting for transfers between devices: 32.1 us -> 23.6 us  [shift(): lax.ppermute(x, axis, [(i, (i + step) % count) for i in range(count)])]
    ppermute x16, starting transfers between devices: 29.9 us -> 32.2 us  [shift(): lax.ppermute(x, axis, [(i, (i + step) % count) for i in range(count)])]
    pallas_call x2, Pallas kernels: 2.64 us -> 4.69 us  [local(): call(functools.partial(middle_kernel, first), 'middle' + suffix, [rows_ty...]
    pallas_call x2, Pallas kernels: 1.57 us -> 3.52 us  [local(): call(functools.partial(heads_kernel, first), 'heads' + suffix, [rows_type...]
    pallas_call x1, Pallas kernels: 6.97 us -> 8.66 us  [local(): call(first_kernel, 'own_first', [VM((slots + 1, size, size), bf16), tall_...]
  transfers between devices with their start and end apart: 16 -> 16, of which waited for: 9 -> 7; matrix products, arithmetic and copies ran while one was open for 0% -> 0% of each run, Pallas kernels for 17% -> 22%
where the time goes in v6:
time: 113 us; the launch traced here: 114 us
  Pallas kernels  32.6 us (29%)
  starting transfers between devices  32.2 us (28%)
  blocking collectives  24.1 us (21%)
  waiting for transfers between devices  23.6 us (21%)
    ppermute x16, starting transfers between devices, shift(): lax.ppermute(x, axis, [(i, (i + step) % count) for i in range(count)])  32.2 us
    all_to_all x1, blocking collectives, local(): sums = lax.all_to_all(message, ('layer', 'tile'), 0, 0, tiled=True)  24.1 us
    ppermute x16, waiting for transfers between devices, shift(): lax.ppermute(x, axis, [(i, (i + step) % count) for i in range(count)])  23.6 us
    pallas_call x1, Pallas kernels, local(): call(first_kernel, 'own_first', [VM((slots + 1, size, size), bf16), tall_...  8.66 us
    pallas_call x2, Pallas kernels, local(): call(adjoint_kernel, 'adjoint' + suffix, [block_f32, norm_type] + ([middl...  6.09 us
    pallas_call x2, Pallas kernels, local(): call(functools.partial(middle_kernel, first), 'middle' + suffix, [rows_ty...  4.69 us
    pallas_call x1, Pallas kernels, local(): call(own_kernel, 'own_next', [block_f32], [SMEM_SPEC] + [VMEM_SPEC] * 4,...  3.62 us
    pallas_call x2, Pallas kernels, local(): call(functools.partial(heads_kernel, first), 'heads' + suffix, [rows_type...  3.52 us
  transfers between devices with their start and end apart: 16, of which 7 were waited for; matrix products, arithmetic and copies ran while one was open for 0% of the time, Pallas kernels for 22%

profile of v6, /device:TPU:1, one launch (start us, length us, event | category | flops | bytes accessed | tf_op | source)
XLA Modules:
  0.0 113.5 jit_solution(10308154069535716796)
XLA Ops:
  0.0 1.1 edges.1
  1.1 4.6 %collective-permute-start.1 = (bf16[1040,128]{1,0:T(8,128)(2,1)S(1)}, bf16[1040,128]{1,0:T(8,128)(2,1)S(1)}, u32[]{:S(2)}, u32[]{:S(2)}) collective-permute-start(bf16[1040,128]{1,0:T(8,128)(2,1)S(1)} %get-tuple-element.37), channel_id=1, source_target_pairs={{0,224},{32,0},{64,32},{96,64},{128,96},{160,128},{192,160},{224,1... | collective-permute-start | bytes 798728 | tf_op jit(solution)/shard_map/ppermute | solution.py:362
  5.7 1.0 collective-permute-start
  6.6 2.3 %collective-permute-start.2 = (bf16[1040,128]{1,0:T(8,128)(2,1)S(1)}, bf16[1040,128]{1,0:T(8,128)(2,1)S(1)}, u32[]{:S(2)}, u32[]{:S(2)}) collective-permute-start(bf16[1040,128]{1,0:T(8,128)(2,1)S(1)} %get-tuple-element.38), channel_id=1, source_target_pairs={{0,1},{1,2},{2,3},{3,4},{4,5},{5,6},{6,7},{7,8},{8,9},{9,10},{10,1... | collective-permute-start | bytes 798728 | tf_op jit(solution)/shard_map/ppermute | solution.py:362
  9.7 8.7 %own_first.1 = (bf16[321,128,128]{2,1,0:T(8,128)(2,1)S(1)}, f32[64,80,128]{2,1,0:T(8,128)S(1)}, s32[8,384]{1,0:T(8,128)S(1)}) custom-call(s32[3]{0:T(128)S(1)} %pad_add_fusion.count, bf16[320,128,128]{2,1,0:T(8,128)(2,1)} %bitcast.17, bf16[64,8192]{1,0:T(8,128)(2,1)} %bitcast.19, s32[1,320]{1,0:T(1,128)} %bitcast.21, s32[1,320]{1,0:T(1,128)} %bitcast.22, ...), custom_call_target="tpu_custom_call" | custom-call | flops 671088640 | bytes 20971520 | tf_op jit(solution)/shard_map/own_first/pallas_call | solution.py:429
  18.4 5.3 %collective-permute-done.right = bf16[1040,128]{1,0:T(8,128)(2,1)S(1)} collective-permute-done((bf16[1040,128]{1,0:T(8,128)(2,1)S(1)}, bf16[1040,128]{1,0:T(8,128)(2,1)S(1)}, u32[]{:S(2)}, u32[]{:S(2)}) %collective-permute-start) | collective-permute-done | bytes 266272 | tf_op jit(solution)/shard_map/ppermute | solution.py:362
  23.6 1.8 %heads_first.1.rows_in = f32[64,80,128]{2,1,0:T(8,128)S(1)} custom-call(s32[8,384]{1,0:T(8,128)S(1)} %get-tuple-element.34.tab, bf16[321,128,128]{2,1,0:T(8,128)(2,1)S(1)} %get-tuple-element.35.matrix, f32[64,80,128]{2,1,0:T(8,128)S(1)} %get-tuple-element.36.rows_in, ...), custom_call_target="tpu_custom_call", output_to_operand_aliasing={{}: (2, {})} | custom-call | flops 167772160 | bytes 2621440 | tf_op jit(solution)/shard_map/heads_first/pallas_call | solution.py:470
  25.4 2.4 %middle_first.1 = (f32[64,80,128]{2,1,0:T(8,128)S(1)}, bf16[65,64,128]{2,1,0:T(8,128)(2,1)S(1)}, f32[64,8,128]{2,1,0:T(8,128)S(1)}, bf16[1024,128]{1,0:T(8,128)(2,1)S(1)}, bf16[1024,128]{1,0:T(8,128)(2,1)S(1)}) custom-call(s32[8,384]{1,0:T(8,128)S(1)} %get-tuple-element.34.tab, ...), custom_call_target="tpu_custom_call", output_to_operand_aliasing={{0}: (2, {})} | custom-call | flops 335544320 | bytes 5242880 | tf_op jit(solution)/shard_map/middle_first/pallas_call | solution.py:481
  27.9 3.1 %collective-permute-start.5 = (bf16[1024,128]{1,0:T(8,128)(2,1)S(1)}, bf16[1024,128]{1,0:T(8,128)(2,1)S(1)}, u32[]{:S(2)}, u32[]{:S(2)}) collective-permute-start(bf16[1024,128]{1,0:T(8,128)(2,1)S(1)} %get-tuple-element.42), channel_id=1, source_target_pairs={{0,1},{1,2},{2,3},{3,4},{4,5},{5,6},{6,7},{7,8},{8,9},{9,10},{10,1... | collective-permute-start | bytes 786440 | tf_op jit(solution)/shard_map/ppermute | solution.py:362
  31.1 1.3 %tails_first.1 = (bf16[1024,128]{1,0:T(8,128)(2,1)S(1)}, bf16[1024,128]{1,0:T(8,128)(2,1)S(1)}) custom-call(s32[8,384]{1,0:T(8,128)S(1)} %get-tuple-element.34.tab, bf16[321,128,128]{2,1,0:T(8,128)(2,1)S(1)} %get-tuple-element.35.matrix, bf16[65,64,128]{2,1,0:T(8,128)(2,1)S(1)} %get-tuple-element.39.image), custom_call_target="tpu_custom_call" | custom-call | flops 167772160 | bytes 2621440 | tf_op jit(solution)/shard_map/tails_first/pallas_call | solution.py:496
  32.4 2.0 %collective-permute-start.6 = (bf16[1024,128]{1,0:T(8,128)(2,1)S(1)}, bf16[1024,128]{1,0:T(8,128)(2,1)S(1)}, u32[]{:S(2)}, u32[]{:S(2)}) collective-permute-start(bf16[1024,128]{1,0:T(8,128)(2,1)S(1)} %get-tuple-element.46), channel_id=1, source_target_pairs={{0,224},{32,0},{64,32},{96,64},{128,96},{160,128},{192,160},{224,1... | collective-permute-start | bytes 786440 | tf_op jit(solution)/shard_map/ppermute | solution.py:362
  34.4 3.1 %adjoint_first.1 = (f32[64,64,128]{2,1,0:T(8,128)S(1)}, f32[64,128]{1,0:T(8,128)S(1)}, bf16[32,64,128]{2,1,0:T(8,128)(2,1)S(1)}) custom-call(s32[8,384]{1,0:T(8,128)S(1)} %get-tuple-element.34.tab, bf16[321,128,128]{2,1,0:T(8,128)(2,1)S(1)} %get-tuple-element.35.matrix, bf16[65,64,128]{2,1,0:T(8,128)(2,1)S(1)} %get-tuple-element.39.image, ...), custom_call_target="tpu_custom_call" | custom-call | flops 335544320 | bytes 5242880 | tf_op jit(solution)/shard_map/adjoint_first/pallas_call | solution.py:506
  37.5 0.8 collective-permute-done.4.one
  38.3 0.2 join_head.1
  38.5 10.6 %collective-permute-start.9 = (bf16[1024,128]{1,0:T(8,128)(2,1)S(1)}, bf16[1024,128]{1,0:T(8,128)(2,1)S(1)}, u32[]{:S(2)}, u32[]{:S(2)}) collective-permute-start(bf16[1024,128]{1,0:T(8,128)(2,1)S(1)} %get-tuple-element.44.head), channel_id=1, source_target_pairs={{0,224},{32,0},{64,32},{96,64},{128,96},{160,128},{192,160},{224,1... | collective-permute-start | bytes 786440 | tf_op jit(solution)/shard_map/ppermute | solution.py:362
  49.1 1.2 %collective-permute-done.7.two = bf16[1024,128]{1,0:T(8,128)(2,1)S(1)} collective-permute-done((bf16[1024,128]{1,0:T(8,128)(2,1)S(1)}, bf16[1024,128]{1,0:T(8,128)(2,1)S(1)}, u32[]{:S(2)}, u32[]{:S(2)}) %collective-permute-start.7) | collective-permute-done | bytes 262176 | tf_op jit(solution)/shard_map/ppermute | solution.py:362
  50.3 0.2 join_tail.1
  50.6 3.7 %collective-permute-start.10 = (bf16[1024,128]{1,0:T(8,128)(2,1)S(1)}, bf16[1024,128]{1,0:T(8,128)(2,1)S(1)}, u32[]{:S(2)}, u32[]{:S(2)}) collective-permute-start(bf16[1024,128]{1,0:T(8,128)(2,1)S(1)} %get-tuple-element.49.tail), channel_id=1, source_target_pairs={{0,1},{1,2},{2,3},{3,4},{4,5},{5,6},{6,7},{7,8},{8,9},{9,10},{10,1... | collective-permute-start | bytes 786440 | tf_op jit(solution)/shard_map/ppermute | solution.py:362
  54.3 3.6 %own_next.1.rows_in = f32[64,64,128]{2,1,0:T(8,128)S(1)} custom-call(s32[8,384]{1,0:T(8,128)S(1)} %get-tuple-element.34.tab, bf16[321,128,128]{2,1,0:T(8,128)(2,1)S(1)} %get-tuple-element.35.matrix, bf16[1024,128]{1,0:T(8,128)(2,1)S(1)} %get-tuple-element.44.head, bf16[32,64,128]{2,1,0:T(8,128)(2,1)S(1)} %get-tuple-element.45.middle, ...), custom_call_target="tpu_custom_call" | custom-call | flops 335544320 | bytes 5242880 | tf_op jit(solution)/shard_map/own_next/pallas_call | solution.py:461
  57.9 8.5 %collective-permute-done.8.right = bf16[1024,128]{1,0:T(8,128)(2,1)S(1)} collective-permute-done((bf16[1024,128]{1,0:T(8,128)(2,1)S(1)}, bf16[1024,128]{1,0:T(8,128)(2,1)S(1)}, u32[]{:S(2)}, u32[]{:S(2)}) %collective-permute-start.8) | collective-permute-done | bytes 262176 | tf_op jit(solution)/shard_map/ppermute | solution.py:362
  66.4 1.8 %heads_next.1.rows_in = f32[64,64,128]{2,1,0:T(8,128)S(1)} custom-call(s32[8,384]{1,0:T(8,128)S(1)} %get-tuple-element.34.tab, bf16[321,128,128]{2,1,0:T(8,128)(2,1)S(1)} %get-tuple-element.35.matrix, f32[64,64,128]{2,1,0:T(8,128)S(1)} %own_next.1.rows_in, bf16[1024,128]{1,0:T(8,128)(2,1)S(1)} %collective-permute-done.8.right, ...), custom_call_target="tpu_custom_call", output_to_operand_aliasing={{}: (2, {})} | custom-call | flops 167772160 | bytes 2621440 | tf_op jit(solution)/shard_map/heads_next/pallas_call | solution.py:470
  68.2 2.3 %middle_next.1 = (f32[64,64,128]{2,1,0:T(8,128)S(1)}, bf16[65,64,128]{2,1,0:T(8,128)(2,1)S(1)}, bf16[1024,128]{1,0:T(8,128)(2,1)S(1)}, bf16[1024,128]{1,0:T(8,128)(2,1)S(1)}) custom-call(s32[8,384]{1,0:T(8,128)S(1)} %get-tuple-element.34.tab, bf16[321,128,128]{2,1,0:T(8,128)(2,1)S(1)} %get-tuple-element.35.matrix, ...), custom_call_target="tpu_custom_call", output_to_operand_aliasing={{0}: (2, {})} | custom-call | flops 335544320 | bytes 5242880 | tf_op jit(solution)/shard_map/middle_next/pallas_call | solution.py:481
  70.6 3.4 %collective-permute-start.13 = (bf16[1024,128]{1,0:T(8,128)(2,1)S(1)}, bf16[1024,128]{1,0:T(8,128)(2,1)S(1)}, u32[]{:S(2)}, u32[]{:S(2)}) collective-permute-start(bf16[1024,128]{1,0:T(8,128)(2,1)S(1)} %get-tuple-element.54), channel_id=1, source_target_pairs={{0,1},{1,2},{2,3},{3,4},{4,5},{5,6},{6,7},{7,8},{8,9},{9,10},{10,1... | collective-permute-start | bytes 786440 | tf_op jit(solution)/shard_map/ppermute | solution.py:362
  74.0 1.3 %tails_next.1 = (bf16[1024,128]{1,0:T(8,128)(2,1)S(1)}, bf16[1024,128]{1,0:T(8,128)(2,1)S(1)}) custom-call(s32[8,384]{1,0:T(8,128)S(1)} %get-tuple-element.34.tab, bf16[321,128,128]{2,1,0:T(8,128)(2,1)S(1)} %get-tuple-element.35.matrix, bf16[65,64,128]{2,1,0:T(8,128)(2,1)S(1)} %get-tuple-element.51.image), custom_call_target="tpu_custom_call" | custom-call | flops 167772160 | bytes 2621440 | tf_op jit(solution)/shard_map/tails_next/pallas_call | solution.py:496
  75.3 1.2 %collective-permute-start.14 = (bf16[1024,128]{1,0:T(8,128)(2,1)S(1)}, bf16[1024,128]{1,0:T(8,128)(2,1)S(1)}, u32[]{:S(2)}, u32[]{:S(2)}) collective-permute-start(bf16[1024,128]{1,0:T(8,128)(2,1)S(1)} %get-tuple-element.55), channel_id=1, source_target_pairs={{0,224},{32,0},{64,32},{96,64},{128,96},{160,128},{192,160},{224,1... | collective-permute-start | bytes 786440 | tf_op jit(solution)/shard_map/ppermute | solution.py:362
  76.5 3.0 %adjoint_next.1 = (f32[64,64,128]{2,1,0:T(8,128)S(1)}, f32[64,128]{1,0:T(8,128)S(1)}) custom-call(s32[8,384]{1,0:T(8,128)S(1)} %get-tuple-element.34.tab, bf16[321,128,128]{2,1,0:T(8,128)(2,1)S(1)} %get-tuple-element.35.matrix, bf16[65,64,128]{2,1,0:T(8,128)(2,1)S(1)} %get-tuple-element.51.image, f32[64,128]{1,0:T(8,128)S(1)} %get-tuple-element.33.weights), custom_call_target="tpu_custom_call" | custom-call | flops 335544320 | bytes 5242880 | tf_op jit(solution)/shard_map/adjoint_next/pallas_call | solution.py:506
  79.6 2.4 %collective-permute-done.12.low0 = bf16[1024,128]{1,0:T(8,128)(2,1)S(1)} collective-permute-done((bf16[1024,128]{1,0:T(8,128)(2,1)S(1)}, bf16[1024,128]{1,0:T(8,128)(2,1)S(1)}, u32[]{:S(2)}, u32[]{:S(2)}) %collective-permute-start.12) | collective-permute-done | bytes 262176 | tf_op jit(solution)/shard_map/ppermute | solution.py:362
  82.0 3.7 %collective-permute-done.14.high0 = bf16[1024,128]{1,0:T(8,128)(2,1)S(1)} collective-permute-done((bf16[1024,128]{1,0:T(8,128)(2,1)S(1)}, bf16[1024,128]{1,0:T(8,128)(2,1)S(1)}, u32[]{:S(2)}, u32[]{:S(2)}) %collective-permute-start.14) | collective-permute-done | bytes 262176 | tf_op jit(solution)/shard_map/ppermute | solution.py:362
  85.7 1.7 %collective-permute-done.15.high1 = bf16[1024,128]{1,0:T(8,128)(2,1)S(1)} collective-permute-done((bf16[1024,128]{1,0:T(8,128)(2,1)S(1)}, bf16[1024,128]{1,0:T(8,128)(2,1)S(1)}, u32[]{:S(2)}, u32[]{:S(2)}) %collective-permute-start.15) | collective-permute-done | bytes 262176 | tf_op jit(solution)/shard_map/ppermute | solution.py:362
  87.4 0.6 join_last.1
  88.0 24.1 %all_to_all.11 = f32[256,1,128]{2,1,0:T(1,128)S(1)} all-to-all(f32[256,1,128]{2,1,0:T(1,128)S(1)} %bitcast.16), channel_id=1, replica_groups=mesh['layer'=8,'tile'=32] {'layer','tile'}, dimensions={0} | all-to-all | bytes 262144 | tf_op jit(solution)/shard_map/all_to_all | solution.py:548
  112.2 1.3 %write_out.1 = bf16[64,8192]{1,0:T(8,128)(2,1)} custom-call(f32[256,128]{1,0:T(8,128)S(1)} %bitcast.15, f32[64,64,128]{2,1,0:T(8,128)S(1)} %get-tuple-element.60.total), custom_call_target="tpu_custom_call" | custom-call | bytes 3145728 | tf_op jit(solution)/shard_map/write_out/pallas_call | solution.py:549
  (17 shorter events, 0.4 us)
Async XLA Ops:
  1.1 17.3 %collective-permute-start.1 = (bf16[1040,128]{1,0:T(8,128)(2,1)S(1)}, bf16[1040,128]{1,0:T(8,128)(2,1)S(1)}, u32[]{:S(2)}, u32[]{:S(2)}) collective-permute-start(bf16[1040,128]{1,0:T(8,128)(2,1)S(1)} %get-tuple-element.37), channel_id=1, source_target_pairs={{0,224},{32,0},{64,32},{96,64},{128,96},{160,128},{192,160},{224,1... | collective-permute-start | bytes 798728 | tf_op jit(solution)/shard_map/ppermute | solution.py:362
  5.7 18.0 %collective-permute-start = (bf16[1040,128]{1,0:T(8,128)(2,1)S(1)}, bf16[1040,128]{1,0:T(8,128)(2,1)S(1)}, u32[]{:S(2)}, u32[]{:S(2)}) collective-permute-start(bf16[1040,128]{1,0:T(8,128)(2,1)S(1)} %get-tuple-element.37), channel_id=1, source_target_pairs={{0,31},{1,0},{2,1},{3,2},{4,3},{5,4},{6,5},{7,6},{8,7},{9,8},{10,9... | collective-permute-start | bytes 798728 | tf_op jit(solution)/shard_map/ppermute | solution.py:362
  6.6 18.8 %collective-permute-start.3 = (bf16[1040,128]{1,0:T(8,128)(2,1)S(1)}, bf16[1040,128]{1,0:T(8,128)(2,1)S(1)}, u32[]{:S(2)}, u32[]{:S(2)}) collective-permute-start(bf16[1040,128]{1,0:T(8,128)(2,1)S(1)} %get-tuple-element.38), channel_id=1, source_target_pairs={{0,32},{32,64},{64,96},{96,128},{128,160},{160,192},{192,224},{224... | collective-permute-start | bytes 798728 | tf_op jit(solution)/shard_map/ppermute | solution.py:362
  6.6 18.8 %collective-permute-start.2 = (bf16[1040,128]{1,0:T(8,128)(2,1)S(1)}, bf16[1040,128]{1,0:T(8,128)(2,1)S(1)}, u32[]{:S(2)}, u32[]{:S(2)}) collective-permute-start(bf16[1040,128]{1,0:T(8,128)(2,1)S(1)} %get-tuple-element.38), channel_id=1, source_target_pairs={{0,1},{1,2},{2,3},{3,4},{4,5},{5,6},{6,7},{7,8},{8,9},{9,10},{10,1... | collective-permute-start | bytes 798728 | tf_op jit(solution)/shard_map/ppermute | solution.py:362
  27.8 10.5 %collective-permute-start.4 = (bf16[1024,128]{1,0:T(8,128)(2,1)S(1)}, bf16[1024,128]{1,0:T(8,128)(2,1)S(1)}, u32[]{:S(2)}, u32[]{:S(2)}) collective-permute-start(bf16[1024,128]{1,0:T(8,128)(2,1)S(1)} %get-tuple-element.41), channel_id=1, source_target_pairs={{0,32},{32,64},{64,96},{96,128},{128,160},{160,192},{192,224},{224... | collective-permute-start | bytes 786440 | tf_op jit(solution)/shard_map/ppermute | solution.py:362
  27.9 10.4 %collective-permute-start.5 = (bf16[1024,128]{1,0:T(8,128)(2,1)S(1)}, bf16[1024,128]{1,0:T(8,128)(2,1)S(1)}, u32[]{:S(2)}, u32[]{:S(2)}) collective-permute-start(bf16[1024,128]{1,0:T(8,128)(2,1)S(1)} %get-tuple-element.42), channel_id=1, source_target_pairs={{0,1},{1,2},{2,3},{3,4},{4,5},{5,6},{6,7},{7,8},{8,9},{9,10},{10,1... | collective-permute-start | bytes 786440 | tf_op jit(solution)/shard_map/ppermute | solution.py:362
  32.4 16.7 %collective-permute-start.6 = (bf16[1024,128]{1,0:T(8,128)(2,1)S(1)}, bf16[1024,128]{1,0:T(8,128)(2,1)S(1)}, u32[]{:S(2)}, u32[]{:S(2)}) collective-permute-start(bf16[1024,128]{1,0:T(8,128)(2,1)S(1)} %get-tuple-element.46), channel_id=1, source_target_pairs={{0,224},{32,0},{64,32},{96,64},{128,96},{160,128},{192,160},{224,1... | collective-permute-start | bytes 786440 | tf_op jit(solution)/shard_map/ppermute | solution.py:362
  34.4 15.9 %collective-permute-start.7 = (bf16[1024,128]{1,0:T(8,128)(2,1)S(1)}, bf16[1024,128]{1,0:T(8,128)(2,1)S(1)}, u32[]{:S(2)}, u32[]{:S(2)}) collective-permute-start(bf16[1024,128]{1,0:T(8,128)(2,1)S(1)} %get-tuple-element.47), channel_id=1, source_target_pairs={{0,31},{1,0},{2,1},{3,2},{4,3},{5,4},{6,5},{7,6},{8,7},{9,8},{10,9... | collective-permute-start | bytes 786440 | tf_op jit(solution)/shard_map/ppermute | solution.py:362
  38.5 19.4 %collective-permute-start.9 = (bf16[1024,128]{1,0:T(8,128)(2,1)S(1)}, bf16[1024,128]{1,0:T(8,128)(2,1)S(1)}, u32[]{:S(2)}, u32[]{:S(2)}) collective-permute-start(bf16[1024,128]{1,0:T(8,128)(2,1)S(1)} %get-tuple-element.44.head), channel_id=1, source_target_pairs={{0,224},{32,0},{64,32},{96,64},{128,96},{160,128},{192,160},{224,1... | collective-permute-start | bytes 786440 | tf_op jit(solution)/shard_map/ppermute | solution.py:362
  49.1 17.3 %collective-permute-start.8 = (bf16[1024,128]{1,0:T(8,128)(2,1)S(1)}, bf16[1024,128]{1,0:T(8,128)(2,1)S(1)}, u32[]{:S(2)}, u32[]{:S(2)}) collective-permute-start(bf16[1024,128]{1,0:T(8,128)(2,1)S(1)} %get-tuple-element.44.head), channel_id=1, source_target_pairs={{0,31},{1,0},{2,1},{3,2},{4,3},{5,4},{6,5},{7,6},{8,7},{9,8},{10,9... | collective-permute-start | bytes 786440 | tf_op jit(solution)/shard_map/ppermute | solution.py:362
  50.5 17.7 %collective-permute-start.11 = (bf16[1024,128]{1,0:T(8,128)(2,1)S(1)}, bf16[1024,128]{1,0:T(8,128)(2,1)S(1)}, u32[]{:S(2)}, u32[]{:S(2)}) collective-permute-start(bf16[1024,128]{1,0:T(8,128)(2,1)S(1)} %get-tuple-element.49.tail), channel_id=1, source_target_pairs={{0,32},{32,64},{64,96},{96,128},{128,160},{160,192},{192,224},{224... | collective-permute-start | bytes 786440 | tf_op jit(solution)/shard_map/ppermute | solution.py:362
  50.6 17.6 %collective-permute-start.10 = (bf16[1024,128]{1,0:T(8,128)(2,1)S(1)}, bf16[1024,128]{1,0:T(8,128)(2,1)S(1)}, u32[]{:S(2)}, u32[]{:S(2)}) collective-permute-start(bf16[1024,128]{1,0:T(8,128)(2,1)S(1)} %get-tuple-element.49.tail), channel_id=1, source_target_pairs={{0,1},{1,2},{2,3},{3,4},{4,5},{5,6},{6,7},{7,8},{8,9},{9,10},{10,1... | collective-permute-start | bytes 786440 | tf_op jit(solution)/shard_map/ppermute | solution.py:362
  70.5 11.5 %collective-permute-start.12 = (bf16[1024,128]{1,0:T(8,128)(2,1)S(1)}, bf16[1024,128]{1,0:T(8,128)(2,1)S(1)}, u32[]{:S(2)}, u32[]{:S(2)}) collective-permute-start(bf16[1024,128]{1,0:T(8,128)(2,1)S(1)} %get-tuple-element.53), channel_id=1, source_target_pairs={{0,32},{32,64},{64,96},{96,128},{128,160},{160,192},{192,224},{224... | collective-permute-start | bytes 786440 | tf_op jit(solution)/shard_map/ppermute | solution.py:362
  70.6 11.5 %collective-permute-start.13 = (bf16[1024,128]{1,0:T(8,128)(2,1)S(1)}, bf16[1024,128]{1,0:T(8,128)(2,1)S(1)}, u32[]{:S(2)}, u32[]{:S(2)}) collective-permute-start(bf16[1024,128]{1,0:T(8,128)(2,1)S(1)} %get-tuple-element.54), channel_id=1, source_target_pairs={{0,1},{1,2},{2,3},{3,4},{4,5},{5,6},{6,7},{7,8},{8,9},{9,10},{10,1... | collective-permute-start | bytes 786440 | tf_op jit(solution)/shard_map/ppermute | solution.py:362
  75.3 10.4 %collective-permute-start.14 = (bf16[1024,128]{1,0:T(8,128)(2,1)S(1)}, bf16[1024,128]{1,0:T(8,128)(2,1)S(1)}, u32[]{:S(2)}, u32[]{:S(2)}) collective-permute-start(bf16[1024,128]{1,0:T(8,128)(2,1)S(1)} %get-tuple-element.55), channel_id=1, source_target_pairs={{0,224},{32,0},{64,32},{96,64},{128,96},{160,128},{192,160},{224,1... | collective-permute-start | bytes 786440 | tf_op jit(solution)/shard_map/ppermute | solution.py:362
  76.5 10.9 %collective-permute-start.15 = (bf16[1024,128]{1,0:T(8,128)(2,1)S(1)}, bf16[1024,128]{1,0:T(8,128)(2,1)S(1)}, u32[]{:S(2)}, u32[]{:S(2)}) collective-permute-start(bf16[1024,128]{1,0:T(8,128)(2,1)S(1)} %get-tuple-element.56), channel_id=1, source_target_pairs={{0,31},{1,0},{2,1},{3,2},{4,3},{5,4},{6,5},{7,6},{8,7},{9,8},{10,9... | collective-permute-start | bytes 786440 | tf_op jit(solution)/shard_map/ppermute | solution.py:362

commit v7 on v6

--- a/solution.py
+++ b/solution.py
@@ -318,27 +318,34 @@
     norm[...] = add_edge(total, weights, from_block, one, two, norm_in[...], store)
 
 
-def sum_kernel(total_in, weights, low0, low1, high0, high1, norm_in, norm_first, total, message):
+def lane_row(norm):
+    ones = jnp.ones((8, norm.shape[1]), jnp.float32)
+    return lax.dot_general(
+        ones, norm, (((1,), (1,)), ((), ())), precision=lax.Precision.HIGHEST, preferred_element_type=jnp.float32
+    )
+
+
+def keep_edge(total, weights, from_block, one, two, sums):
+    def store(b, rows, value, weighted):
+        total[from_block + b] = value
+
+    return add_edge(total, weights, from_block, one, two, sums, store)
+
+
+def low_kernel(total_in, weights, one, two, norm_in, norm_first, total, norm, row):
     del total_in
-    sums = norm_in[...]
-    size = total.shape[2]
-    for from_block, one, two in ((0, low0, low1), (total.shape[0] // 4 * 3, high0, high1)):
-
-        def store(b, rows, value, weighted, from_block=from_block):
-            total[from_block + b] = value
-
-        sums = add_edge(total, weights, from_block, one, two, sums, store)
-    ones = jnp.ones((8, size), jnp.float32)
-    both = [
-        lax.dot_general(
-            ones, part, (((1,), (1,)), ((), ())), precision=lax.Precision.HIGHEST, preferred_element_type=jnp.float32
-        )
-        for part in (norm_first[...], sums)
-    ]
-    message[...] = jnp.broadcast_to(jnp.concatenate(both, axis=1)[:1], message.shape)
-
-
-def final_kernel(total_cells, sums, total, out):
+    norm[...] = keep_edge(total, weights, 0, one, two, norm_in[...])
+    row[...] = lane_row(norm_first[...])
+
+
+def sum_kernel(total_in, weights, one, two, norm_in, row, total, message):
+    del total_in
+    sums = keep_edge(total, weights, total.shape[0] // 4 * 3, one, two, norm_in[...])
+    both = jnp.concatenate([row[...], lane_row(sums)], axis=1)[:1]
+    message[...] = jnp.broadcast_to(both, message.shape)
+
+
+def final_kernel(total_cells, sums, total, out, held, sems):
     num_blocks, vectors, size = total.shape
     both = jnp.sum(sums[...], axis=0, keepdims=True) * (1.0 / total_cells)
     diagonal = lax.broadcasted_iota(jnp.int32, (vectors, size), 0)
@@ -351,10 +358,18 @@
 
     def body(b, carry):
         cells = pl.ds(pl.multiple_of(b * size, size), size)
-        out[:, cells] = (total[b] * scale).astype(jnp.bfloat16)
+        held[:, cells] = (total[b] * scale).astype(jnp.bfloat16)
         return carry
 
-    lax.fori_loop(0, num_blocks, body, 0, unroll=4)
+    quarter = num_blocks // 4
+    copies = []
+    for part in range(4):
+        lax.fori_loop(part * quarter, (part + 1) * quarter, body, 0, unroll=4)
+        cells = pl.ds(part * quarter * size, quarter * size)
+        copies.append(pltpu.make_async_copy(held.at[:, cells], out.at[:, cells], sems.at[part]))
+        copies[-1].start()
+    for copy in copies:
+        copy.wait()
 
 
 def shift(x, axis, step):
@@ -370,13 +385,13 @@
     return shift(tail, "tile", 1), shift(tail, "layer", 1)
 
 
-def call(kernel, name, outs, in_specs, scratch, flops, nbytes, aliases={}):
+def call(kernel, name, outs, in_specs, scratch, flops, nbytes, aliases={}, out_spec=VMEM_SPEC):
     return pl.pallas_call(
         kernel,
         name=name,
         out_shape=outs,
         in_specs=in_specs,
-        out_specs=[VMEM_SPEC] * len(outs),
+        out_specs=[out_spec] * len(outs),
         scratch_shapes=scratch,
         input_output_aliases=aliases,
         compiler_params=pltpu.CompilerParams(vmem_limit_bytes=16 * 1024 * 1024),
@@ -535,25 +550,36 @@
                 edge * vectors * size * 8,
             )(total, weights, *highs, norm)
             tails = tails_out(tail)
+    total, norm, row = call(
+        low_kernel,
+        "join_low",
+        [block_f32, norm_type, VM((8, vectors), f32)],
+        [VMEM_SPEC] * 6,
+        [],
+        0,
+        edge * vectors * size * 8,
+        {0: 0},
+    )(total, weights, *lows, norm, norm_first)
     total, message = call(
         sum_kernel,
         "join_last",
         [block_f32, VM((devices, 2 * vectors), f32)],
-        [VMEM_SPEC] * 8,
+        [VMEM_SPEC] * 6,
         [],
         0,
-        2 * edge * vectors * size * 8,
+        edge * vectors * size * 8,
         {0: 0},
-    )(total, weights, *lows, *highs, norm, norm_first)
+    )(total, weights, *highs, norm, row)
     sums = lax.all_to_all(message, ("layer", "tile"), 0, 0, tiled=True)
     out = call(
         functools.partial(final_kernel, total_cells),
         "write_out",
         [jax.ShapeDtypeStruct((vectors, cells), bf16)],
         [VMEM_SPEC] * 2,
-        [],
+        [VM((vectors, cells), bf16), pltpu.SemaphoreType.DMA((4,))],
         0,
         cells * vectors * 6,
+        out_spec=HBM_SPEC,
     )(sums, total)[0]
     return out[None, None]
 

time: 113 us -> 113 us (level)
  starting transfers between devices: 32.2 us -> 30.4 us
  waiting for transfers between devices: 23.6 us -> 25.3 us
  Pallas kernels: 32.6 us -> 31.4 us
  blocking collectives: 24.1 us -> 25.3 us
    ppermute x16, starting transfers between devices: 32.2 us -> 30.4 us  [shift(): lax.ppermute(x, axis, [(i, (i + step) % count) for i in range(count)])]
    ppermute x16, waiting for transfers between devices: 23.6 us -> 25.3 us  [shift(): lax.ppermute(x, axis, [(i, (i + step) % count) for i in range(count)])]
    all_to_all x1, blocking collectives: 24.1 us -> 25.3 us  [local(): sums = lax.all_to_all(message, ('layer', 'tile'), 0, 0, tiled=True)]
  transfers between devices with their start and end apart: 16 -> 16, of which waited for: 7 -> 9; matrix products, arithmetic and copies ran while one was open for 0% -> 0% of each run, Pallas kernels for 22% -> 21%
where the time goes in v7:
time: 113 us
  Pallas kernels  31.4 us (28%)
  starting transfers between devices  30.4 us (27%)
  waiting for transfers between devices  25.3 us (22%)
  blocking collectives  25.3 us (22%)
    ppermute x16, starting transfers between devices, shift(): lax.ppermute(x, axis, [(i, (i + step) % count) for i in range(count)])  30.4 us
    ppermute x16, waiting for transfers between devices, shift(): lax.ppermute(x, axis, [(i, (i + step) % count) for i in range(count)])  25.3 us
    all_to_all x1, blocking collectives, local(): sums = lax.all_to_all(message, ('layer', 'tile'), 0, 0, tiled=True)  25.3 us
    pallas_call x1, Pallas kernels, local(): call(first_kernel, 'own_first', [VM((slots + 1, size, size), bf16), tall_...  8.37 us
    pallas_call x2, Pallas kernels, local(): call(adjoint_kernel, 'adjoint' + suffix, [block_f32, norm_type] + ([middl...  6.1 us
    pallas_call x2, Pallas kernels, local(): call(functools.partial(middle_kernel, first), 'middle' + suffix, [rows_ty...  4.34 us
    pallas_call x1, Pallas kernels, local(): call(own_kernel, 'own_next', [block_f32], [SMEM_SPEC] + [VMEM_SPEC] * 4,...  3.61 us
    pallas_call x2, Pallas kernels, local(): call(functools.partial(heads_kernel, first), 'heads' + suffix, [rows_type...  3.15 us
  transfers between devices with their start and end apart: 16, of which 9 were waited for; matrix products, arithmetic and copies ran while one was open for 0% of the time, Pallas kernels for 21%

profile of v7, /device:TPU:1, one launch (start us, length us, event | category | flops | bytes accessed | tf_op | source)
XLA Modules:
  0.0 113.4 jit_solution(8792516505610687331)
XLA Ops:
  0.0 1.1 edges.1
  1.1 4.6 %collective-permute-start.1 = (bf16[1040,128]{1,0:T(8,128)(2,1)S(1)}, bf16[1040,128]{1,0:T(8,128)(2,1)S(1)}, u32[]{:S(2)}, u32[]{:S(2)}) collective-permute-start(bf16[1040,128]{1,0:T(8,128)(2,1)S(1)} %get-tuple-element.40), channel_id=1, source_target_pairs={{0,224},{32,0},{64,32},{96,64},{128,96},{160,128},{192,160},{224,1... | collective-permute-start | bytes 798728 | tf_op jit(solution)/shard_map/ppermute | solution.py:377
  5.7 1.0 collective-permute-start
  6.6 2.3 %collective-permute-start.2 = (bf16[1040,128]{1,0:T(8,128)(2,1)S(1)}, bf16[1040,128]{1,0:T(8,128)(2,1)S(1)}, u32[]{:S(2)}, u32[]{:S(2)}) collective-permute-start(bf16[1040,128]{1,0:T(8,128)(2,1)S(1)} %get-tuple-element.41), channel_id=1, source_target_pairs={{0,1},{1,2},{2,3},{3,4},{4,5},{5,6},{6,7},{7,8},{8,9},{9,10},{10,1... | collective-permute-start | bytes 798728 | tf_op jit(solution)/shard_map/ppermute | solution.py:377
  9.7 8.4 %own_first.1 = (bf16[321,128,128]{2,1,0:T(8,128)(2,1)S(1)}, f32[64,80,128]{2,1,0:T(8,128)S(1)}, s32[8,384]{1,0:T(8,128)S(1)}) custom-call(s32[3]{0:T(128)S(1)} %pad_add_fusion.count, bf16[320,128,128]{2,1,0:T(8,128)(2,1)} %bitcast.17, bf16[64,8192]{1,0:T(8,128)(2,1)} %bitcast.19, s32[1,320]{1,0:T(1,128)} %bitcast.21, s32[1,320]{1,0:T(1,128)} %bitcast.22, ...), custom_call_target="tpu_custom_call" | custom-call | flops 671088640 | bytes 20971520 | tf_op jit(solution)/shard_map/own_first/pallas_call | solution.py:444
  18.1 5.5 %collective-permute-done.right = bf16[1040,128]{1,0:T(8,128)(2,1)S(1)} collective-permute-done((bf16[1040,128]{1,0:T(8,128)(2,1)S(1)}, bf16[1040,128]{1,0:T(8,128)(2,1)S(1)}, u32[]{:S(2)}, u32[]{:S(2)}) %collective-permute-start) | collective-permute-done | bytes 266272 | tf_op jit(solution)/shard_map/ppermute | solution.py:377
  23.6 1.6 %heads_first.1.rows_in = f32[64,80,128]{2,1,0:T(8,128)S(1)} custom-call(s32[8,384]{1,0:T(8,128)S(1)} %get-tuple-element.37.tab, bf16[321,128,128]{2,1,0:T(8,128)(2,1)S(1)} %get-tuple-element.38.matrix, f32[64,80,128]{2,1,0:T(8,128)S(1)} %get-tuple-element.39.rows_in, ...), custom_call_target="tpu_custom_call", output_to_operand_aliasing={{}: (2, {})} | custom-call | flops 167772160 | bytes 2621440 | tf_op jit(solution)/shard_map/heads_first/pallas_call | solution.py:485
  25.2 2.2 %middle_first.1 = (f32[64,80,128]{2,1,0:T(8,128)S(1)}, bf16[65,64,128]{2,1,0:T(8,128)(2,1)S(1)}, f32[64,8,128]{2,1,0:T(8,128)S(1)}, bf16[1024,128]{1,0:T(8,128)(2,1)S(1)}, bf16[1024,128]{1,0:T(8,128)(2,1)S(1)}) custom-call(s32[8,384]{1,0:T(8,128)S(1)} %get-tuple-element.37.tab, ...), custom_call_target="tpu_custom_call", output_to_operand_aliasing={{0}: (2, {})} | custom-call | flops 335544320 | bytes 5242880 | tf_op jit(solution)/shard_map/middle_first/pallas_call | solution.py:496
  27.6 3.7 %collective-permute-start.5 = (bf16[1024,128]{1,0:T(8,128)(2,1)S(1)}, bf16[1024,128]{1,0:T(8,128)(2,1)S(1)}, u32[]{:S(2)}, u32[]{:S(2)}) collective-permute-start(bf16[1024,128]{1,0:T(8,128)(2,1)S(1)} %get-tuple-element.45), channel_id=1, source_target_pairs={{0,1},{1,2},{2,3},{3,4},{4,5},{5,6},{6,7},{7,8},{8,9},{9,10},{10,1... | collective-permute-start | bytes 786440 | tf_op jit(solution)/shard_map/ppermute | solution.py:377
  31.3 1.2 %tails_first.1 = (bf16[1024,128]{1,0:T(8,128)(2,1)S(1)}, bf16[1024,128]{1,0:T(8,128)(2,1)S(1)}) custom-call(s32[8,384]{1,0:T(8,128)S(1)} %get-tuple-element.37.tab, bf16[321,128,128]{2,1,0:T(8,128)(2,1)S(1)} %get-tuple-element.38.matrix, bf16[65,64,128]{2,1,0:T(8,128)(2,1)S(1)} %get-tuple-element.42.image), custom_call_target="tpu_custom_call" | custom-call | flops 167772160 | bytes 2621440 | tf_op jit(solution)/shard_map/tails_first/pallas_call | solution.py:511
  32.5 1.3 %collective-permute-start.6 = (bf16[1024,128]{1,0:T(8,128)(2,1)S(1)}, bf16[1024,128]{1,0:T(8,128)(2,1)S(1)}, u32[]{:S(2)}, u32[]{:S(2)}) collective-permute-start(bf16[1024,128]{1,0:T(8,128)(2,1)S(1)} %get-tuple-element.49), channel_id=1, source_target_pairs={{0,224},{32,0},{64,32},{96,64},{128,96},{160,128},{192,160},{224,1... | collective-permute-start | bytes 786440 | tf_op jit(solution)/shard_map/ppermute | solution.py:377
  34.1 3.1 %adjoint_first.1 = (f32[64,64,128]{2,1,0:T(8,128)S(1)}, f32[64,128]{1,0:T(8,128)S(1)}, bf16[32,64,128]{2,1,0:T(8,128)(2,1)S(1)}) custom-call(s32[8,384]{1,0:T(8,128)S(1)} %get-tuple-element.37.tab, bf16[321,128,128]{2,1,0:T(8,128)(2,1)S(1)} %get-tuple-element.38.matrix, bf16[65,64,128]{2,1,0:T(8,128)(2,1)S(1)} %get-tuple-element.42.image, ...), custom_call_target="tpu_custom_call" | custom-call | flops 335544320 | bytes 5242880 | tf_op jit(solution)/shard_map/adjoint_first/pallas_call | solution.py:521
  37.2 0.7 collective-permute-done.5.two
  38.1 9.0 %collective-permute-start.9 = (bf16[1024,128]{1,0:T(8,128)(2,1)S(1)}, bf16[1024,128]{1,0:T(8,128)(2,1)S(1)}, u32[]{:S(2)}, u32[]{:S(2)}) collective-permute-start(bf16[1024,128]{1,0:T(8,128)(2,1)S(1)} %get-tuple-element.47.head), channel_id=1, source_target_pairs={{0,224},{32,0},{64,32},{96,64},{128,96},{160,128},{192,160},{224,1... | collective-permute-start | bytes 786440 | tf_op jit(solution)/shard_map/ppermute | solution.py:377
  47.1 1.7 %collective-permute-done.6.one = bf16[1024,128]{1,0:T(8,128)(2,1)S(1)} collective-permute-done((bf16[1024,128]{1,0:T(8,128)(2,1)S(1)}, bf16[1024,128]{1,0:T(8,128)(2,1)S(1)}, u32[]{:S(2)}, u32[]{:S(2)}) %collective-permute-start.6) | collective-permute-done | bytes 262176 | tf_op jit(solution)/shard_map/ppermute | solution.py:377
  48.8 0.6 collective-permute-done.7.two
  49.7 2.7 %collective-permute-start.10 = (bf16[1024,128]{1,0:T(8,128)(2,1)S(1)}, bf16[1024,128]{1,0:T(8,128)(2,1)S(1)}, u32[]{:S(2)}, u32[]{:S(2)}) collective-permute-start(bf16[1024,128]{1,0:T(8,128)(2,1)S(1)} %get-tuple-element.52.tail), channel_id=1, source_target_pairs={{0,1},{1,2},{2,3},{3,4},{4,5},{5,6},{6,7},{7,8},{8,9},{9,10},{10,1... | collective-permute-start | bytes 786440 | tf_op jit(solution)/shard_map/ppermute | solution.py:377
  52.3 3.6 %own_next.1.rows_in = f32[64,64,128]{2,1,0:T(8,128)S(1)} custom-call(s32[8,384]{1,0:T(8,128)S(1)} %get-tuple-element.37.tab, bf16[321,128,128]{2,1,0:T(8,128)(2,1)S(1)} %get-tuple-element.38.matrix, bf16[1024,128]{1,0:T(8,128)(2,1)S(1)} %get-tuple-element.47.head, bf16[32,64,128]{2,1,0:T(8,128)(2,1)S(1)} %get-tuple-element.48.middle, ...), custom_call_target="tpu_custom_call" | custom-call | flops 335544320 | bytes 5242880 | tf_op jit(solution)/shard_map/own_next/pallas_call | solution.py:476
  55.9 8.5 %collective-permute-done.8.right = bf16[1024,128]{1,0:T(8,128)(2,1)S(1)} collective-permute-done((bf16[1024,128]{1,0:T(8,128)(2,1)S(1)}, bf16[1024,128]{1,0:T(8,128)(2,1)S(1)}, u32[]{:S(2)}, u32[]{:S(2)}) %collective-permute-start.8) | collective-permute-done | bytes 262176 | tf_op jit(solution)/shard_map/ppermute | solution.py:377
  64.4 1.6 %heads_next.1.rows_in = f32[64,64,128]{2,1,0:T(8,128)S(1)} custom-call(s32[8,384]{1,0:T(8,128)S(1)} %get-tuple-element.37.tab, bf16[321,128,128]{2,1,0:T(8,128)(2,1)S(1)} %get-tuple-element.38.matrix, f32[64,64,128]{2,1,0:T(8,128)S(1)} %own_next.1.rows_in, bf16[1024,128]{1,0:T(8,128)(2,1)S(1)} %collective-permute-done.8.right, ...), custom_call_target="tpu_custom_call", output_to_operand_aliasing={{}: (2, {})} | custom-call | flops 167772160 | bytes 2621440 | tf_op jit(solution)/shard_map/heads_next/pallas_call | solution.py:485
  66.0 2.1 %middle_next.1 = (f32[64,64,128]{2,1,0:T(8,128)S(1)}, bf16[65,64,128]{2,1,0:T(8,128)(2,1)S(1)}, bf16[1024,128]{1,0:T(8,128)(2,1)S(1)}, bf16[1024,128]{1,0:T(8,128)(2,1)S(1)}) custom-call(s32[8,384]{1,0:T(8,128)S(1)} %get-tuple-element.37.tab, bf16[321,128,128]{2,1,0:T(8,128)(2,1)S(1)} %get-tuple-element.38.matrix, ...), custom_call_target="tpu_custom_call", output_to_operand_aliasing={{0}: (2, {})} | custom-call | flops 335544320 | bytes 5242880 | tf_op jit(solution)/shard_map/middle_next/pallas_call | solution.py:496
  68.2 5.0 %collective-permute-start.13 = (bf16[1024,128]{1,0:T(8,128)(2,1)S(1)}, bf16[1024,128]{1,0:T(8,128)(2,1)S(1)}, u32[]{:S(2)}, u32[]{:S(2)}) collective-permute-start(bf16[1024,128]{1,0:T(8,128)(2,1)S(1)} %get-tuple-element.57), channel_id=1, source_target_pairs={{0,1},{1,2},{2,3},{3,4},{4,5},{5,6},{6,7},{7,8},{8,9},{9,10},{10,1... | collective-permute-start | bytes 786440 | tf_op jit(solution)/shard_map/ppermute | solution.py:377
  73.2 1.2 %tails_next.1 = (bf16[1024,128]{1,0:T(8,128)(2,1)S(1)}, bf16[1024,128]{1,0:T(8,128)(2,1)S(1)}) custom-call(s32[8,384]{1,0:T(8,128)S(1)} %get-tuple-element.37.tab, bf16[321,128,128]{2,1,0:T(8,128)(2,1)S(1)} %get-tuple-element.38.matrix, bf16[65,64,128]{2,1,0:T(8,128)(2,1)S(1)} %get-tuple-element.54.image), custom_call_target="tpu_custom_call" | custom-call | flops 167772160 | bytes 2621440 | tf_op jit(solution)/shard_map/tails_next/pallas_call | solution.py:511
  74.5 0.3 collective-permute-start.14
  74.8 3.0 %adjoint_next.1 = (f32[64,64,128]{2,1,0:T(8,128)S(1)}, f32[64,128]{1,0:T(8,128)S(1)}) custom-call(s32[8,384]{1,0:T(8,128)S(1)} %get-tuple-element.37.tab, bf16[321,128,128]{2,1,0:T(8,128)(2,1)S(1)} %get-tuple-element.38.matrix, bf16[65,64,128]{2,1,0:T(8,128)(2,1)S(1)} %get-tuple-element.54.image, f32[64,128]{1,0:T(8,128)S(1)} %get-tuple-element.36.weights), custom_call_target="tpu_custom_call" | custom-call | flops 335544320 | bytes 5242880 | tf_op jit(solution)/shard_map/adjoint_next/pallas_call | solution.py:521
  77.8 3.4 %collective-permute-done.12.one = bf16[1024,128]{1,0:T(8,128)(2,1)S(1)} collective-permute-done((bf16[1024,128]{1,0:T(8,128)(2,1)S(1)}, bf16[1024,128]{1,0:T(8,128)(2,1)S(1)}, u32[]{:S(2)}, u32[]{:S(2)}) %collective-permute-start.12) | collective-permute-done | bytes 262176 | tf_op jit(solution)/shard_map/ppermute | solution.py:377
  81.4 0.3 join_low.1
  81.7 3.3 %collective-permute-done.14.one = bf16[1024,128]{1,0:T(8,128)(2,1)S(1)} collective-permute-done((bf16[1024,128]{1,0:T(8,128)(2,1)S(1)}, bf16[1024,128]{1,0:T(8,128)(2,1)S(1)}, u32[]{:S(2)}, u32[]{:S(2)}) %collective-permute-start.14) | collective-permute-done | bytes 262176 | tf_op jit(solution)/shard_map/ppermute | solution.py:377
  85.0 1.4 %collective-permute-done.15.two = bf16[1024,128]{1,0:T(8,128)(2,1)S(1)} collective-permute-done((bf16[1024,128]{1,0:T(8,128)(2,1)S(1)}, bf16[1024,128]{1,0:T(8,128)(2,1)S(1)}, u32[]{:S(2)}, u32[]{:S(2)}) %collective-permute-start.15) | collective-permute-done | bytes 262176 | tf_op jit(solution)/shard_map/ppermute | solution.py:377
  86.4 0.4 join_last.1
  86.8 25.3 %all_to_all.11 = f32[256,1,128]{2,1,0:T(1,128)S(1)} all-to-all(f32[256,1,128]{2,1,0:T(1,128)S(1)} %bitcast.16), channel_id=1, replica_groups=mesh['layer'=8,'tile'=32] {'layer','tile'}, dimensions={0} | all-to-all | bytes 262144 | tf_op jit(solution)/shard_map/all_to_all | solution.py:573
  112.1 1.2 %write_out.1 = bf16[64,8192]{1,0:T(8,128)(2,1)} custom-call(f32[256,128]{1,0:T(8,128)S(1)} %bitcast.15, f32[64,64,128]{2,1,0:T(8,128)S(1)} %get-tuple-element.66.total), custom_call_target="tpu_custom_call" | custom-call | bytes 3145728 | tf_op jit(solution)/shard_map/write_out/pallas_call | solution.py:574
  (18 shorter events, 1.2 us)
Async XLA Ops:
  1.1 17.0 %collective-permute-start.1 = (bf16[1040,128]{1,0:T(8,128)(2,1)S(1)}, bf16[1040,128]{1,0:T(8,128)(2,1)S(1)}, u32[]{:S(2)}, u32[]{:S(2)}) collective-permute-start(bf16[1040,128]{1,0:T(8,128)(2,1)S(1)} %get-tuple-element.40), channel_id=1, source_target_pairs={{0,224},{32,0},{64,32},{96,64},{128,96},{160,128},{192,160},{224,1... | collective-permute-start | bytes 798728 | tf_op jit(solution)/shard_map/ppermute | solution.py:377
  5.7 18.0 %collective-permute-start = (bf16[1040,128]{1,0:T(8,128)(2,1)S(1)}, bf16[1040,128]{1,0:T(8,128)(2,1)S(1)}, u32[]{:S(2)}, u32[]{:S(2)}) collective-permute-start(bf16[1040,128]{1,0:T(8,128)(2,1)S(1)} %get-tuple-element.40), channel_id=1, source_target_pairs={{0,31},{1,0},{2,1},{3,2},{4,3},{5,4},{6,5},{7,6},{8,7},{9,8},{10,9... | collective-permute-start | bytes 798728 | tf_op jit(solution)/shard_map/ppermute | solution.py:377
  6.6 18.6 %collective-permute-start.3 = (bf16[1040,128]{1,0:T(8,128)(2,1)S(1)}, bf16[1040,128]{1,0:T(8,128)(2,1)S(1)}, u32[]{:S(2)}, u32[]{:S(2)}) collective-permute-start(bf16[1040,128]{1,0:T(8,128)(2,1)S(1)} %get-tuple-element.41), channel_id=1, source_target_pairs={{0,32},{32,64},{64,96},{96,128},{128,160},{160,192},{192,224},{224... | collective-permute-start | bytes 798728 | tf_op jit(solution)/shard_map/ppermute | solution.py:377
  6.6 18.6 %collective-permute-start.2 = (bf16[1040,128]{1,0:T(8,128)(2,1)S(1)}, bf16[1040,128]{1,0:T(8,128)(2,1)S(1)}, u32[]{:S(2)}, u32[]{:S(2)}) collective-permute-start(bf16[1040,128]{1,0:T(8,128)(2,1)S(1)} %get-tuple-element.41), channel_id=1, source_target_pairs={{0,1},{1,2},{2,3},{3,4},{4,5},{5,6},{6,7},{7,8},{8,9},{9,10},{10,1... | collective-permute-start | bytes 798728 | tf_op jit(solution)/shard_map/ppermute | solution.py:377
  27.5 9.7 %collective-permute-start.4 = (bf16[1024,128]{1,0:T(8,128)(2,1)S(1)}, bf16[1024,128]{1,0:T(8,128)(2,1)S(1)}, u32[]{:S(2)}, u32[]{:S(2)}) collective-permute-start(bf16[1024,128]{1,0:T(8,128)(2,1)S(1)} %get-tuple-element.44), channel_id=1, source_target_pairs={{0,32},{32,64},{64,96},{96,128},{128,160},{160,192},{192,224},{224... | collective-permute-start | bytes 786440 | tf_op jit(solution)/shard_map/ppermute | solution.py:377
  27.6 10.4 %collective-permute-start.5 = (bf16[1024,128]{1,0:T(8,128)(2,1)S(1)}, bf16[1024,128]{1,0:T(8,128)(2,1)S(1)}, u32[]{:S(2)}, u32[]{:S(2)}) collective-permute-start(bf16[1024,128]{1,0:T(8,128)(2,1)S(1)} %get-tuple-element.45), channel_id=1, source_target_pairs={{0,1},{1,2},{2,3},{3,4},{4,5},{5,6},{6,7},{7,8},{8,9},{9,10},{10,1... | collective-permute-start | bytes 786440 | tf_op jit(solution)/shard_map/ppermute | solution.py:377
  32.5 16.2 %collective-permute-start.6 = (bf16[1024,128]{1,0:T(8,128)(2,1)S(1)}, bf16[1024,128]{1,0:T(8,128)(2,1)S(1)}, u32[]{:S(2)}, u32[]{:S(2)}) collective-permute-start(bf16[1024,128]{1,0:T(8,128)(2,1)S(1)} %get-tuple-element.49), channel_id=1, source_target_pairs={{0,224},{32,0},{64,32},{96,64},{128,96},{160,128},{192,160},{224,1... | collective-permute-start | bytes 786440 | tf_op jit(solution)/shard_map/ppermute | solution.py:377
  33.9 15.5 %collective-permute-start.7 = (bf16[1024,128]{1,0:T(8,128)(2,1)S(1)}, bf16[1024,128]{1,0:T(8,128)(2,1)S(1)}, u32[]{:S(2)}, u32[]{:S(2)}) collective-permute-start(bf16[1024,128]{1,0:T(8,128)(2,1)S(1)} %get-tuple-element.50), channel_id=1, source_target_pairs={{0,31},{1,0},{2,1},{3,2},{4,3},{5,4},{6,5},{7,6},{8,7},{9,8},{10,9... | collective-permute-start | bytes 786440 | tf_op jit(solution)/shard_map/ppermute | solution.py:377
  38.1 17.8 %collective-permute-start.9 = (bf16[1024,128]{1,0:T(8,128)(2,1)S(1)}, bf16[1024,128]{1,0:T(8,128)(2,1)S(1)}, u32[]{:S(2)}, u32[]{:S(2)}) collective-permute-start(bf16[1024,128]{1,0:T(8,128)(2,1)S(1)} %get-tuple-element.47.head), channel_id=1, source_target_pairs={{0,224},{32,0},{64,32},{96,64},{128,96},{160,128},{192,160},{224,1... | collective-permute-start | bytes 786440 | tf_op jit(solution)/shard_map/ppermute | solution.py:377
  47.1 17.3 %collective-permute-start.8 = (bf16[1024,128]{1,0:T(8,128)(2,1)S(1)}, bf16[1024,128]{1,0:T(8,128)(2,1)S(1)}, u32[]{:S(2)}, u32[]{:S(2)}) collective-permute-start(bf16[1024,128]{1,0:T(8,128)(2,1)S(1)} %get-tuple-element.47.head), channel_id=1, source_target_pairs={{0,31},{1,0},{2,1},{3,2},{4,3},{5,4},{6,5},{7,6},{8,7},{9,8},{10,9... | collective-permute-start | bytes 786440 | tf_op jit(solution)/shard_map/ppermute | solution.py:377
  49.6 16.4 %collective-permute-start.11 = (bf16[1024,128]{1,0:T(8,128)(2,1)S(1)}, bf16[1024,128]{1,0:T(8,128)(2,1)S(1)}, u32[]{:S(2)}, u32[]{:S(2)}) collective-permute-start(bf16[1024,128]{1,0:T(8,128)(2,1)S(1)} %get-tuple-element.52.tail), channel_id=1, source_target_pairs={{0,32},{32,64},{64,96},{96,128},{128,160},{160,192},{192,224},{224... | collective-permute-start | bytes 786440 | tf_op jit(solution)/shard_map/ppermute | solution.py:377
  49.7 16.3 %collective-permute-start.10 = (bf16[1024,128]{1,0:T(8,128)(2,1)S(1)}, bf16[1024,128]{1,0:T(8,128)(2,1)S(1)}, u32[]{:S(2)}, u32[]{:S(2)}) collective-permute-start(bf16[1024,128]{1,0:T(8,128)(2,1)S(1)} %get-tuple-element.52.tail), channel_id=1, source_target_pairs={{0,1},{1,2},{2,3},{3,4},{4,5},{5,6},{6,7},{7,8},{8,9},{9,10},{10,1... | collective-permute-start | bytes 786440 | tf_op jit(solution)/shard_map/ppermute | solution.py:377
  68.1 13.1 %collective-permute-start.12 = (bf16[1024,128]{1,0:T(8,128)(2,1)S(1)}, bf16[1024,128]{1,0:T(8,128)(2,1)S(1)}, u32[]{:S(2)}, u32[]{:S(2)}) collective-permute-start(bf16[1024,128]{1,0:T(8,128)(2,1)S(1)} %get-tuple-element.56), channel_id=1, source_target_pairs={{0,32},{32,64},{64,96},{96,128},{128,160},{160,192},{192,224},{224... | collective-permute-start | bytes 786440 | tf_op jit(solution)/shard_map/ppermute | solution.py:377
  68.2 13.1 %collective-permute-start.13 = (bf16[1024,128]{1,0:T(8,128)(2,1)S(1)}, bf16[1024,128]{1,0:T(8,128)(2,1)S(1)}, u32[]{:S(2)}, u32[]{:S(2)}) collective-permute-start(bf16[1024,128]{1,0:T(8,128)(2,1)S(1)} %get-tuple-element.57), channel_id=1, source_target_pairs={{0,1},{1,2},{2,3},{3,4},{4,5},{5,6},{6,7},{7,8},{8,9},{9,10},{10,1... | collective-permute-start | bytes 786440 | tf_op jit(solution)/shard_map/ppermute | solution.py:377
  74.5 10.5 %collective-permute-start.14 = (bf16[1024,128]{1,0:T(8,128)(2,1)S(1)}, bf16[1024,128]{1,0:T(8,128)(2,1)S(1)}, u32[]{:S(2)}, u32[]{:S(2)}) collective-permute-start(bf16[1024,128]{1,0:T(8,128)(2,1)S(1)} %get-tuple-element.61), channel_id=1, source_target_pairs={{0,224},{32,0},{64,32},{96,64},{128,96},{160,128},{192,160},{224,1... | collective-permute-start | bytes 786440 | tf_op jit(solution)/shard_map/ppermute | solution.py:377
  74.8 11.6 %collective-permute-start.15 = (bf16[1024,128]{1,0:T(8,128)(2,1)S(1)}, bf16[1024,128]{1,0:T(8,128)(2,1)S(1)}, u32[]{:S(2)}, u32[]{:S(2)}) collective-permute-start(bf16[1024,128]{1,0:T(8,128)(2,1)S(1)} %get-tuple-element.62), channel_id=1, source_target_pairs={{0,31},{1,0},{2,1},{3,2},{4,3},{5,4},{6,5},{7,6},{8,7},{9,8},{10,9... | collective-permute-start | bytes 786440 | tf_op jit(solution)/shard_map/ppermute | solution.py:377
